TPU v7x, 512 devices: a whole 4x4x16 slice. The times are simulated.
512 devices in a mesh: tile: 128 (over x, z, core), mode: 4 (over y).
Axes of the slice: x: 4, y: 4, z: 16, core: 2. Of those that a mesh axis runs over, the one named last changes fastest.
Arguments:
- obj_x: float32 [2, 4096, 512], P(None, 'tile', 'mode'), may hold values from -6 to 6
- dual_u: float32 [2, 4096, 512], P(None, 'tile', 'mode'), may hold values from -6 to 6
- probes: float32 [4, 2, 256, 256], P('mode'), may hold values from -4 to 4
- intensity: float32 [128, 256, 256], P('tile'), may hold values from 0.1 to 4
- corners: int32 [2, 128], replicated, may hold values from 0 to 3840, as said below
- owner: int32 [128], replicated, may hold values from 0 to 127, as said below
- w_in: bfloat16 [9, 48, 2], replicated, may hold values from -1.5 to 1.5
- b_in: float32 [48], replicated, may hold values from -3 to 3
- w_down: bfloat16 [4, 48, 48], replicated, may hold values from -0.4375 to 0.4375
- b_down: float32 [48], replicated, may hold values from -3 to 3
- w_mid: bfloat16 [9, 48, 48], replicated, may hold values from -0.3125 to 0.3125
- b_mid: float32 [48], replicated, may hold values from -3 to 3
- w_out: bfloat16 [9, 2, 48], replicated, may hold values from -0.3125 to 0.3125
- b_out: float32 [2], replicated, may hold values from -3 to 3
Outputs:
- obj_next: float32 [2, 4096, 512], P(None, 'tile', 'mode')
- aux_next: float32 [2, 4096, 512], P(None, 'tile', 'mode')
- dual_next: float32 [2, 4096, 512], P(None, 'tile', 'mode')
- misfit: float32 [128], P('tile')
Inputs may be any that keep to these rules, and one draw needn't show every extreme that they name: Row corners lie in 0 to 3840 and column corners in 0 to 256; the upper ends are reached in every draw. Every index of tile owns between 1 and 1 positions and some owns exactly 1; of the positions of one owner at most 1 have patterns that touch one block of 32 object rows held by one index of tile, and in every draw some owner and block reach 1.
All inputs are finite; a program needn't handle non-finite values.
Results may differ from a plain program's by a relative error of at most 0.01.
Values may be sent and summed in bfloat16 or wider, within the bound.
No kernel may reach another device: no remote copies, remote signals or barrier semaphores. Data moves between devices by JAX's collectives and lax.ppermute only.
A program may use at most 128 MiB of HBM per device.

v0:
```python
import math

import jax
import jax.numpy as jnp
from jax import lax
from jax.sharding import PartitionSpec as P

HALO = 6


rho_weight = 2.0
floor_level = 0.25


def extended_2(value, sides, width):
    for axis, dim in sides:
        count, length = (lax.axis_size(axis), value.shape[dim])
        up = [(i, (i + 1) % count) for i in range(count - 1)]
        down = [(j, i) for i, j in up]
        last = lax.slice_in_dim(value, length - width, length, axis=dim)
        first = lax.slice_in_dim(value, 0, width, axis=dim)
        before = lax.ppermute(last, axis, up)
        after = lax.ppermute(first, axis, down)
        value = jnp.concatenate([before, value, after], axis=dim)
    return value


def conv_block(act, weight):
    height = act.shape[1]
    width = act.shape[2]
    padded = jnp.pad(act, ((0, 0), (1, 1), (1, 1)))
    total = jnp.zeros((weight.shape[1], height, width), jnp.float32)
    for tap in range(9):
        shift_row = tap // 3
        shift_col = tap % 3
        window = padded[:, shift_row : shift_row + height, shift_col : shift_col + width]
        total = total + jnp.einsum(
            "oc,chw->ohw", weight[tap], window, preferred_element_type=jnp.float32
        )
    return total


def dft_tables(length, sign):
    grid = (
        jnp.arange(length, dtype=jnp.int32)[:, None]
        * jnp.arange(length, dtype=jnp.int32)[None, :]
        % length
    )
    angle = 2.0 * math.pi / length * grid.astype(jnp.float32)
    factor = 1.0 / math.sqrt(length)
    return (jnp.cos(angle) * factor, sign * jnp.sin(angle) * factor)


def left_product(table, values):
    return jnp.einsum("ab,nbc->nac", table, values, precision=lax.Precision.HIGHEST)


def right_product(values, table):
    return jnp.einsum("nab,bc->nac", values, table, precision=lax.Precision.HIGHEST)


def left_apply(table_re, table_im, real_x, imag_x):
    real_out = left_product(table_re, real_x) - left_product(table_im, imag_x)
    imag_out = left_product(table_re, imag_x) + left_product(table_im, real_x)
    return (real_out, imag_out)


def right_apply(real_x, imag_x, table_re, table_im):
    real_out = right_product(real_x, table_re) - right_product(imag_x, table_im)
    imag_out = right_product(real_x, table_im) + right_product(imag_x, table_re)
    return (real_out, imag_out)


def window_plan(
    index_list,
    pos_count,
    first_strip,
    last_strip,
    row_corner,
    rows_dev,
    strips_per,
    tile_count,
    pair_most,
):
    live = index_list < pos_count
    where_pos = jnp.minimum(index_list, pos_count - 1)
    own_first = first_strip[where_pos]
    own_last = last_strip[where_pos]
    strip_of = own_first[:, None] + jnp.arange(strips_per, dtype=jnp.int32)[None, :]
    order = jnp.arange(index_list.shape[0], dtype=jnp.int32)
    before = (order[None, None, :] < order[:, None, None]) & live[None, None, :]
    hits = (
        before
        & (own_first[None, None, :] <= strip_of[:, :, None])
        & (own_last[None, None, :] >= strip_of[:, :, None])
    )
    rank_at = jnp.sum(hits.astype(jnp.int32), axis=2)
    in_use = live[:, None] & (strip_of <= own_last[:, None])
    strip_safe = jnp.minimum(strip_of, tile_count - 1)
    rank_safe = jnp.minimum(rank_at, pair_most - 1)
    offsets = row_corner[where_pos] - own_first * rows_dev
    return (live, strip_of, rank_at, in_use, strip_safe, rank_safe, offsets)


def send_slots(touches, owner, indices, pair_most, slot_count, pos_count):
    earlier_same = (
        (owner[:, None] == owner[None, :])
        & touches[None, :]
        & (indices[None, :] < indices[:, None])
    )
    send_rank = jnp.sum(earlier_same.astype(jnp.int32), axis=1)
    send_target = jnp.where(touches, owner * pair_most + send_rank, slot_count)
    send_table = (
        jnp.full((slot_count,), pos_count, jnp.int32).at[send_target].set(indices, mode="drop")
    )
    return (jnp.minimum(send_table, pos_count - 1), send_table < pos_count)


def per_device(
    obj_x,
    dual_u,
    probes,
    intensity,
    corners,
    owner,
    w_in,
    b_in,
    w_down,
    b_down,
    w_mid,
    b_mid,
    w_out,
    b_out,
):
    tile_id = lax.axis_index("tile")
    mode_id = lax.axis_index("mode")
    tile_count = lax.axis_size("tile")
    mode_count = lax.axis_size("mode")
    rows_dev = obj_x.shape[1]
    cols_dev = obj_x.shape[2]
    width_all = cols_dev * mode_count
    height_all = rows_dev * tile_count
    patch = probes.shape[-1]
    own_most = intensity.shape[0]
    pos_count = owner.shape[0]
    chans = w_in.shape[1]
    bands = max(1, (height_all - patch - rows_dev) // (patch + 2 * rows_dev))
    pair_most = (own_most + bands - 1) // bands
    slot_count = tile_count * pair_most
    strips_per = patch // rows_dev + 1
    row_corner = corners[0]
    col_corner = corners[1]
    first_strip = row_corner // rows_dev
    last_strip = (row_corner + patch - 1) // rows_dev
    indices = jnp.arange(pos_count, dtype=jnp.int32)
    touches = (first_strip <= tile_id) & (last_strip >= tile_id)
    is_mine = owner == tile_id
    mine_rank = jnp.cumsum(is_mine.astype(jnp.int32)) - 1
    own_index = (
        jnp.full((own_most,), pos_count, jnp.int32)
        .at[jnp.where(is_mine, mine_rank, own_most)]
        .set(indices, mode="drop")
    )
    obj_low = obj_x.astype(jnp.bfloat16)
    strip_full = lax.all_gather(obj_low, "mode", axis=2, tiled=True)
    anchor = jnp.zeros((), jnp.int32)
    den_plane = jnp.full((), 2, jnp.int32)
    table_re, table_im = dft_tables(patch, -1.0)
    slot_pos, slot_live = send_slots(touches, owner, indices, pair_most, slot_count, pos_count)
    plan = window_plan(
        own_index,
        pos_count,
        first_strip,
        last_strip,
        row_corner,
        rows_dev,
        strips_per,
        tile_count,
        pair_most,
    )
    own_live = plan[0]
    starts = col_corner[slot_pos] + 0

    def take(start):
        return lax.dynamic_slice_in_dim(strip_full, start, patch, 2)

    cut = jax.vmap(take)(starts)
    arrived = lax.all_to_all(
        cut.reshape(tile_count, pair_most, 2, rows_dev * patch),
        "tile",
        split_axis=0,
        concat_axis=0,
        tiled=True,
    )
    strip_safe = plan[4]
    rank_safe = plan[5]
    offsets = plan[6]
    count = offsets.shape[0]
    blocks = arrived.reshape(tile_count, pair_most, 2, rows_dev, patch)
    picked = blocks[strip_safe, rank_safe]
    tall = jnp.transpose(picked, (0, 2, 1, 3, 4)).reshape(count, 2, strips_per * rows_dev, patch)

    def crop(block, offset):
        return lax.dynamic_slice_in_dim(block, offset, patch, 1)

    patches = jax.vmap(crop)(tall, offsets)
    probe_re = probes[0, 0]
    probe_im = probes[0, 1]
    obj_re = patches[:, 0].astype(jnp.float32)
    obj_im = patches[:, 1].astype(jnp.float32)
    wave_re = probe_re * obj_re - probe_im * obj_im
    wave_im = probe_re * obj_im + probe_im * obj_re
    far_re, far_im = left_apply(table_re, table_im, wave_re, wave_im)
    far_re, far_im = right_apply(far_re, far_im, table_re, table_im)
    power = far_re * far_re + far_im * far_im
    power_all, probe_power = lax.psum((power, probe_re * probe_re + probe_im * probe_im), "mode")
    measured = jnp.sqrt(intensity)
    misfit = jnp.mean((jnp.sqrt(power_all) - measured) ** 2, axis=(1, 2)) * own_live.astype(
        jnp.float32
    )
    scale = measured / jnp.sqrt(jnp.maximum(power_all, floor_level))
    back_re, back_im = left_apply(table_re, -table_im, far_re * scale, far_im * scale)
    back_re, back_im = right_apply(back_re, back_im, table_re, -table_im)
    grad = jnp.stack(
        [probe_re * back_re + probe_im * back_im, probe_re * back_im - probe_im * back_re], axis=1
    ).astype(jnp.bfloat16)
    probe_pad = jnp.pad(probe_power, ((rows_dev, rows_dev), (0, 0)))
    den_gate = (mode_id == 0).astype(jnp.float32)
    strip_of = plan[1]
    rank_at = plan[2]
    in_use = plan[3]
    offsets = plan[6]
    count = offsets.shape[0]
    tall = jnp.zeros((count, 2, strips_per * rows_dev, patch), grad.dtype)

    def place(block, piece, offset):
        return lax.dynamic_update_slice_in_dim(block, piece, offset, 1)

    tall = jax.vmap(place)(tall, grad, offsets)
    blocks = jnp.transpose(tall.reshape(count, 2, strips_per, rows_dev, patch), (0, 2, 1, 3, 4))
    target = jnp.where(in_use, strip_of * pair_most + rank_at, slot_count).reshape(-1)
    buffer = jnp.zeros((slot_count, 2, rows_dev * patch), grad.dtype)
    buffer = buffer.at[target].set(
        blocks.reshape(count * strips_per, 2, rows_dev * patch), mode="drop"
    )
    back_pieces = lax.all_to_all(
        buffer.reshape(tile_count, pair_most, 2, rows_dev * patch),
        "tile",
        split_axis=0,
        concat_axis=0,
        tiled=True,
    )
    flat = back_pieces.reshape(slot_count, 2, rows_dev, patch)

    def add_slot(slot_no, acc):
        where_pos = slot_pos[slot_no]
        alive = slot_live[slot_no].astype(jnp.float32)
        col = col_corner[where_pos]
        piece = flat[slot_no].astype(jnp.float32) * alive
        row_start = tile_id * rows_dev - row_corner[where_pos] + rows_dev
        weight_rows = lax.dynamic_slice_in_dim(probe_pad, row_start, rows_dev, 0) * (
            alive * den_gate
        )
        old_num = lax.dynamic_slice(acc, (anchor, anchor, col + 0), (2, rows_dev, patch))
        acc = lax.dynamic_update_slice(acc, old_num + piece, (anchor, anchor, col + 0))
        old_den = lax.dynamic_slice(acc, (den_plane, anchor, col), (1, rows_dev, patch))
        return lax.dynamic_update_slice(acc, old_den + weight_rows[None], (den_plane, anchor, col))

    start_acc = jnp.zeros((3, rows_dev, width_all), jnp.float32)
    acc_rows = lax.fori_loop(0, slot_count, add_slot, start_acc)
    totals = lax.psum_scatter(acc_rows, "mode", scatter_dimension=2, tiled=True)
    base = obj_x + dual_u
    extended = extended_2(base.astype(jnp.bfloat16), (("tile", 1), ("mode", 2)), HALO)
    ext_rows = rows_dev + 2 * HALO
    ext_cols = cols_dev + 2 * HALO
    row_ids = tile_id * rows_dev - HALO + jnp.arange(ext_rows, dtype=jnp.int32)
    col_ids = mode_id * cols_dev - HALO + jnp.arange(ext_cols, dtype=jnp.int32)
    row_inside = (row_ids >= 0) & (row_ids < height_all)
    col_inside = (col_ids >= 0) & (col_ids < width_all)
    fine_mask = (row_inside[:, None] & col_inside[None, :]).astype(jnp.float32)
    coarse_mask = fine_mask[::2, ::2]
    first_map = (jax.nn.relu(conv_block(extended, w_in) + b_in[:, None, None]) * fine_mask).astype(
        jnp.bfloat16
    )
    pairs = first_map.reshape(chans, ext_rows // 2, 2, ext_cols // 2, 2)
    down_kernel = w_down.reshape(2, 2, chans, chans)
    coarse = jnp.einsum("ijoc,chiwj->ohw", down_kernel, pairs, preferred_element_type=jnp.float32)
    second_map = (jax.nn.relu(coarse + b_down[:, None, None]) * coarse_mask).astype(jnp.bfloat16)
    third_map = jax.nn.relu(conv_block(second_map, w_mid) + b_mid[:, None, None]).astype(
        jnp.bfloat16
    )
    upsampled = jnp.repeat(jnp.repeat(third_map.astype(jnp.float32), 2, axis=1), 2, axis=2)
    fourth_map = (upsampled * fine_mask + first_map.astype(jnp.float32)).astype(jnp.bfloat16)
    denoised = conv_block(fourth_map, w_out) + b_out[:, None, None]
    center = denoised[:, HALO : HALO + rows_dev, HALO : HALO + cols_dev]
    aux_next = base - center
    obj_next = (totals[0:2] + rho_weight * (aux_next - dual_u)) / (totals[2] + rho_weight)
    dual_next = dual_u + obj_next - aux_next
    return (obj_next, aux_next, dual_next, misfit)


def solution(mesh):
    return jax.shard_map(
        per_device,
        mesh=mesh,
        in_specs=(
            P(None, "tile", "mode"),
            P(None, "tile", "mode"),
            P("mode", None, None, None),
            P("tile", None, None),
            P(),
            P(),
            P(),
            P(),
            P(),
            P(),
            P(),
            P(),
            P(),
            P(),
        ),
        out_specs=(
            P(None, "tile", "mode"),
            P(None, "tile", "mode"),
            P(None, "tile", "mode"),
            P("tile"),
        ),
        check_vma=False,
    )
```

profile of v0, /device:TPU:2, one launch (start us, length us, event | category | flops | bytes accessed | tf_op | source)
XLA Modules:
  0.0 1950.9 jit_solution(8107913524456249471)
XLA Ops:
  8.6 0.9 convert_reduce_fusion
  10.3 1.0 scatter_custom_fusion
  11.3 1.2 gather_fusion
  13.3 11.3 all_gather.3
  24.8 35.4 %gather_fusion.1 = bf16[128,2,32,256]{2,1,3,0:T(2,128)(2,1)} fusion(bf16[2,32,512]{1,0,2:T(2,128)(2,1)S(1)} %copy.84, s32[128]{0:T(128)S(1)} %fusion.151), kind=kCustom, calls=%fused_computation.1 | custom fusion | bytes 8390144 | tf_op jit(solution)/shard_map/vmap()/gather | solution.py:185
  60.1 27.1 %copy.85 = bf16[128,2,32,256]{0,3,2,1:T(8,128)(2,1)} copy(bf16[128,2,32,256]{2,1,3,0:T(2,128)(2,1)} %gather_fusion.1) | data formatting | bytes 8388608 | tf_op jit(solution)/shard_map/vmap()/gather | solution.py:185
  87.2 11.3 copy.86
  98.5 20.1 %all-to-all-start = ((bf16[128,1,2,8192]{3,2,1,0:T(2,128)(2,1)}), bf16[128,1,2,8192]{3,2,1,0:T(2,128)(2,1)}, u32[]{:S(2)}, u32[]{:S(2)}) async-start(bf16[128,1,2,8192]{3,2,1,0:T(2,128)(2,1)} %copy.86), calls=%async_computation | async-start | bytes 8388608 | tf_op jit(solution)/shard_map/all_to_all | solution.py:188
  119.0 2.0 scatter_fusion
  126.1 179.7 %all-to-all-done = bf16[128,1,2,8192]{3,2,1,0:T(2,128)(2,1)} async-done(((bf16[128,1,2,8192]{3,2,1,0:T(2,128)(2,1)}), bf16[128,1,2,8192]{3,2,1,0:T(2,128)(2,1)}, u32[]{:S(2)}, u32[]{:S(2)}) %all-to-all-start) | async-done | bytes 4194336 | tf_op jit(solution)/shard_map/all_to_all | solution.py:188
  305.8 7.8 reshape.464
  313.7 2.8 gather_fusion.2
  317.3 1.5 fusion.93
  318.8 1.5 fusion.95
  320.2 1.5 fusion.29
  321.7 1.5 fusion.94
  323.2 1.5 fusion.96
  324.7 1.5 fusion.28
  326.2 1.5 convolution_subtract_fusion.2
  327.7 1.9 convolution_add_fusion.10
  330.4 1.3 fusion.148
  332.4 2.7 and_reduce_fusion
  335.0 48.0 %all-reduce.9.cloned.1.call-done = (f32[1,256,256]{2,1,0:T(8,128)}, f32[256,256]{1,0:T(8,128)}) async-done(((f32[1,256,256]{2,1,0:T(8,128)}, f32[256,256]{1,0:T(8,128)}), (f32[1,256,256]{2,1,0:T(8,128)}, f32[256,256]{1,0:T(8,128)})) %all-reduce.9.cloned.1.call-update) | async-done | bytes 524304 | tf_op jit(solution)/shard_map/psum | solution.py:216
  383.0 1.7 multiply_reduce_fusion
  384.7 1.5 fusion.63
  386.2 1.5 fusion.67
  387.7 1.5 fusion.27
  389.2 1.5 fusion.77
  390.7 1.5 fusion.92
  392.2 1.5 fusion.26
  393.7 1.5 convolution_add_fusion.8
  395.2 1.7 fusion.91
  397.6 2.2 scatter.28
  399.8 6.2 broadcast_in_dim.39
  406.0 4.1 scatter_fusion.1
  410.1 17.2 all-to-all-start.1
  427.5 2.0 collective-permute-start
  429.5 5.6 collective-permute-start.1
  435.3 169.3 %collective-permute-done = bf16[2,6,128]{2,0,1:T(2,128)(2,1)S(1)} collective-permute-done((bf16[2,6,128]{2,0,1:T(2,128)(2,1)S(1)}, bf16[2,6,128]{2,0,1:T(2,128)(2,1)S(1)}, u32[]{:S(2)}, u32[]{:S(2)}) %collective-permute-start) | collective-permute-done | bytes 3104 | tf_op jit(solution)/shard_map/ppermute | solution.py:22
  604.7 2.4 collective-permute-start.2
  607.1 1.3 collective-permute-start.3
  608.8 4.3 collective-permute-done.3
  617.2 1.4 fusion.2
  618.6 1.2 copy.93
  619.8 1.5 reshape.477
  621.3 2.3 fusion.23
  626.5 2.8 broadcast_in_dim.85
  629.3 3.9 reshape.480
  633.2 2.8 copy.96
  636.1 2.4 add_convert_fusion
  641.6 7.6 reshape.476
  649.3 1234.0 %while.20 = (s32[]{:T(128)}, f32[3,32,512]{2,1,0:T(8,128)S(1)}, s32[128]{0:T(128)S(1)}, s32[128]{0:T(128)S(1)}, bf16[128,2,32,256]{3,2,1,0:T(8,128)(2,1)}, /*ind...) while((s32[]{:T(128)}, f32[3,32,512]{2,1,0:T(8,128)S(1)}, ...), condition=%wide.region_9.10_spmd, body=%wide.region_8.9_spmd.sunk | while | flops 65551 | bytes 459135 | solution.py:270
  654.8 0.9 bitcast_add_fusion.4
  674.1 0.9 bitcast_add_fusion.4
  693.4 0.9 bitcast_add_fusion.4
  712.6 0.9 bitcast_add_fusion.4
  722.4 0.9 bitcast_add_fusion.4
  1883.3 7.8 copy.103
  1891.1 8.8 reshape.663
  1901.4 30.2 %reduce-scatter.4.cloned.1.call-done = f32[128,96]{1,0:T(8,128)} async-done(((f32[512,96]{1,0:T(8,128)}), f32[128,96]{1,0:T(8,128)}) %reduce-scatter.4.cloned.1.call-update) | async-done | bytes 49168
  1931.6 3.0 reshape.664
  1934.6 2.0 slice_add_fusion
  1936.5 2.7 copy.108
  1939.2 1.4 copy.106
  (1134 shorter events, 597.2 us)
Async XLA Ops:
  7.2 614.2 %copy-start = (bf16[4,48,48]{2,1,0:T(8,128)(2,1)S(1)}, bf16[4,48,48]{2,1,0:T(8,128)(2,1)}, u32[]{:S(2)}) copy-start(bf16[4,48,48]{2,1,0:T(8,128)(2,1)} %param.26) | copy-start | bytes 55300
  98.5 20.1 %copy-start.8 = (s32[128]{0:T(128)S(1)}, s32[128]{0:T(128)}, u32[]{:S(2)}) copy-start(s32[128]{0:T(128)} %param.23) | copy-start | bytes 1540
  98.5 207.3 %all-to-all-start = ((bf16[128,1,2,8192]{3,2,1,0:T(2,128)(2,1)}), bf16[128,1,2,8192]{3,2,1,0:T(2,128)(2,1)}, u32[]{:S(2)}, u32[]{:S(2)}) async-start(bf16[128,1,2,8192]{3,2,1,0:T(2,128)(2,1)} %copy.86), calls=%async_computation | async-start | bytes 8388608 | tf_op jit(solution)/shard_map/all_to_all | solution.py:188
  118.5 264.5 %all-reduce.9.cloned.1.call-start = ((), (), s32[]{:S(2)}) async-start(), calls=%async_computation.4 | async-start | bytes 1048576 | tf_op jit(solution)/shard_map/psum | solution.py:216
  126.1 190.4 %copy-start.2 = (f32[1,2,256,256]{3,2,1,0:T(8,128)S(1)}, f32[1,2,256,256]{3,2,1,0:T(8,128)}, u32[]{:S(2)}) copy-start(f32[1,2,256,256]{3,2,1,0:T(8,128)} %param.20) | copy-start | bytes 1572868
  326.2 5.5 copy-start.13
  326.2 6.2 copy-start.12
  326.2 56.8 %copy-start.5 = (f32[1,256,256]{2,1,0:T(8,128)S(1)}, f32[1,256,256]{2,1,0:T(8,128)}, u32[]{:S(2)}) copy-start(f32[1,256,256]{2,1,0:T(8,128)} %param.21) | copy-start | bytes 786436
  410.1 17.3 copy-start.3
  410.1 17.3 copy-start.6
  410.1 203.1 %copy-start.9 = (bf16[9,48,2]{1,2,0:T(2,128)(2,1)S(1)}, bf16[9,48,2]{1,2,0:T(2,128)(2,1)}, u32[]{:S(2)}) copy-start(bf16[9,48,2]{1,2,0:T(2,128)(2,1)} %param.24) | copy-start | bytes 5188
  410.1 231.5 %all-to-all-start.1 = ((bf16[128,1,2,8192]{3,2,1,0:T(2,128)(2,1)}), bf16[128,1,2,8192]{3,2,1,0:T(2,128)(2,1)}, u32[]{:S(2)}, u32[]{:S(2)}) async-start(bf16[128,1,2,8192]{3,2,1,0:T(2,128)(2,1)} %bitcast.336), calls=%async_computation.1 | async-start | bytes 8388608 | tf_op jit(solution)/shard_map/all_to_all | solution.py:246
  427.3 1504.2 %reduce-scatter.4.cloned.1.call-start = ((), (), s32[]{:S(2)}) async-start(), calls=%async_computation.3 | async-start | bytes 327680
  427.5 177.1 %collective-permute-start = (bf16[2,6,128]{2,0,1:T(2,128)(2,1)S(1)}, bf16[2,6,128]{2,0,1:T(2,128)(2,1)S(1)}, u32[]{:S(2)}, u32[]{:S(2)}) collective-permute-start(bf16[2,6,128]{2,0,1:T(2,128)(2,1)S(1)} %get-tuple-element.362), channel_id=1, source_target_pairs={{0,4},{4,8},{8,12},{12,16},{16,20},{20,24},{24,28},{28,32},{32,36}... | collective-permute-start | bytes 9224 | tf_op jit(solution)/shard_map/ppermute | solution.py:22
  429.5 175.1 %collective-permute-start.1 = (bf16[2,6,128]{2,0,1:T(2,128)(2,1)S(1)}, bf16[2,6,128]{2,0,1:T(2,128)(2,1)S(1)}, u32[]{:S(2)}, u32[]{:S(2)}) collective-permute-start(bf16[2,6,128]{2,0,1:T(2,128)(2,1)S(1)} %get-tuple-element.363), channel_id=1, source_target_pairs={{4,0},{8,4},{12,8},{16,12},{20,16},{24,20},{28,24},{32,28},{36,32}... | collective-permute-start | bytes 9224 | tf_op jit(solution)/shard_map/ppermute | solution.py:23
  604.7 4.0 collective-permute-start.2
  607.1 5.9 collective-permute-start.3
  616.2 1.0 copy-start.11
  618.6 2.7 copy-start.1
  619.8 1.5 copy-start.15
  621.3 2.3 copy-start.7
  624.9 0.8 copy-start.10
  636.1 2.4 copy-start.14
  640.3 1.3 copy-start.4
  1891.1 9.1 copy-start.16
Sparse Core Ops, SparseCore 0:
  330.5 52.4 all-reduce.8
  1900.0 31.5 reduce-scatter.3
where the time goes:
time: 1980 us; the launch traced here: 1950 us
  loops' own time  655 us (33%)
  local copies, waits for them, and re-layouts  609 us (31%)
  waiting for transfers between devices  432 us (22%)
  other arithmetic  137 us (7%)
  starting transfers between devices  48.7 us (2%)
  matrix products  38.1 us (2%)
    another operation x1, loops' own time, per_device(): acc_rows = lax.fori_loop(0, slot_count, add_slot, start_acc)  655 us
    all_to_all x1, waiting for transfers between devices, per_device(): lax.all_to_all(cut.reshape(tile_count, pair_most, 2, rows_dev * patch), '...  180 us
    ppermute x2, waiting for transfers between devices, extended_2(): before = lax.ppermute(last, axis, up)  169 us
    add x128, other arithmetic, add_slot(): old_num + piece  109 us
    dynamic_update_slice x128, local copies, waits for them, and re-layouts, add_slot(): lax.dynamic_update_slice(acc, old_num + piece, (anchor, anchor, col + 0))  91.1 us
    dynamic_slice x128, local copies, waits for them, and re-layouts, add_slot(): row_start = tile_id * rows_dev - row_corner[where_pos] + rows_dev  85.3 us
    dynamic_slice x128, local copies, waits for them, and re-layouts, add_slot(): alive = slot_live[slot_no].astype(jnp.float32)  71.7 us
    dynamic_slice x128, local copies, waits for them, and re-layouts, add_slot(): where_pos = slot_pos[slot_no]  71.5 us
  transfers between devices with their start and end apart: 8, of which 5 were waited for; matrix products, arithmetic and copies ran while one was open for 2% of the time, Pallas kernels for 0%

commit v1 on v0

v1 whole, which is shorter than its diff:
```python
import math

import jax
import jax.numpy as jnp
import numpy as np
from jax import lax
from jax.experimental import pallas as pl
from jax.experimental.pallas import tpu as pltpu
from jax.sharding import Mesh, PartitionSpec as P

HALO = 6
NX, NZ, NC, NM = 4, 16, 2, 4
PATCH = 256
ROWS = 32
COLS = 128
STRIPS = PATCH // ROWS + 1
HALF = (STRIPS + 1) // 2

rho_weight = 2.0
floor_level = 0.25
f32 = jnp.float32
bf16 = jnp.bfloat16
TILE_AXES = ("x", "z", "core")


def shifted(value, axes, step):
    count = math.prod(lax.axis_size(a) for a in axes)
    pairs = [(i, i + step) for i in range(count) if 0 <= i + step < count]
    return lax.ppermute(value, axes, pairs)


def extended_2(value, sides, width):
    for axes, dim in sides:
        length = value.shape[dim]
        last = lax.slice_in_dim(value, length - width, length, axis=dim)
        first = lax.slice_in_dim(value, 0, width, axis=dim)
        before = shifted(last, axes, 1)
        after = shifted(first, axes, -1)
        value = jnp.concatenate([before, value, after], axis=dim)
    return value

def vmem_spec():
    return pl.BlockSpec(memory_space=pltpu.VMEM)


def smem_spec():
    return pl.BlockSpec(memory_space=pltpu.SMEM)


def ids(meta):
    return meta[2, 0], meta[2, 1], meta[2, 2], meta[2, 3]


def first_strip(s0, core):
    return s0 + ((s0 + core) & 1)


def pack_kernel(meta, near, out):
    x, z, core, mode = ids(meta)
    for target in range(NX * NC):
        tx, tc = target // NC, target % NC
        tile = tx * (NZ * NC) + z * NC + tc
        begin = first_strip(meta[0, tile] // ROWS, core)
        for j in range(HALF):
            slot = ((begin + 2 * j) % (NZ * NC)) // NC
            out[target, j] = near[slot]


def window_kernel(meta, got, out, tall):
    x, z, core, mode = ids(meta)
    row = meta[0, x * (NZ * NC) + z * NC + core]
    s0 = row // ROWS
    for i in range(STRIPS):
        strip = s0 + i
        source = jnp.minimum(strip // (NZ * NC), NX - 1) * NC + (strip & 1)
        block = got[source, i // 2].astype(f32)
        tall[0, pl.ds(i * ROWS, ROWS)] = block[:ROWS]
        tall[1, pl.ds(i * ROWS, ROWS)] = block[ROWS:]
    offset = row - s0 * ROWS
    for plane in range(2):
        out[plane] = tall[plane, pl.ds(offset, PATCH)].astype(bf16)


def dot(a, b):
    return jnp.dot(a, b, preferred_element_type=f32)


def wave_kernel(meta, wins, probe0, probe1, probe2, probe3, intensity, table, out, err, far_all, tall):
    x, z, core, mode = ids(meta)
    mine = x * (NZ * NC) + z * NC + core
    row = meta[0, mine]
    col = meta[1, mine]
    s0 = row // ROWS
    offset = row - s0 * ROWS
    t_re = table[0]
    t_im = table[1]
    t_neg = -t_im
    left = jnp.concatenate(
        [jnp.concatenate([t_re, t_neg], axis=1), jnp.concatenate([t_im, t_re], axis=1)], axis=0
    )
    right = jnp.concatenate(
        [jnp.concatenate([t_re, t_im], axis=1), jnp.concatenate([t_neg, t_re], axis=1)], axis=0
    )
    full = jnp.concatenate(
        [jnp.concatenate([wins[m, p] for m in range(NM)], axis=1) for p in range(2)], axis=0
    )
    src = lax.broadcasted_iota(jnp.int32, (NM * COLS, PATCH), 0)
    dst = lax.broadcasted_iota(jnp.int32, (NM * COLS, PATCH), 1)
    take = jnp.where(src == dst + col, 1.0, 0.0).astype(bf16)
    patch = dot(full, take)
    obj_re = patch[:PATCH]
    obj_im = patch[PATCH:]
    probes = (probe0, probe1, probe2, probe3)
    power = jnp.zeros((PATCH, PATCH), f32)
    for m in range(NM):
        p_re = probes[m][0].astype(f32)
        p_im = probes[m][1].astype(f32)
        wave = jnp.concatenate(
            [(p_re * obj_re - p_im * obj_im).astype(bf16), (p_re * obj_im + p_im * obj_re).astype(bf16)],
            axis=0,
        )
        half = dot(left, wave).astype(bf16)
        far = dot(jnp.concatenate([half[:PATCH], half[PATCH:]], axis=1), right)
        far_all[m] = far
        power = power + far[:, :PATCH] * far[:, :PATCH] + far[:, PATCH:] * far[:, PATCH:]
    measured = jnp.sqrt(intensity[0])
    gap = jnp.sqrt(power) - measured
    err[...] = jnp.sum(gap * gap, keepdims=True) * (1.0 / (PATCH * PATCH))
    scale = measured / jnp.sqrt(jnp.maximum(power, floor_level))
    b_src = lax.broadcasted_iota(jnp.int32, (PATCH, COLS), 0)
    b_dst = lax.broadcasted_iota(jnp.int32, (PATCH, COLS), 1)
    keep = jnp.where(b_src == b_dst + (mode * COLS - col), 1.0, 0.0).astype(bf16)
    k_re = dot(t_re, keep).astype(bf16)
    k_im = dot(t_im, keep).astype(bf16)
    back_right = jnp.concatenate(
        [jnp.concatenate([k_re, -k_im], axis=1), jnp.concatenate([k_im, k_re], axis=1)], axis=0
    )
    sum_re = jnp.zeros((PATCH, COLS), f32)
    sum_im = jnp.zeros((PATCH, COLS), f32)
    for m in range(NM):
        far = far_all[m]
        scaled = jnp.concatenate(
            [(far[:, :PATCH] * scale).astype(bf16), (far[:, PATCH:] * scale).astype(bf16)], axis=1
        )
        half = dot(scaled, back_right).astype(bf16)
        back = dot(right, jnp.concatenate([half[:, :COLS], half[:, COLS:]], axis=0))
        back_re = back[:PATCH]
        back_im = back[PATCH:]
        q_re = dot(probes[m][0], keep)
        q_im = dot(probes[m][1], keep)
        sum_re = sum_re + (q_re * back_re + q_im * back_im)
        sum_im = sum_im + (q_re * back_im - q_im * back_re)
    tall[...] = jnp.zeros(tall.shape, f32)
    tall[0, pl.ds(offset, PATCH)] = sum_re
    tall[1, pl.ds(offset, PATCH)] = sum_im
    out[...] = jnp.zeros(out.shape, bf16)
    for i in range(STRIPS):
        strip = s0 + i
        target = jnp.minimum(strip // (NZ * NC), NX - 1) * NC + (strip & 1)
        piece = [tall[p, pl.ds(i * ROWS, ROWS)] for p in range(2)]
        out[target, i // 2] = jnp.concatenate(piece, axis=0).astype(bf16)


def gather_kernel(meta, got, out, acc):
    x, z, core, mode = ids(meta)
    acc[...] = jnp.zeros(acc.shape, f32)
    for source in range(NX * NC):
        sx, sc = source // NC, source % NC
        begin = first_strip(meta[0, sx * (NZ * NC) + z * NC + sc] // ROWS, core)
        for j in range(HALF):
            slot = ((begin + 2 * j) % (NZ * NC)) // NC
            acc[slot] = acc[slot] + got[source, j].astype(f32)
    out[...] = acc[...].astype(bf16)


def weight_kernel(meta, probe0, probe1, probe2, probe3, out, padded):
    x, z, core, mode = ids(meta)
    row0 = (x * (NZ * NC) + z * NC + core) * ROWS
    col0 = mode * COLS
    total = jnp.zeros((PATCH, PATCH), f32)
    for probe in (probe0, probe1, probe2, probe3):
        p_re = probe[0].astype(f32)
        p_im = probe[1].astype(f32)
        total = total + p_re * p_re + p_im * p_im
    padded[...] = jnp.zeros(padded.shape, f32)
    for half in range(PATCH // COLS):
        padded[1 + half, pl.ds(ROWS, PATCH)] = total[:, half * COLS : (half + 1) * COLS]
    out[...] = jnp.zeros(out.shape, f32)

    def add(k, carry):
        down = row0 - meta[0, k] + ROWS
        over = col0 - meta[1, k] + COLS
        hit = (down > 0) & (down < PATCH + ROWS) & (over > 0) & (over < PATCH + COLS)

        @pl.when(hit)
        def _():
            rows = jnp.concatenate([padded[q, pl.ds(down, ROWS)] for q in range(4)], axis=1)
            moved = pltpu.roll(rows, PATCH + 2 * COLS - over, 1)
            out[...] = out[...] + moved[:, :COLS]

        return carry

    lax.fori_loop(0, meta.shape[1], add, 0)


def dft_table():
    grid = np.arange(PATCH)[:, None] * np.arange(PATCH)[None, :] % PATCH
    angle = 2.0 * np.pi / PATCH * grid
    factor = 1.0 / math.sqrt(PATCH)
    table = np.stack([np.cos(angle) * factor, -np.sin(angle) * factor])
    return jnp.asarray(table.astype(np.float32)).astype(bf16)


CY, CX = (ROWS + 2 * HALO) // 2, (COLS + 2 * HALO) // 2
FLAT = CY * 128
CHUNK = 256
PHASES = ((0, 0), (0, 1), (1, 0), (1, 1))
SHIFTS = tuple((dy, dx) for dy in (-1, 0, 1) for dx in (-1, 0, 1))


def split_tables():
    first = np.zeros((9, 2, 4, 72), np.float32)
    last = np.zeros((9, 36, 4), np.float32)
    for tap in range(9):
        for ij, (i, j) in enumerate(PHASES):
            r, c = i + tap // 3 - 1, j + tap % 3 - 1
            p, q, dy, dx = r & 1, c & 1, r >> 1, c >> 1
            s = (dy + 1) * 3 + dx + 1
            for ch in range(2):
                first[tap, ch, ij, s * 8 + q * 4 + ch * 2 + p] = 1
            last[tap, s * 4 + ij, p * 2 + q] = 1
    return jnp.asarray(first).astype(bf16), jnp.asarray(last).astype(bf16)


def moved(value, dy, dx):
    if dx:
        value = pltpu.roll(value, (-dx) % FLAT, 1)
    if dy == 1:
        value = jnp.concatenate([value[:, 128:], value[:, :128]], axis=1)
    if dy == -1:
        value = jnp.concatenate([value[:, FLAT - 128 :], value[:, : FLAT - 128]], axis=1)
    return value


def denoise_kernel(
    meta,
    b_out,
    ext,
    first_w,
    first_b,
    down_w,
    down_b,
    mid_w,
    mid_b,
    last_w,
    out,
    halves,
    planes,
    taps1,
    maps,
    coarse,
    taps2,
    fourth,
    parts,
    inter,
):
    x, z, core, mode = ids(meta)
    chans = coarse.shape[0]
    height = ROWS + 2 * HALO
    width = COLS + 2 * HALO
    src = lax.broadcasted_iota(jnp.int32, (width, 256), 0)
    dst = lax.broadcasted_iota(jnp.int32, (width, 256), 1)
    lane = dst & 127
    even_odd = jnp.where((src == 2 * lane + (dst >> 7)) & (lane < CX), 1.0, 0.0).astype(bf16)
    for ch in range(2):
        row = dot(ext[ch], even_odd)
        for q in range(2):
            halves[q, pl.ds(ch * height, height)] = row[:, q * 128 : (q + 1) * 128]
    for y in range(CY):
        pieces = [
            halves[q, pl.ds(ch * height + 2 * y, 2)] for q in range(2) for ch in range(2)
        ]
        planes[:, pl.ds(y * 128, 128)] = jnp.concatenate(pieces, axis=0)
    full = planes[...]
    taps1[...] = jnp.concatenate([moved(full, dy, dx) for dy, dx in SHIFTS], axis=0).astype(bf16)

    row0 = (x * (NZ * NC) + z * NC + core) * ROWS - HALO
    col0 = mode * COLS - HALO
    height_all, width_all = NX * NZ * NC * ROWS, NM * COLS

    def masks(start):
        spot = lax.broadcasted_iota(jnp.int32, (1, CHUNK), 1) + start
        rows = row0 + 2 * (spot >> 7)
        cols = col0 + 2 * (spot & 127)
        found = []
        for p, q in PHASES:
            inside = (rows + p >= 0) & (rows + p < height_all)
            inside = inside & (cols + q >= 0) & (cols + q < width_all)
            found.append(jnp.where(inside, 1.0, 0.0))
        return found

    for start in range(0, FLAT, CHUNK):
        span = pl.ds(start, CHUNK)
        found = masks(start)
        value = dot(first_w[...], taps1[:, span])
        for n in range(4):
            part = value[n * chans : (n + 1) * chans] + first_b[...]
            maps[pl.ds(n * chans, chans), span] = (jnp.maximum(part, 0.0) * found[n]).astype(bf16)
        value = dot(down_w[...], maps[:, span]) + down_b[...]
        coarse[:, span] = (jnp.maximum(value, 0.0) * found[0]).astype(bf16).astype(f32)
    for s, (dy, dx) in enumerate(SHIFTS):
        taps2[pl.ds(s * chans, chans)] = moved(coarse[...], dy, dx).astype(bf16)
    for start in range(0, FLAT, CHUNK):
        span = pl.ds(start, CHUNK)
        found = masks(start)
        value = dot(mid_w[...], taps2[:, span]) + mid_b[...]
        third = jnp.maximum(value, 0.0).astype(bf16).astype(f32)
        for n in range(4):
            rows = pl.ds(n * chans, chans)
            fourth[rows, span] = (third * found[n] + maps[rows, span].astype(f32)).astype(bf16)
        parts[:, span] = dot(last_w[...], fourth[:, span])
    total = moved(parts[pl.ds(0, 8)], *SHIFTS[0])
    for s in range(1, 9):
        total = total + moved(parts[pl.ds(s * 8, 8)], *SHIFTS[s])
    planes[...] = total
    for y in range(HALO // 2, HALO // 2 + ROWS // 2):
        tile = planes[:, pl.ds(y * 128, 128)]
        for i, j in PHASES:
            for ch in range(2):
                n = (i * 2 + j) * 2 + ch
                inter[j, pl.ds(ch * ROWS + 2 * y - HALO + i, 1)] = tile[n : n + 1]
    e_src = lax.broadcasted_iota(jnp.int32, (256, COLS), 0)
    e_dst = lax.broadcasted_iota(jnp.int32, (256, COLS), 1)
    weave = jnp.where(2 * (e_src & 127) - HALO + (e_src >> 7) == e_dst, 1.0, 0.0).astype(bf16)
    wide = jnp.concatenate([inter[0], inter[1]], axis=1)
    high = wide.astype(bf16)
    low = (wide - high.astype(f32)).astype(bf16)
    woven = dot(high, weave) + dot(low, weave)
    for ch in range(2):
        out[ch] = woven[ch * ROWS : (ch + 1) * ROWS] + b_out[ch]


def denoise(base, meta, w_in, b_in, w_down, b_down, w_mid, b_mid, w_out, b_out):
    chans = w_in.shape[1]
    extended = extended_2(base.astype(bf16), ((TILE_AXES, 1), (("mode",), 2)), HALO)
    first, last = split_tables()
    first_w = jnp.einsum("toc,tcik->iok", w_in, first).reshape(4 * chans, 72)
    last_w = jnp.einsum("tcd,tmp->mcpd", w_out, last).reshape(72, 4 * chans)
    down_w = jnp.transpose(w_down, (1, 0, 2)).reshape(chans, 4 * chans)
    mid_w = jnp.transpose(w_mid, (1, 0, 2)).reshape(chans, 9 * chans)
    return pl.pallas_call(
        denoise_kernel,
        out_shape=jax.ShapeDtypeStruct((2, ROWS, COLS), f32),
        in_specs=[smem_spec(), smem_spec()] + [vmem_spec()] * 8,
        out_specs=vmem_spec(),
        scratch_shapes=[
            pltpu.VMEM((2, 2 * (ROWS + 2 * HALO), 128), f32),
            pltpu.VMEM((8, FLAT), f32),
            pltpu.VMEM((72, FLAT), bf16),
            pltpu.VMEM((4 * chans, FLAT), bf16),
            pltpu.VMEM((chans, FLAT), f32),
            pltpu.VMEM((9 * chans, FLAT), bf16),
            pltpu.VMEM((4 * chans, FLAT), bf16),
            pltpu.VMEM((72, FLAT), f32),
            pltpu.VMEM((2, 2 * ROWS, 128), f32),
        ],
        cost_estimate=pl.CostEstimate(
            flops=4 * 10**9, bytes_accessed=2 * 10**7, transcendentals=0
        ),
        name="denoise",
    )(
        meta,
        b_out,
        extended,
        first_w,
        b_in.reshape(chans, 1),
        down_w,
        b_down.reshape(chans, 1),
        mid_w,
        b_mid.reshape(chans, 1),
        last_w,
    )


def per_device(
    obj_x,
    dual_u,
    probes,
    intensity,
    corners,
    owner,
    w_in,
    b_in,
    w_down,
    b_down,
    w_mid,
    b_mid,
    w_out,
    b_out,
):
    x = lax.axis_index("x")
    z = lax.axis_index("z")
    core = lax.axis_index("core")
    mode = lax.axis_index("mode")
    tiles = NX * NZ * NC
    lanes = jnp.arange(tiles, dtype=jnp.int32)
    owned = owner[None, :] == lanes[:, None]
    by_owner = jnp.sum(jnp.where(owned[None], corners[:, None, :], 0), axis=2)
    place = jnp.where(lanes == 0, x, jnp.where(lanes == 1, z, jnp.where(lanes == 2, core, mode)))
    meta = jnp.concatenate([by_owner, place[None]], axis=0).astype(jnp.int32)

    low = obj_x.astype(bf16).reshape(1, 2 * ROWS, COLS)
    near = lax.all_to_all(jnp.broadcast_to(low, (NZ, 2 * ROWS, COLS)), "z", 0, 0, tiled=True)
    probe0 = probes[0].astype(bf16)
    others = [
        lax.ppermute(probe0, "mode", [(i, (i + k) % NM) for i in range(NM)]) for k in range(1, NM)
    ]
    all_probes = (probe0, *others)
    packed = pl.pallas_call(
        pack_kernel,
        out_shape=jax.ShapeDtypeStruct((NX * NC, HALF, 2 * ROWS, COLS), bf16),
        in_specs=[smem_spec(), vmem_spec()],
        out_specs=vmem_spec(),
        name="pack",
    )(meta, near)
    got = lax.all_to_all(packed, ("x", "core"), 0, 0, tiled=True)
    window = pl.pallas_call(
        window_kernel,
        out_shape=jax.ShapeDtypeStruct((2, PATCH, COLS), bf16),
        in_specs=[smem_spec(), vmem_spec()],
        out_specs=vmem_spec(),
        scratch_shapes=[pltpu.VMEM((2, STRIPS * ROWS, COLS), f32)],
        name="window",
    )(meta, got)
    wins = lax.all_gather(window, "mode", axis=0)
    updates, misfit = pl.pallas_call(
        wave_kernel,
        out_shape=(
            jax.ShapeDtypeStruct((NX * NC, HALF, 2 * ROWS, COLS), bf16),
            jax.ShapeDtypeStruct((1, 1), f32),
        ),
        in_specs=[smem_spec()] + [vmem_spec()] * 7,
        out_specs=(vmem_spec(), vmem_spec()),
        scratch_shapes=[
            pltpu.VMEM((NM, PATCH, 2 * PATCH), f32),
            pltpu.VMEM((2, STRIPS * ROWS, COLS), f32),
        ],
        name="wave",
    )(meta, wins, *all_probes, intensity, dft_table())
    back = lax.all_to_all(updates, ("x", "core"), 0, 0, tiled=True)
    partial = pl.pallas_call(
        gather_kernel,
        out_shape=jax.ShapeDtypeStruct((NZ, 2 * ROWS, COLS), bf16),
        in_specs=[smem_spec(), vmem_spec()],
        out_specs=vmem_spec(),
        scratch_shapes=[pltpu.VMEM((NZ, 2 * ROWS, COLS), f32)],
        name="gather",
    )(meta, back)
    pieces = lax.all_to_all(partial, "z", 0, 0, tiled=True)
    denom = pl.pallas_call(
        weight_kernel,
        out_shape=jax.ShapeDtypeStruct((ROWS, COLS), f32),
        in_specs=[smem_spec()] + [vmem_spec()] * NM,
        out_specs=vmem_spec(),
        scratch_shapes=[pltpu.VMEM((PATCH // COLS + 2, PATCH + 2 * ROWS, COLS), f32)],
        name="weight",
    )(meta, *all_probes)
    base = obj_x + dual_u
    center = denoise(base, meta, w_in, b_in, w_down, b_down, w_mid, b_mid, w_out, b_out)
    aux_next = base - center
    numer = jnp.sum(pieces.astype(f32), axis=0).reshape(2, ROWS, COLS)
    obj_next = (numer + rho_weight * (aux_next - dual_u)) / (denom + rho_weight)
    dual_next = dual_u + obj_next - aux_next
    return (obj_next, aux_next, dual_next, misfit.reshape(1))


def solution(mesh):
    split = Mesh(mesh.devices.reshape(NX, NZ, NC, NM), TILE_AXES + ("mode",))
    grid = P(None, TILE_AXES, "mode")
    return jax.shard_map(
        per_device,
        mesh=split,
        in_specs=(
            grid,
            grid,
            P("mode", None, None, None),
            P(TILE_AXES, None, None),
        )
        + (P(),) * 10,
        out_specs=(grid, grid, grid, P(TILE_AXES)),
        check_vma=False,
    )
```

time: 1980 us -> 133 us (0.07)
  the two profiles are of different devices: /device:TPU:2 before, /device:TPU:40 now
where the time goes in v1:
time: 133 us; the launch traced here: 131 us
  starting transfers between devices  52.7 us (40%)
  Pallas kernels  23.8 us (18%)
  waiting for transfers between devices  21.5 us (16%)
  blocking collectives  14.7 us (11%)
  local copies, waits for them, and re-layouts  13 us (10%)
  other arithmetic  3.74 us (3%)
    all_to_all x1, waiting for transfers between devices, per_device(): lax.all_to_all(jnp.broadcast_to(low, (NZ, 2 * ROWS, COLS)), 'z', 0, 0, ti...  15.9 us
    all_to_all x1, starting transfers between devices, per_device(): lax.all_to_all(jnp.broadcast_to(low, (NZ, 2 * ROWS, COLS)), 'z', 0, 0, ti...  15.2 us
    all_gather x1, blocking collectives, per_device(): wins = lax.all_gather(window, 'mode', axis=0)  14.7 us
    ppermute x4, starting transfers between devices, shifted(): return lax.ppermute(value, axes, pairs)  11.5 us
    ppermute x3, starting transfers between devices, per_device(): lax.ppermute(probe0, 'mode', [(i, (i + k) % NM) for i in range(NM)])  10.7 us
    unnamed x42, local copies, waits for them, and re-layouts  7.8 us
    pallas_call x1, Pallas kernels, denoise(): pl.pallas_call(denoise_kernel, out_shape=jax.ShapeDtypeStruct((2, ROWS, C...  6.66 us
    pallas_call x1, Pallas kernels, per_device(): pl.pallas_call(wave_kernel, out_shape=(jax.ShapeDtypeStruct((NX * NC, HAL...  6.36 us
  transfers between devices with their start and end apart: 11, of which 3 were waited for; matrix products, arithmetic and copies ran while one was open for 6% of the time, Pallas kernels for 12%

profile of v1, /device:TPU:40, one launch (start us, length us, event | category | flops | bytes accessed | tf_op | source)
XLA Modules:
  0.0 131.3 jit_solution(9759860927085915463)
XLA Ops:
  0.6 0.8 fusion.5
  1.5 0.7 broadcast_in_dim.56
  2.2 15.2 %all-to-all-start = ((bf16[16,64,128]{2,1,0:T(8,128)(2,1)}), bf16[16,64,128]{2,1,0:T(8,128)(2,1)S(1)}, u32[]{:S(2)}, u32[]{:S(2)}) async-start(bf16[16,64,128]{2,1,0:T(8,128)(2,1)} %broadcast_in_dim.56), calls=%async_computation | async-start | bytes 524288 | tf_op jit(solution)/shard_map/all_to_all | solution.py:413
  17.5 0.6 copy-done.17
  18.1 0.7 copy-done.16
  18.8 0.1 select_reduce_fusion
  18.9 0.6 pad_add_fusion.meta
  19.5 15.9 %all-to-all-done.near = bf16[16,64,128]{2,1,0:T(8,128)(2,1)S(1)} async-done(((bf16[16,64,128]{2,1,0:T(8,128)(2,1)}), bf16[16,64,128]{2,1,0:T(8,128)(2,1)S(1)}, u32[]{:S(2)}, u32[]{:S(2)}) %all-to-all-start) | async-done | bytes 262176 | tf_op jit(solution)/shard_map/all_to_all | solution.py:413
  35.3 0.7 copy-done.3
  36.1 2.1 %pack.1 = bf16[8,5,64,128]{3,2,1,0:T(8,128)(2,1)} custom-call(s32[3,128]{1,0:T(4,128)} %pad_add_fusion.meta, bf16[16,64,128]{2,1,0:T(8,128)(2,1)} %copy-done.3), custom_call_target="tpu_custom_call" | custom-call | tf_op jit(solution)/shard_map/pack/pallas_call | solution.py:419
  38.2 4.4 %all-to-all-start.1 = ((bf16[8,5,64,128]{3,2,1,0:T(8,128)(2,1)}), bf16[8,5,64,128]{3,2,1,0:T(8,128)(2,1)S(1)}, u32[]{:S(2)}, u32[]{:S(2)}) async-start(bf16[8,5,64,128]{3,2,1,0:T(8,128)(2,1)} %pack.1), calls=%async_computation.1 | async-start | bytes 1310720 | tf_op jit(solution)/shard_map/all_to_all | solution.py:426
  42.7 3.5 %collective-permute-start = (bf16[2,256,256]{2,1,0:T(8,128)(2,1)S(1)}, bf16[2,256,256]{2,1,0:T(8,128)(2,1)S(1)}, u32[]{:S(2)}, u32[]{:S(2)}) collective-permute-start(bf16[2,256,256]{2,1,0:T(8,128)(2,1)S(1)} %convert_bitcast_fusion.probe0), channel_id=1, source_target_pairs={{0,1},{1,2},{2,3},{3,0},{4,5},{5,6},{6,7},{7,4},{8,9},{9,10},{10,1... | collective-permute-start | bytes 786440 | tf_op jit(solution)/shard_map/ppermute | solution.py:416
  46.2 2.8 %collective-permute-start.1 = (bf16[2,256,256]{2,1,0:T(8,128)(2,1)S(1)}, bf16[2,256,256]{2,1,0:T(8,128)(2,1)S(1)}, u32[]{:S(2)}, u32[]{:S(2)}) collective-permute-start(bf16[2,256,256]{2,1,0:T(8,128)(2,1)S(1)} %convert_bitcast_fusion.probe0), channel_id=1, source_target_pairs={{0,2},{1,3},{2,0},{3,1},{4,6},{5,7},{6,4},{7,5},{8,10},{9,11},{10,... | collective-permute-start | bytes 786440 | tf_op jit(solution)/shard_map/ppermute | solution.py:416
  49.0 4.3 %collective-permute-start.2 = (bf16[2,256,256]{2,1,0:T(8,128)(2,1)S(1)}, bf16[2,256,256]{2,1,0:T(8,128)(2,1)S(1)}, u32[]{:S(2)}, u32[]{:S(2)}) collective-permute-start(bf16[2,256,256]{2,1,0:T(8,128)(2,1)S(1)} %convert_bitcast_fusion.probe0), channel_id=1, source_target_pairs={{0,3},{1,0},{2,1},{3,2},{4,7},{5,4},{6,5},{7,6},{8,11},{9,8},{10,9... | collective-permute-start | bytes 786440 | tf_op jit(solution)/shard_map/ppermute | solution.py:416
  53.4 1.0 all-to-all-done.1.got
  54.4 0.8 copy-done.1
  55.2 1.8 %window.1 = bf16[2,256,128]{2,1,0:T(8,128)(2,1)} custom-call(s32[3,128]{1,0:T(4,128)} %pad_add_fusion.meta, bf16[8,5,64,128]{3,2,1,0:T(8,128)(2,1)} %copy-done.1), custom_call_target="tpu_custom_call" | custom-call | tf_op jit(solution)/shard_map/window/pallas_call | solution.py:427
  57.0 14.7 %all-gather = bf16[8,256,128]{2,1,0:T(8,128)(2,1)} all-gather(bf16[2,256,128]{2,1,0:T(8,128)(2,1)} %window.1), channel_id=2, replica_groups=mesh['x'=4,'z'=16,'core'=2,'mode'=4] {'mode'}, dimensions={0}, use_global_device_ids=true | all-gather | bytes 655360 | tf_op jit(solution)/shard_map/all_gather | solution.py:435
  71.7 0.0 collective-permute-done.probe1
  71.7 0.0 collective-permute-done.1.probe2
  71.7 0.0 collective-permute-done.2.probe3
  71.8 0.7 copy-done.4
  72.4 0.1 copy-done.5
  72.5 0.1 copy-done.6
  72.6 6.4 %wave.1 = (bf16[8,5,64,128]{3,2,1,0:T(8,128)(2,1)}, f32[1,1]{1,0:T(1,128)}) custom-call(s32[3,128]{1,0:T(4,128)} %pad_add_fusion.meta, bf16[4,2,256,128]{3,2,1,0:T(8,128)(2,1)} %bitcast.31, bf16[2,256,256]{2,1,0:T(8,128)(2,1)} %copy-done.2, bf16[2,256,256]{2,1,0:T(8,128)(2,1)} %copy-done.4, bf16[2,256,256]{2,1,0:T(8,128)(2,1)} %copy-done.5, ...), custom_call_target="tpu_custom_call" | custom-call | tf_op jit(solution)/shard_map/wave/pallas_call | solution.py:436
  79.0 4.6 %all-to-all-start.2 = ((bf16[8,5,64,128]{3,2,1,0:T(8,128)(2,1)}), bf16[8,5,64,128]{3,2,1,0:T(8,128)(2,1)S(1)}, u32[]{:S(2)}, u32[]{:S(2)}) async-start(bf16[8,5,64,128]{3,2,1,0:T(8,128)(2,1)} %get-tuple-element.6), calls=%async_computation.2 | async-start | bytes 1310720 | tf_op jit(solution)/shard_map/all_to_all | solution.py:450
  83.6 0.0 copy-start.14
  83.6 2.5 %collective-permute-start.3 = (bf16[2,6,128]{2,1,0:T(8,128)(2,1)S(1)}, bf16[2,6,128]{2,1,0:T(8,128)(2,1)S(1)}, u32[]{:S(2)}, u32[]{:S(2)}) collective-permute-start(bf16[2,6,128]{2,1,0:T(8,128)(2,1)S(1)} %get-tuple-element.16), channel_id=1, source_target_pairs={{0,4},{4,8},{8,12},{12,16},{16,20},{20,24},{24,28},{28,32},{32,36}... | collective-permute-start | bytes 9224 | tf_op jit(solution)/shard_map/ppermute | solution.py:29
  86.1 0.0 copy-start.12
  86.2 3.0 %collective-permute-start.4 = (bf16[2,6,128]{2,1,0:T(8,128)(2,1)S(1)}, bf16[2,6,128]{2,1,0:T(8,128)(2,1)S(1)}, u32[]{:S(2)}, u32[]{:S(2)}) collective-permute-start(bf16[2,6,128]{2,1,0:T(8,128)(2,1)S(1)} %get-tuple-element.17), channel_id=1, source_target_pairs={{4,0},{8,4},{12,8},{16,12},{20,16},{24,20},{28,24},{32,28},{36,32}... | collective-permute-start | bytes 9224 | tf_op jit(solution)/shard_map/ppermute | solution.py:29
  89.2 0.0 copy-start.15
  89.2 0.2 convolution_bitcast_fusion
  89.4 0.5 copy-done.15
  89.9 0.8 fusion.1
  90.7 4.6 %all-to-all-done.2.got = bf16[8,5,64,128]{3,2,1,0:T(8,128)(2,1)S(1)} async-done(((bf16[8,5,64,128]{3,2,1,0:T(8,128)(2,1)}), bf16[8,5,64,128]{3,2,1,0:T(8,128)(2,1)S(1)}, u32[]{:S(2)}, u32[]{:S(2)}) %all-to-all-start.2) | async-done | bytes 655392 | tf_op jit(solution)/shard_map/all_to_all | solution.py:450
  95.3 0.8 copy-done
  96.1 2.2 %gather.1 = bf16[16,64,128]{2,1,0:T(8,128)(2,1)} custom-call(s32[3,128]{1,0:T(4,128)} %pad_add_fusion.meta, bf16[8,5,64,128]{3,2,1,0:T(8,128)(2,1)} %copy-done), custom_call_target="tpu_custom_call" | custom-call | tf_op jit(solution)/shard_map/gather/pallas_call | solution.py:451
  98.3 6.2 %all-to-all-start.3 = ((bf16[16,64,128]{2,1,0:T(8,128)(2,1)}), bf16[16,64,128]{2,1,0:T(8,128)(2,1)S(1)}, u32[]{:S(2)}, u32[]{:S(2)}) async-start(bf16[16,64,128]{2,1,0:T(8,128)(2,1)} %gather.1), calls=%async_computation.3 | async-start | bytes 524288 | tf_op jit(solution)/shard_map/all_to_all | solution.py:459
  104.6 0.0 collective-permute-done.3
  104.6 0.0 collective-permute-done.4
  104.6 0.1 fusion.6
  104.7 1.9 %collective-permute-start.5 = (bf16[2,44,6]{2,1,0:T(8,128)(2,1)S(1)}, bf16[2,44,6]{2,1,0:T(8,128)(2,1)S(1)}, u32[]{:S(2)}, u32[]{:S(2)}) collective-permute-start(bf16[2,44,6]{2,1,0:T(8,128)(2,1)S(1)} %get-tuple-element.14), channel_id=1, source_target_pairs={{0,1},{1,2},{2,3},{4,5},{5,6},{6,7},{8,9},{9,10},{10,11},{12,13},{... | collective-permute-start | bytes 3176 | tf_op jit(solution)/shard_map/ppermute | solution.py:29
  106.6 0.0 copy-start.9
  106.6 4.1 %collective-permute-start.6 = (bf16[2,44,6]{2,1,0:T(8,128)(2,1)S(1)}, bf16[2,44,6]{2,1,0:T(8,128)(2,1)S(1)}, u32[]{:S(2)}, u32[]{:S(2)}) collective-permute-start(bf16[2,44,6]{2,1,0:T(8,128)(2,1)S(1)} %get-tuple-element.15), channel_id=1, source_target_pairs={{1,0},{2,1},{3,2},{5,4},{6,5},{7,6},{9,8},{10,9},{11,10},{13,12},{... | collective-permute-start | bytes 3176 | tf_op jit(solution)/shard_map/ppermute | solution.py:29
  110.7 0.7 reshape.96.last_w
  111.4 0.1 copy.49
  111.6 0.0 copy-start.10
  111.6 0.7 copy.54.mid_w
  112.3 0.1 copy-done.10
  112.4 0.7 reshape.92.down_w
  113.1 0.7 copy-done.18
  113.8 0.7 copy.52.first_b
  114.5 0.7 copy-done.19
  115.1 0.7 copy.53.down_b
  115.8 0.7 copy-done.20
  116.5 0.7 copy.55.mid_b
  117.1 0.0 collective-permute-done.5
  117.1 0.7 pad_maximum_fusion.ext
  117.9 6.7 %denoise.1 = f32[2,32,128]{2,1,0:T(8,128)} custom-call(s32[3,128]{1,0:T(4,128)} %pad_add_fusion.meta, f32[2]{0:T(128)} %b_out.1, bf16[2,44,140]{2,1,0:T(8,128)(2,1)} %pad_maximum_fusion.ext, bf16[192,72]{1,0:T(8,128)(2,1)} %bitcast.37, f32[48,1]{1,0:T(8,128)} %copy.52.first_b, bf16[48,192]{1,0:T(8,128)(2,1)} %reshape.92.down_w, f32[48,1]{1,0:T(8,128)} %copy.53.down_b, ...), custom_call_target="tpu_custom_call" | custom-call | flops 4000000000 | bytes 20000000 | tf_op jit(solution)/shard_map/denoise/pallas_call | solution.py:351
  124.5 4.6 %weight.1 = f32[32,128]{1,0:T(8,128)} custom-call(s32[3,128]{1,0:T(4,128)} %pad_add_fusion.meta, bf16[2,256,256]{2,1,0:T(8,128)(2,1)} %copy-done.2, bf16[2,256,256]{2,1,0:T(8,128)(2,1)} %copy-done.4, bf16[2,256,256]{2,1,0:T(8,128)(2,1)} %copy-done.5, bf16[2,256,256]{2,1,0:T(8,128)(2,1)} %copy-done.6), custom_call_target="tpu_custom_call" | custom-call | tf_op jit(solution)/shard_map/weight/pallas_call | solution.py:460
  129.2 0.7 broadcast_add_fusion
  129.9 0.7 copy-done.8
  130.6 0.0 copy-done.11
  130.7 0.6 add_subtract_fusion
  (32 shorter events, 0.2 us)
Async XLA Ops:
  2.2 33.1 %all-to-all-start = ((bf16[16,64,128]{2,1,0:T(8,128)(2,1)}), bf16[16,64,128]{2,1,0:T(8,128)(2,1)S(1)}, u32[]{:S(2)}, u32[]{:S(2)}) async-start(bf16[16,64,128]{2,1,0:T(8,128)(2,1)} %broadcast_in_dim.56), calls=%async_computation | async-start | bytes 524288 | tf_op jit(solution)/shard_map/all_to_all | solution.py:413
  17.4 0.7 copy-start.17
  18.1 0.7 copy-start.16
  35.3 0.7 copy-start.3
  38.2 4.4 %copy-start.7 = (f32[1,2,256,256]{3,2,1,0:T(8,128)S(1)}, f32[1,2,256,256]{3,2,1,0:T(8,128)}, u32[]{:S(2)}) copy-start(f32[1,2,256,256]{3,2,1,0:T(8,128)} %param.19) | copy-start | bytes 1572868
  38.2 16.2 %all-to-all-start.1 = ((bf16[8,5,64,128]{3,2,1,0:T(8,128)(2,1)}), bf16[8,5,64,128]{3,2,1,0:T(8,128)(2,1)S(1)}, u32[]{:S(2)}, u32[]{:S(2)}) async-start(bf16[8,5,64,128]{3,2,1,0:T(8,128)(2,1)} %pack.1), calls=%async_computation.1 | async-start | bytes 1310720 | tf_op jit(solution)/shard_map/all_to_all | solution.py:426
  42.7 29.1 %copy-start.2 = (bf16[2,256,256]{2,1,0:T(8,128)(2,1)}, bf16[2,256,256]{2,1,0:T(8,128)(2,1)S(1)}, u32[]{:S(2)}) copy-start(bf16[2,256,256]{2,1,0:T(8,128)(2,1)S(1)} %convert_bitcast_fusion.probe0) | copy-start | bytes 786436
  42.7 29.0 %collective-permute-start = (bf16[2,256,256]{2,1,0:T(8,128)(2,1)S(1)}, bf16[2,256,256]{2,1,0:T(8,128)(2,1)S(1)}, u32[]{:S(2)}, u32[]{:S(2)}) collective-permute-start(bf16[2,256,256]{2,1,0:T(8,128)(2,1)S(1)} %convert_bitcast_fusion.probe0), channel_id=1, source_target_pairs={{0,1},{1,2},{2,3},{3,0},{4,5},{5,6},{6,7},{7,4},{8,9},{9,10},{10,1... | collective-permute-start | bytes 786440 | tf_op jit(solution)/shard_map/ppermute | solution.py:416
  46.2 25.6 %collective-permute-start.1 = (bf16[2,256,256]{2,1,0:T(8,128)(2,1)S(1)}, bf16[2,256,256]{2,1,0:T(8,128)(2,1)S(1)}, u32[]{:S(2)}, u32[]{:S(2)}) collective-permute-start(bf16[2,256,256]{2,1,0:T(8,128)(2,1)S(1)} %convert_bitcast_fusion.probe0), channel_id=1, source_target_pairs={{0,2},{1,3},{2,0},{3,1},{4,6},{5,7},{6,4},{7,5},{8,10},{9,11},{10,... | collective-permute-start | bytes 786440 | tf_op jit(solution)/shard_map/ppermute | solution.py:416
  49.0 22.7 %collective-permute-start.2 = (bf16[2,256,256]{2,1,0:T(8,128)(2,1)S(1)}, bf16[2,256,256]{2,1,0:T(8,128)(2,1)S(1)}, u32[]{:S(2)}, u32[]{:S(2)}) collective-permute-start(bf16[2,256,256]{2,1,0:T(8,128)(2,1)S(1)} %convert_bitcast_fusion.probe0), channel_id=1, source_target_pairs={{0,3},{1,0},{2,1},{3,2},{4,7},{5,4},{6,5},{7,6},{8,11},{9,8},{10,9... | collective-permute-start | bytes 786440 | tf_op jit(solution)/shard_map/ppermute | solution.py:416
  54.4 0.8 copy-start.1
  71.7 0.7 copy-start.4
  71.7 0.8 copy-start.5
  71.8 0.9 copy-start.6
  79.0 16.3 %all-to-all-start.2 = ((bf16[8,5,64,128]{3,2,1,0:T(8,128)(2,1)}), bf16[8,5,64,128]{3,2,1,0:T(8,128)(2,1)S(1)}, u32[]{:S(2)}, u32[]{:S(2)}) async-start(bf16[8,5,64,128]{3,2,1,0:T(8,128)(2,1)} %get-tuple-element.6), calls=%async_computation.2 | async-start | bytes 1310720 | tf_op jit(solution)/shard_map/all_to_all | solution.py:450
  83.6 5.6 %copy-start.13 = (bf16[9,36,4,1]{1,0,3,2:T(8,128)(2,1)S(1)}, bf16[9,36,4,1]{1,0,3,2:T(8,128)(2,1)}, u32[]{:S(2)}) copy-start(bf16[9,36,4,1]{1,0,3,2:T(8,128)(2,1)} %constant.46) | copy-start | bytes 7780
  83.6 5.6 %copy-start.14 = (bf16[9,2,48]{2,1,0:T(2,128)(2,1)S(1)}, bf16[9,2,48]{2,1,0:T(2,128)(2,1)}, u32[]{:S(2)}) copy-start(bf16[9,2,48]{2,1,0:T(2,128)(2,1)} %param.29) | copy-start | bytes 5188
  83.6 21.0 %collective-permute-start.3 = (bf16[2,6,128]{2,1,0:T(8,128)(2,1)S(1)}, bf16[2,6,128]{2,1,0:T(8,128)(2,1)S(1)}, u32[]{:S(2)}, u32[]{:S(2)}) collective-permute-start(bf16[2,6,128]{2,1,0:T(8,128)(2,1)S(1)} %get-tuple-element.16), channel_id=1, source_target_pairs={{0,4},{4,8},{8,12},{12,16},{16,20},{20,24},{24,28},{28,32},{32,36}... | collective-permute-start | bytes 9224 | tf_op jit(solution)/shard_map/ppermute | solution.py:29
  86.1 3.3 %copy-start.12 = (bf16[9,2,4,72]{3,0,1,2:T(8,128)(2,1)S(1)}, bf16[9,2,4,72]{3,0,1,2:T(8,128)(2,1)}, u32[]{:S(2)}) copy-start(bf16[9,2,4,72]{3,0,1,2:T(8,128)(2,1)} %constant.44) | copy-start | bytes 31108
  86.2 18.4 %collective-permute-start.4 = (bf16[2,6,128]{2,1,0:T(8,128)(2,1)S(1)}, bf16[2,6,128]{2,1,0:T(8,128)(2,1)S(1)}, u32[]{:S(2)}, u32[]{:S(2)}) collective-permute-start(bf16[2,6,128]{2,1,0:T(8,128)(2,1)S(1)} %get-tuple-element.17), channel_id=1, source_target_pairs={{4,0},{8,4},{12,8},{16,12},{20,16},{24,20},{28,24},{32,28},{36,32}... | collective-permute-start | bytes 9224 | tf_op jit(solution)/shard_map/ppermute | solution.py:29
  89.2 0.7 copy-start.15
  95.3 0.8 copy-start
  98.3 31.6 %all-to-all-start.3 = ((bf16[16,64,128]{2,1,0:T(8,128)(2,1)}), bf16[16,64,128]{2,1,0:T(8,128)(2,1)S(1)}, u32[]{:S(2)}, u32[]{:S(2)}) async-start(bf16[16,64,128]{2,1,0:T(8,128)(2,1)} %gather.1), calls=%async_computation.3 | async-start | bytes 524288 | tf_op jit(solution)/shard_map/all_to_all | solution.py:459
  104.7 12.5 %collective-permute-start.5 = (bf16[2,44,6]{2,1,0:T(8,128)(2,1)S(1)}, bf16[2,44,6]{2,1,0:T(8,128)(2,1)S(1)}, u32[]{:S(2)}, u32[]{:S(2)}) collective-permute-start(bf16[2,44,6]{2,1,0:T(8,128)(2,1)S(1)} %get-tuple-element.14), channel_id=1, source_target_pairs={{0,1},{1,2},{2,3},{4,5},{5,6},{6,7},{8,9},{9,10},{10,11},{12,13},{... | collective-permute-start | bytes 3176 | tf_op jit(solution)/shard_map/ppermute | solution.py:29
  106.6 4.8 %copy-start.9 = (bf16[9,48,48]{2,1,0:T(8,128)(2,1)S(1)}, bf16[9,48,48]{2,1,0:T(8,128)(2,1)}, u32[]{:S(2)}) copy-start(bf16[9,48,48]{2,1,0:T(8,128)(2,1)} %param.27) | copy-start | bytes 124420
  106.6 10.5 %collective-permute-start.6 = (bf16[2,44,6]{2,1,0:T(8,128)(2,1)S(1)}, bf16[2,44,6]{2,1,0:T(8,128)(2,1)S(1)}, u32[]{:S(2)}, u32[]{:S(2)}) collective-permute-start(bf16[2,44,6]{2,1,0:T(8,128)(2,1)S(1)} %get-tuple-element.15), channel_id=1, source_target_pairs={{1,0},{2,1},{3,2},{5,4},{6,5},{7,6},{9,8},{10,9},{11,10},{13,12},{... | collective-permute-start | bytes 3176 | tf_op jit(solution)/shard_map/ppermute | solution.py:29
  111.6 0.8 copy-start.10
  113.1 0.7 copy-start.18
  114.5 0.7 copy-start.19
  115.8 0.7 copy-start.20
  129.9 0.8 copy-start.8
  129.9 0.8 copy-start.11

commit v2 on v1

--- a/solution.py
+++ b/solution.py
@@ -39,6 +39,7 @@
         value = jnp.concatenate([before, value, after], axis=dim)
     return value
 
+
 def vmem_spec():
     return pl.BlockSpec(memory_space=pltpu.VMEM)
 
@@ -56,7 +57,7 @@
 
 
 def pack_kernel(meta, near, out):
-    x, z, core, mode = ids(meta)
+    _, z, core, _ = ids(meta)
     for target in range(NX * NC):
         tx, tc = target // NC, target % NC
         tile = tx * (NZ * NC) + z * NC + tc
@@ -67,7 +68,7 @@
 
 
 def window_kernel(meta, got, out, tall):
-    x, z, core, mode = ids(meta)
+    x, z, core, _ = ids(meta)
     row = meta[0, x * (NZ * NC) + z * NC + core]
     s0 = row // ROWS
     for i in range(STRIPS):
@@ -162,7 +163,7 @@
 
 
 def gather_kernel(meta, got, out, acc):
-    x, z, core, mode = ids(meta)
+    _, z, core, _ = ids(meta)
     acc[...] = jnp.zeros(acc.shape, f32)
     for source in range(NX * NC):
         sx, sc = source // NC, source % NC
@@ -413,7 +414,8 @@
     near = lax.all_to_all(jnp.broadcast_to(low, (NZ, 2 * ROWS, COLS)), "z", 0, 0, tiled=True)
     probe0 = probes[0].astype(bf16)
     others = [
-        lax.ppermute(probe0, "mode", [(i, (i + k) % NM) for i in range(NM)]) for k in range(1, NM)
+        lax.ppermute(probe0, "mode", [(i, (i + k) % NM) for i in range(NM)])
+        for k in range(1, NM)
     ]
     all_probes = (probe0, *others)
     packed = pl.pallas_call(
@@ -432,7 +434,7 @@
         scratch_shapes=[pltpu.VMEM((2, STRIPS * ROWS, COLS), f32)],
         name="window",
     )(meta, got)
-    wins = lax.all_gather(window, "mode", axis=0)
+    wins = lax.all_to_all(jnp.broadcast_to(window, (NM, *window.shape)), "mode", 0, 0, tiled=True)
     updates, misfit = pl.pallas_call(
         wave_kernel,
         out_shape=(

time: 133 us -> 143 us (1.075)
  waiting for transfers between devices: 21.5 us -> 29.3 us
  local copies, waits for them, and re-layouts: 13 us -> 14.6 us
  blocking collectives: 14.7 us -> 16.2 us
    all_to_all x0 -> x1, blocking collectives: none -> 16.2 us  [per_device(): got = lax.all_to_all(packed, ('x', 'core'), 0, 0, tiled=True)]
    all_gather x1 -> x0, blocking collectives: 14.7 us -> none  [per_device(): wins = lax.all_gather(window, 'mode', axis=0)]
    ppermute x3, waiting for transfers between devices: 0.01 us -> 8.95 us  [per_device(): lax.ppermute(probe0, 'mode', [(i, (i + k) % NM) for i in range(NM)])]
    broadcast_in_dim x0 -> x1, local copies, waits for them, and re-layouts: none -> 1.75 us  [per_device(): jnp.broadcast_to(window, (NM, *window.shape))]
  transfers between devices with their start and end apart: 11 -> 11, of which waited for: 3 -> 4; matrix products, arithmetic and copies ran while one was open for 6% -> 5% of each run, Pallas kernels for 12% -> 10%
where the time goes in v2:
time: 143 us; the launch traced here: 142 us
  starting transfers between devices  52 us (36%)
  waiting for transfers between devices  29.3 us (20%)
  Pallas kernels  23.9 us (17%)
  blocking collectives  16.2 us (11%)
  local copies, waits for them, and re-layouts  14.6 us (10%)
  other arithmetic  3.74 us (3%)
    all_to_all x1, blocking collectives, per_device(): got = lax.all_to_all(packed, ('x', 'core'), 0, 0, tiled=True)  16.2 us
    all_to_all x1, waiting for transfers between devices, per_device(): lax.all_to_all(jnp.broadcast_to(low, (NZ, 2 * ROWS, COLS)), 'z', 0, 0, ti...  15.9 us
    all_to_all x1, starting transfers between devices, per_device(): lax.all_to_all(jnp.broadcast_to(low, (NZ, 2 * ROWS, COLS)), 'z', 0, 0, ti...  15.2 us
    ppermute x4, starting transfers between devices, shifted(): return lax.ppermute(value, axes, pairs)  11.5 us
    ppermute x3, starting transfers between devices, per_device(): lax.ppermute(probe0, 'mode', [(i, (i + k) % NM) for i in range(NM)])  10.4 us
    ppermute x3, waiting for transfers between devices, per_device(): lax.ppermute(probe0, 'mode', [(i, (i + k) % NM) for i in range(NM)])  8.95 us
    unnamed x42, local copies, waits for them, and re-layouts  7.6 us
    pallas_call x1, Pallas kernels, denoise(): pl.pallas_call(denoise_kernel, out_shape=jax.ShapeDtypeStruct((2, ROWS, C...  6.67 us
  transfers between devices with their start and end apart: 11, of which 4 were waited for; matrix products, arithmetic and copies ran while one was open for 5% of the time, Pallas kernels for 10%

profile of v2, /device:TPU:40, one launch (start us, length us, event | category | flops | bytes accessed | tf_op | source)
XLA Modules:
  0.0 141.6 jit_solution(2948471191079603669)
XLA Ops:
  0.6 0.8 fusion.5
  1.5 0.7 broadcast_in_dim.59
  2.2 15.2 %all-to-all-start = ((bf16[16,64,128]{2,1,0:T(8,128)(2,1)}), bf16[16,64,128]{2,1,0:T(8,128)(2,1)S(1)}, u32[]{:S(2)}, u32[]{:S(2)}) async-start(bf16[16,64,128]{2,1,0:T(8,128)(2,1)} %broadcast_in_dim.59), calls=%async_computation | async-start | bytes 524288 | tf_op jit(solution)/shard_map/all_to_all | solution.py:414
  17.5 0.6 copy-done.17
  18.1 0.7 copy-done.16
  18.8 0.1 select_reduce_fusion
  18.9 0.6 pad_add_fusion.meta
  19.5 15.9 %all-to-all-done.near = bf16[16,64,128]{2,1,0:T(8,128)(2,1)S(1)} async-done(((bf16[16,64,128]{2,1,0:T(8,128)(2,1)}), bf16[16,64,128]{2,1,0:T(8,128)(2,1)S(1)}, u32[]{:S(2)}, u32[]{:S(2)}) %all-to-all-start) | async-done | bytes 262176 | tf_op jit(solution)/shard_map/all_to_all | solution.py:414
  35.3 0.7 copy-done.3
  36.1 2.1 %pack.1 = bf16[8,5,64,128]{3,2,1,0:T(8,128)(2,1)} custom-call(s32[3,128]{1,0:T(4,128)} %pad_add_fusion.meta, bf16[16,64,128]{2,1,0:T(8,128)(2,1)} %copy-done.3), custom_call_target="tpu_custom_call" | custom-call | tf_op jit(solution)/shard_map/pack/pallas_call | solution.py:421
  38.2 16.2 %all_to_all.25.got = bf16[8,5,64,128]{3,2,1,0:T(8,128)(2,1)} all-to-all(bf16[8,5,64,128]{3,2,1,0:T(8,128)(2,1)} %pack.1), channel_id=1, replica_groups=mesh['x'=4,'z'=16,'core'=2,'mode'=4] {'x','core'}, dimensions={0} | all-to-all | bytes 1310720 | tf_op jit(solution)/shard_map/all_to_all | solution.py:428
  54.4 1.8 %window.1 = bf16[2,256,128]{2,1,0:T(8,128)(2,1)} custom-call(s32[3,128]{1,0:T(4,128)} %pad_add_fusion.meta, bf16[8,5,64,128]{3,2,1,0:T(8,128)(2,1)} %all_to_all.25.got), custom_call_target="tpu_custom_call" | custom-call | tf_op jit(solution)/shard_map/window/pallas_call | solution.py:429
  56.2 1.8 %broadcast_in_dim.60 = bf16[4,2,256,128]{3,2,1,0:T(8,128)(2,1)} broadcast(bf16[2,256,128]{2,1,0:T(8,128)(2,1)} %window.1), dimensions={1,2,3} | broadcast | bytes 655360 | tf_op jit(solution)/shard_map/broadcast_in_dim | solution.py:437
  58.0 5.0 %all-to-all-start.2 = ((bf16[4,2,256,128]{3,2,1,0:T(8,128)(2,1)}), bf16[4,2,256,128]{3,2,1,0:T(8,128)(2,1)S(1)}, u32[]{:S(2)}, u32[]{:S(2)}) async-start(bf16[4,2,256,128]{3,2,1,0:T(8,128)(2,1)} %broadcast_in_dim.60), calls=%async_computation.2 | async-start | bytes 1048576 | tf_op jit(solution)/shard_map/all_to_all | solution.py:437
  63.0 3.4 %collective-permute-start = (bf16[2,256,256]{2,1,0:T(8,128)(2,1)S(1)}, bf16[2,256,256]{2,1,0:T(8,128)(2,1)S(1)}, u32[]{:S(2)}, u32[]{:S(2)}) collective-permute-start(bf16[2,256,256]{2,1,0:T(8,128)(2,1)S(1)} %convert_bitcast_fusion.probe0), channel_id=1, source_target_pairs={{0,1},{1,2},{2,3},{3,0},{4,5},{5,6},{6,7},{7,4},{8,9},{9,10},{10,1... | collective-permute-start | bytes 786440 | tf_op jit(solution)/shard_map/ppermute | solution.py:417
  66.4 2.5 %collective-permute-start.1 = (bf16[2,256,256]{2,1,0:T(8,128)(2,1)S(1)}, bf16[2,256,256]{2,1,0:T(8,128)(2,1)S(1)}, u32[]{:S(2)}, u32[]{:S(2)}) collective-permute-start(bf16[2,256,256]{2,1,0:T(8,128)(2,1)S(1)} %convert_bitcast_fusion.probe0), channel_id=1, source_target_pairs={{0,2},{1,3},{2,0},{3,1},{4,6},{5,7},{6,4},{7,5},{8,10},{9,11},{10,... | collective-permute-start | bytes 786440 | tf_op jit(solution)/shard_map/ppermute | solution.py:417
  69.0 4.5 %collective-permute-start.2 = (bf16[2,256,256]{2,1,0:T(8,128)(2,1)S(1)}, bf16[2,256,256]{2,1,0:T(8,128)(2,1)S(1)}, u32[]{:S(2)}, u32[]{:S(2)}) collective-permute-start(bf16[2,256,256]{2,1,0:T(8,128)(2,1)S(1)} %convert_bitcast_fusion.probe0), channel_id=1, source_target_pairs={{0,3},{1,0},{2,1},{3,2},{4,7},{5,4},{6,5},{7,6},{8,11},{9,8},{10,9... | collective-permute-start | bytes 786440 | tf_op jit(solution)/shard_map/ppermute | solution.py:417
  73.5 6.1 %collective-permute-done.probe1 = bf16[2,256,256]{2,1,0:T(8,128)(2,1)S(1)} collective-permute-done((bf16[2,256,256]{2,1,0:T(8,128)(2,1)S(1)}, bf16[2,256,256]{2,1,0:T(8,128)(2,1)S(1)}, u32[]{:S(2)}, u32[]{:S(2)}) %collective-permute-start) | collective-permute-done | bytes 262176 | tf_op jit(solution)/shard_map/ppermute | solution.py:417
  79.6 0.0 collective-permute-done.1.probe2
  79.6 2.9 %collective-permute-done.2.probe3 = bf16[2,256,256]{2,1,0:T(8,128)(2,1)S(1)} collective-permute-done((bf16[2,256,256]{2,1,0:T(8,128)(2,1)S(1)}, bf16[2,256,256]{2,1,0:T(8,128)(2,1)S(1)}, u32[]{:S(2)}, u32[]{:S(2)}) %collective-permute-start.2) | collective-permute-done | bytes 262176 | tf_op jit(solution)/shard_map/ppermute | solution.py:417
  82.4 0.0 all-to-all-done.2.wins
  82.5 0.7 copy-done.6
  83.1 0.8 copy-done.2
  84.0 6.4 %wave.1 = (bf16[8,5,64,128]{3,2,1,0:T(8,128)(2,1)}, f32[1,1]{1,0:T(1,128)}) custom-call(s32[3,128]{1,0:T(4,128)} %pad_add_fusion.meta, bf16[4,2,256,128]{3,2,1,0:T(8,128)(2,1)} %copy-done.2, bf16[2,256,256]{2,1,0:T(8,128)(2,1)} %copy-done.1, bf16[2,256,256]{2,1,0:T(8,128)(2,1)} %copy-done.4, bf16[2,256,256]{2,1,0:T(8,128)(2,1)} %copy-done.5, ...), custom_call_target="tpu_custom_call" | custom-call | tf_op jit(solution)/shard_map/wave/pallas_call | solution.py:438
  90.3 3.5 %all-to-all-start.3 = ((bf16[8,5,64,128]{3,2,1,0:T(8,128)(2,1)}), bf16[8,5,64,128]{3,2,1,0:T(8,128)(2,1)S(1)}, u32[]{:S(2)}, u32[]{:S(2)}) async-start(bf16[8,5,64,128]{3,2,1,0:T(8,128)(2,1)} %get-tuple-element.6), calls=%async_computation.3 | async-start | bytes 1310720 | tf_op jit(solution)/shard_map/all_to_all | solution.py:452
  93.9 0.0 copy-start.13
  93.9 0.0 copy-start.14
  93.9 2.4 %collective-permute-start.3 = (bf16[2,6,128]{2,1,0:T(8,128)(2,1)S(1)}, bf16[2,6,128]{2,1,0:T(8,128)(2,1)S(1)}, u32[]{:S(2)}, u32[]{:S(2)}) collective-permute-start(bf16[2,6,128]{2,1,0:T(8,128)(2,1)S(1)} %get-tuple-element.16), channel_id=1, source_target_pairs={{0,4},{4,8},{8,12},{12,16},{16,20},{20,24},{24,28},{28,32},{32,36}... | collective-permute-start | bytes 9224 | tf_op jit(solution)/shard_map/ppermute | solution.py:29
  96.3 0.0 copy-start.12
  96.3 3.1 %collective-permute-start.4 = (bf16[2,6,128]{2,1,0:T(8,128)(2,1)S(1)}, bf16[2,6,128]{2,1,0:T(8,128)(2,1)S(1)}, u32[]{:S(2)}, u32[]{:S(2)}) collective-permute-start(bf16[2,6,128]{2,1,0:T(8,128)(2,1)S(1)} %get-tuple-element.17), channel_id=1, source_target_pairs={{4,0},{8,4},{12,8},{16,12},{20,16},{24,20},{28,24},{32,28},{36,32}... | collective-permute-start | bytes 9224 | tf_op jit(solution)/shard_map/ppermute | solution.py:29
  99.5 0.0 copy-start.15
  99.5 0.2 convolution_bitcast_fusion
  99.7 0.5 copy-done.15
  100.2 0.8 fusion.1
  101.0 4.5 %all-to-all-done.3.got = bf16[8,5,64,128]{3,2,1,0:T(8,128)(2,1)S(1)} async-done(((bf16[8,5,64,128]{3,2,1,0:T(8,128)(2,1)}), bf16[8,5,64,128]{3,2,1,0:T(8,128)(2,1)S(1)}, u32[]{:S(2)}, u32[]{:S(2)}) %all-to-all-start.3) | async-done | bytes 655392 | tf_op jit(solution)/shard_map/all_to_all | solution.py:452
  105.5 0.8 copy-done
  106.3 2.2 %gather.1 = bf16[16,64,128]{2,1,0:T(8,128)(2,1)} custom-call(s32[3,128]{1,0:T(4,128)} %pad_add_fusion.meta, bf16[8,5,64,128]{3,2,1,0:T(8,128)(2,1)} %copy-done), custom_call_target="tpu_custom_call" | custom-call | tf_op jit(solution)/shard_map/gather/pallas_call | solution.py:453
  108.5 6.2 %all-to-all-start.4 = ((bf16[16,64,128]{2,1,0:T(8,128)(2,1)}), bf16[16,64,128]{2,1,0:T(8,128)(2,1)S(1)}, u32[]{:S(2)}, u32[]{:S(2)}) async-start(bf16[16,64,128]{2,1,0:T(8,128)(2,1)} %gather.1), calls=%async_computation.4 | async-start | bytes 524288 | tf_op jit(solution)/shard_map/all_to_all | solution.py:461
  114.8 0.0 collective-permute-done.3
  114.8 0.1 fusion.6
  114.9 2.5 %collective-permute-start.5 = (bf16[2,44,6]{2,1,0:T(8,128)(2,1)S(1)}, bf16[2,44,6]{2,1,0:T(8,128)(2,1)S(1)}, u32[]{:S(2)}, u32[]{:S(2)}) collective-permute-start(bf16[2,44,6]{2,1,0:T(8,128)(2,1)S(1)} %get-tuple-element.14), channel_id=1, source_target_pairs={{0,1},{1,2},{2,3},{4,5},{5,6},{6,7},{8,9},{9,10},{10,11},{12,13},{... | collective-permute-start | bytes 3176 | tf_op jit(solution)/shard_map/ppermute | solution.py:29
  117.4 0.0 copy-start.9
  117.4 3.5 %collective-permute-start.6 = (bf16[2,44,6]{2,1,0:T(8,128)(2,1)S(1)}, bf16[2,44,6]{2,1,0:T(8,128)(2,1)S(1)}, u32[]{:S(2)}, u32[]{:S(2)}) collective-permute-start(bf16[2,44,6]{2,1,0:T(8,128)(2,1)S(1)} %get-tuple-element.15), channel_id=1, source_target_pairs={{1,0},{2,1},{3,2},{5,4},{6,5},{7,6},{9,8},{10,9},{11,10},{13,12},{... | collective-permute-start | bytes 3176 | tf_op jit(solution)/shard_map/ppermute | solution.py:29
  120.9 0.7 reshape.96.last_w
  121.6 0.1 copy.40
  121.8 0.0 copy-start.10
  121.8 0.7 copy.45.mid_w
  122.5 0.1 copy-done.10
  122.6 0.7 reshape.92.down_w
  123.3 0.7 copy-done.18
  124.0 0.7 copy.43.first_b
  124.7 0.7 copy-done.19
  125.3 0.7 copy.44.down_b
  126.0 0.7 copy-done.20
  126.7 0.7 copy.46.mid_b
  127.4 0.0 collective-permute-done.5
  127.4 0.0 collective-permute-done.6
  127.4 0.7 pad_maximum_fusion.ext
  128.1 6.7 %denoise.1 = f32[2,32,128]{2,1,0:T(8,128)} custom-call(s32[3,128]{1,0:T(4,128)} %pad_add_fusion.meta, f32[2]{0:T(128)} %b_out.1, bf16[2,44,140]{2,1,0:T(8,128)(2,1)} %pad_maximum_fusion.ext, bf16[192,72]{1,0:T(8,128)(2,1)} %bitcast.35, f32[48,1]{1,0:T(8,128)} %copy.43.first_b, bf16[48,192]{1,0:T(8,128)(2,1)} %reshape.92.down_w, f32[48,1]{1,0:T(8,128)} %copy.44.down_b, ...), custom_call_target="tpu_custom_call" | custom-call | flops 4000000000 | bytes 20000000 | tf_op jit(solution)/shard_map/denoise/pallas_call | solution.py:352
  134.7 4.7 %weight.1 = f32[32,128]{1,0:T(8,128)} custom-call(s32[3,128]{1,0:T(4,128)} %pad_add_fusion.meta, bf16[2,256,256]{2,1,0:T(8,128)(2,1)} %copy-done.1, bf16[2,256,256]{2,1,0:T(8,128)(2,1)} %copy-done.4, bf16[2,256,256]{2,1,0:T(8,128)(2,1)} %copy-done.5, bf16[2,256,256]{2,1,0:T(8,128)(2,1)} %copy-done.6), custom_call_target="tpu_custom_call" | custom-call | tf_op jit(solution)/shard_map/weight/pallas_call | solution.py:462
  139.5 0.7 broadcast_add_fusion
  140.2 0.7 copy-done.8
  140.9 0.0 copy-done.11
  141.0 0.6 add_subtract_fusion
  (33 shorter events, 0.2 us)
Async XLA Ops:
  2.2 33.1 %all-to-all-start = ((bf16[16,64,128]{2,1,0:T(8,128)(2,1)}), bf16[16,64,128]{2,1,0:T(8,128)(2,1)S(1)}, u32[]{:S(2)}, u32[]{:S(2)}) async-start(bf16[16,64,128]{2,1,0:T(8,128)(2,1)} %broadcast_in_dim.59), calls=%async_computation | async-start | bytes 524288 | tf_op jit(solution)/shard_map/all_to_all | solution.py:414
  17.4 0.7 copy-start.17
  18.1 0.7 copy-start.16
  35.3 0.7 copy-start.3
  58.0 5.0 %copy-start.7 = (f32[1,2,256,256]{3,2,1,0:T(8,128)S(1)}, f32[1,2,256,256]{3,2,1,0:T(8,128)}, u32[]{:S(2)}) copy-start(f32[1,2,256,256]{3,2,1,0:T(8,128)} %param.19) | copy-start | bytes 1572868
  58.0 24.5 %all-to-all-start.2 = ((bf16[4,2,256,128]{3,2,1,0:T(8,128)(2,1)}), bf16[4,2,256,128]{3,2,1,0:T(8,128)(2,1)S(1)}, u32[]{:S(2)}, u32[]{:S(2)}) async-start(bf16[4,2,256,128]{3,2,1,0:T(8,128)(2,1)} %broadcast_in_dim.60), calls=%async_computation.2 | async-start | bytes 1048576 | tf_op jit(solution)/shard_map/all_to_all | solution.py:437
  63.0 19.4 %copy-start.1 = (bf16[2,256,256]{2,1,0:T(8,128)(2,1)}, bf16[2,256,256]{2,1,0:T(8,128)(2,1)S(1)}, u32[]{:S(2)}) copy-start(bf16[2,256,256]{2,1,0:T(8,128)(2,1)S(1)} %convert_bitcast_fusion.probe0) | copy-start | bytes 786436
  63.0 16.5 %collective-permute-start = (bf16[2,256,256]{2,1,0:T(8,128)(2,1)S(1)}, bf16[2,256,256]{2,1,0:T(8,128)(2,1)S(1)}, u32[]{:S(2)}, u32[]{:S(2)}) collective-permute-start(bf16[2,256,256]{2,1,0:T(8,128)(2,1)S(1)} %convert_bitcast_fusion.probe0), channel_id=1, source_target_pairs={{0,1},{1,2},{2,3},{3,0},{4,5},{5,6},{6,7},{7,4},{8,9},{9,10},{10,1... | collective-permute-start | bytes 786440 | tf_op jit(solution)/shard_map/ppermute | solution.py:417
  66.4 13.2 %collective-permute-start.1 = (bf16[2,256,256]{2,1,0:T(8,128)(2,1)S(1)}, bf16[2,256,256]{2,1,0:T(8,128)(2,1)S(1)}, u32[]{:S(2)}, u32[]{:S(2)}) collective-permute-start(bf16[2,256,256]{2,1,0:T(8,128)(2,1)S(1)} %convert_bitcast_fusion.probe0), channel_id=1, source_target_pairs={{0,2},{1,3},{2,0},{3,1},{4,6},{5,7},{6,4},{7,5},{8,10},{9,11},{10,... | collective-permute-start | bytes 786440 | tf_op jit(solution)/shard_map/ppermute | solution.py:417
  69.0 13.5 %collective-permute-start.2 = (bf16[2,256,256]{2,1,0:T(8,128)(2,1)S(1)}, bf16[2,256,256]{2,1,0:T(8,128)(2,1)S(1)}, u32[]{:S(2)}, u32[]{:S(2)}) collective-permute-start(bf16[2,256,256]{2,1,0:T(8,128)(2,1)S(1)} %convert_bitcast_fusion.probe0), channel_id=1, source_target_pairs={{0,3},{1,0},{2,1},{3,2},{4,7},{5,4},{6,5},{7,6},{8,11},{9,8},{10,9... | collective-permute-start | bytes 786440 | tf_op jit(solution)/shard_map/ppermute | solution.py:417
  79.6 2.9 %copy-start.4 = (bf16[2,256,256]{2,1,0:T(8,128)(2,1)}, bf16[2,256,256]{2,1,0:T(8,128)(2,1)S(1)}, u32[]{:S(2)}) copy-start(bf16[2,256,256]{2,1,0:T(8,128)(2,1)S(1)} %collective-permute-done.probe1) | copy-start | bytes 786436
  79.6 2.9 %copy-start.5 = (bf16[2,256,256]{2,1,0:T(8,128)(2,1)}, bf16[2,256,256]{2,1,0:T(8,128)(2,1)S(1)}, u32[]{:S(2)}) copy-start(bf16[2,256,256]{2,1,0:T(8,128)(2,1)S(1)} %collective-permute-done.1.probe2) | copy-start | bytes 786436
  82.4 0.7 copy-start.6
  83.1 0.8 copy-start.2
  90.3 15.2 %all-to-all-start.3 = ((bf16[8,5,64,128]{3,2,1,0:T(8,128)(2,1)}), bf16[8,5,64,128]{3,2,1,0:T(8,128)(2,1)S(1)}, u32[]{:S(2)}, u32[]{:S(2)}) async-start(bf16[8,5,64,128]{3,2,1,0:T(8,128)(2,1)} %get-tuple-element.6), calls=%async_computation.3 | async-start | bytes 1310720 | tf_op jit(solution)/shard_map/all_to_all | solution.py:452
  93.9 5.6 %copy-start.13 = (bf16[9,36,4,1]{1,0,3,2:T(8,128)(2,1)S(1)}, bf16[9,36,4,1]{1,0,3,2:T(8,128)(2,1)}, u32[]{:S(2)}) copy-start(bf16[9,36,4,1]{1,0,3,2:T(8,128)(2,1)} %constant.46) | copy-start | bytes 7780
  93.9 5.6 %copy-start.14 = (bf16[9,2,48]{2,1,0:T(2,128)(2,1)S(1)}, bf16[9,2,48]{2,1,0:T(2,128)(2,1)}, u32[]{:S(2)}) copy-start(bf16[9,2,48]{2,1,0:T(2,128)(2,1)} %param.29) | copy-start | bytes 5188
  93.9 20.9 %collective-permute-start.3 = (bf16[2,6,128]{2,1,0:T(8,128)(2,1)S(1)}, bf16[2,6,128]{2,1,0:T(8,128)(2,1)S(1)}, u32[]{:S(2)}, u32[]{:S(2)}) collective-permute-start(bf16[2,6,128]{2,1,0:T(8,128)(2,1)S(1)} %get-tuple-element.16), channel_id=1, source_target_pairs={{0,4},{4,8},{8,12},{12,16},{16,20},{20,24},{24,28},{28,32},{32,36}... | collective-permute-start | bytes 9224 | tf_op jit(solution)/shard_map/ppermute | solution.py:29
  96.3 3.4 %copy-start.12 = (bf16[9,2,4,72]{3,0,1,2:T(8,128)(2,1)S(1)}, bf16[9,2,4,72]{3,0,1,2:T(8,128)(2,1)}, u32[]{:S(2)}) copy-start(bf16[9,2,4,72]{3,0,1,2:T(8,128)(2,1)} %constant.44) | copy-start | bytes 31108
  96.3 18.4 %collective-permute-start.4 = (bf16[2,6,128]{2,1,0:T(8,128)(2,1)S(1)}, bf16[2,6,128]{2,1,0:T(8,128)(2,1)S(1)}, u32[]{:S(2)}, u32[]{:S(2)}) collective-permute-start(bf16[2,6,128]{2,1,0:T(8,128)(2,1)S(1)} %get-tuple-element.17), channel_id=1, source_target_pairs={{4,0},{8,4},{12,8},{16,12},{20,16},{24,20},{28,24},{32,28},{36,32}... | collective-permute-start | bytes 9224 | tf_op jit(solution)/shard_map/ppermute | solution.py:29
  99.5 0.7 copy-start.15
  105.5 0.8 copy-start
  108.5 31.7 %all-to-all-start.4 = ((bf16[16,64,128]{2,1,0:T(8,128)(2,1)}), bf16[16,64,128]{2,1,0:T(8,128)(2,1)S(1)}, u32[]{:S(2)}, u32[]{:S(2)}) async-start(bf16[16,64,128]{2,1,0:T(8,128)(2,1)} %gather.1), calls=%async_computation.4 | async-start | bytes 524288 | tf_op jit(solution)/shard_map/all_to_all | solution.py:461
  114.9 12.5 %collective-permute-start.5 = (bf16[2,44,6]{2,1,0:T(8,128)(2,1)S(1)}, bf16[2,44,6]{2,1,0:T(8,128)(2,1)S(1)}, u32[]{:S(2)}, u32[]{:S(2)}) collective-permute-start(bf16[2,44,6]{2,1,0:T(8,128)(2,1)S(1)} %get-tuple-element.14), channel_id=1, source_target_pairs={{0,1},{1,2},{2,3},{4,5},{5,6},{6,7},{8,9},{9,10},{10,11},{12,13},{... | collective-permute-start | bytes 3176 | tf_op jit(solution)/shard_map/ppermute | solution.py:29
  117.4 4.3 %copy-start.9 = (bf16[9,48,48]{2,1,0:T(8,128)(2,1)S(1)}, bf16[9,48,48]{2,1,0:T(8,128)(2,1)}, u32[]{:S(2)}) copy-start(bf16[9,48,48]{2,1,0:T(8,128)(2,1)} %param.27) | copy-start | bytes 124420
  117.4 10.0 %collective-permute-start.6 = (bf16[2,44,6]{2,1,0:T(8,128)(2,1)S(1)}, bf16[2,44,6]{2,1,0:T(8,128)(2,1)S(1)}, u32[]{:S(2)}, u32[]{:S(2)}) collective-permute-start(bf16[2,44,6]{2,1,0:T(8,128)(2,1)S(1)} %get-tuple-element.15), channel_id=1, source_target_pairs={{1,0},{2,1},{3,2},{5,4},{6,5},{7,6},{9,8},{10,9},{11,10},{13,12},{... | collective-permute-start | bytes 3176 | tf_op jit(solution)/shard_map/ppermute | solution.py:29
  121.8 0.8 copy-start.10
  123.3 0.7 copy-start.18
  124.7 0.7 copy-start.19
  126.0 0.7 copy-start.20
  140.2 0.8 copy-start.8
  140.2 0.8 copy-start.11

commit v3 on v2

--- a/solution.py
+++ b/solution.py
@@ -44,6 +44,10 @@
     return pl.BlockSpec(memory_space=pltpu.VMEM)
 
 
+def near_core(*arrays):
+    return [pltpu.with_memory_space_constraint(a, pltpu.VMEM) for a in arrays]
+
+
 def smem_spec():
     return pl.BlockSpec(memory_space=pltpu.SMEM)
 
@@ -54,6 +58,12 @@
 
 def first_strip(s0, core):
     return s0 + ((s0 + core) & 1)
+
+
+def spread_kernel(obj, out):
+    rows = jnp.concatenate([obj[0], obj[1]], axis=0).astype(bf16)
+    for slot in range(NZ):
+        out[slot] = rows
 
 
 def pack_kernel(meta, near, out):
@@ -79,7 +89,9 @@
         tall[1, pl.ds(i * ROWS, ROWS)] = block[ROWS:]
     offset = row - s0 * ROWS
     for plane in range(2):
-        out[plane] = tall[plane, pl.ds(offset, PATCH)].astype(bf16)
+        rows = tall[plane, pl.ds(offset, PATCH)].astype(bf16)
+        for peer in range(NM):
+            out[peer, plane] = rows
 
 
 def dot(a, b):
@@ -248,12 +260,10 @@
     b_out,
     ext,
     first_w,
-    first_b,
     down_w,
-    down_b,
     mid_w,
-    mid_b,
     last_w,
+    biases,
     out,
     halves,
     planes,
@@ -305,16 +315,16 @@
         found = masks(start)
         value = dot(first_w[...], taps1[:, span])
         for n in range(4):
-            part = value[n * chans : (n + 1) * chans] + first_b[...]
+            part = value[n * chans : (n + 1) * chans] + biases[:, 0:1]
             maps[pl.ds(n * chans, chans), span] = (jnp.maximum(part, 0.0) * found[n]).astype(bf16)
-        value = dot(down_w[...], maps[:, span]) + down_b[...]
+        value = dot(down_w[...], maps[:, span]) + biases[:, 1:2]
         coarse[:, span] = (jnp.maximum(value, 0.0) * found[0]).astype(bf16).astype(f32)
     for s, (dy, dx) in enumerate(SHIFTS):
         taps2[pl.ds(s * chans, chans)] = moved(coarse[...], dy, dx).astype(bf16)
     for start in range(0, FLAT, CHUNK):
         span = pl.ds(start, CHUNK)
         found = masks(start)
-        value = dot(mid_w[...], taps2[:, span]) + mid_b[...]
+        value = dot(mid_w[...], taps2[:, span]) + biases[:, 2:3]
         third = jnp.maximum(value, 0.0).astype(bf16).astype(f32)
         for n in range(4):
             rows = pl.ds(n * chans, chans)
@@ -352,7 +362,7 @@
     return pl.pallas_call(
         denoise_kernel,
         out_shape=jax.ShapeDtypeStruct((2, ROWS, COLS), f32),
-        in_specs=[smem_spec(), smem_spec()] + [vmem_spec()] * 8,
+        in_specs=[smem_spec(), smem_spec()] + [vmem_spec()] * 6,
         out_specs=vmem_spec(),
         scratch_shapes=[
             pltpu.VMEM((2, 2 * (ROWS + 2 * HALO), 128), f32),
@@ -374,12 +384,10 @@
         b_out,
         extended,
         first_w,
-        b_in.reshape(chans, 1),
         down_w,
-        b_down.reshape(chans, 1),
         mid_w,
-        b_mid.reshape(chans, 1),
         last_w,
+        jnp.stack([b_in, b_down, b_mid], axis=1),
     )
 
 
@@ -410,8 +418,14 @@
     place = jnp.where(lanes == 0, x, jnp.where(lanes == 1, z, jnp.where(lanes == 2, core, mode)))
     meta = jnp.concatenate([by_owner, place[None]], axis=0).astype(jnp.int32)
 
-    low = obj_x.astype(bf16).reshape(1, 2 * ROWS, COLS)
-    near = lax.all_to_all(jnp.broadcast_to(low, (NZ, 2 * ROWS, COLS)), "z", 0, 0, tiled=True)
+    spread = pl.pallas_call(
+        spread_kernel,
+        out_shape=jax.ShapeDtypeStruct((NZ, 2 * ROWS, COLS), bf16),
+        in_specs=[vmem_spec()],
+        out_specs=vmem_spec(),
+        name="spread",
+    )(obj_x)
+    near = lax.all_to_all(spread, "z", 0, 0, tiled=True)
     probe0 = probes[0].astype(bf16)
     others = [
         lax.ppermute(probe0, "mode", [(i, (i + k) % NM) for i in range(NM)])
@@ -424,17 +438,17 @@
         in_specs=[smem_spec(), vmem_spec()],
         out_specs=vmem_spec(),
         name="pack",
-    )(meta, near)
+    )(meta, *near_core(near))
     got = lax.all_to_all(packed, ("x", "core"), 0, 0, tiled=True)
     window = pl.pallas_call(
         window_kernel,
-        out_shape=jax.ShapeDtypeStruct((2, PATCH, COLS), bf16),
+        out_shape=jax.ShapeDtypeStruct((NM, 2, PATCH, COLS), bf16),
         in_specs=[smem_spec(), vmem_spec()],
         out_specs=vmem_spec(),
         scratch_shapes=[pltpu.VMEM((2, STRIPS * ROWS, COLS), f32)],
         name="window",
-    )(meta, got)
-    wins = lax.all_to_all(jnp.broadcast_to(window, (NM, *window.shape)), "mode", 0, 0, tiled=True)
+    )(meta, *near_core(got))
+    wins = lax.all_to_all(window, "mode", 0, 0, tiled=True)
     updates, misfit = pl.pallas_call(
         wave_kernel,
         out_shape=(
@@ -448,7 +462,7 @@
             pltpu.VMEM((2, STRIPS * ROWS, COLS), f32),
         ],
         name="wave",
-    )(meta, wins, *all_probes, intensity, dft_table())
+    )(meta, *near_core(wins, *all_probes), intensity, dft_table())
     back = lax.all_to_all(updates, ("x", "core"), 0, 0, tiled=True)
     partial = pl.pallas_call(
         gather_kernel,
@@ -457,7 +471,7 @@
         out_specs=vmem_spec(),
         scratch_shapes=[pltpu.VMEM((NZ, 2 * ROWS, COLS), f32)],
         name="gather",
-    )(meta, back)
+    )(meta, *near_core(back))
     pieces = lax.all_to_all(partial, "z", 0, 0, tiled=True)
     denom = pl.pallas_call(
         weight_kernel,
@@ -466,7 +480,7 @@
         out_specs=vmem_spec(),
         scratch_shapes=[pltpu.VMEM((PATCH // COLS + 2, PATCH + 2 * ROWS, COLS), f32)],
         name="weight",
-    )(meta, *all_probes)
+    )(meta, *near_core(*all_probes))
     base = obj_x + dual_u
     center = denoise(base, meta, w_in, b_in, w_down, b_down, w_mid, b_mid, w_out, b_out)
     aux_next = base - center

time: 143 us -> 133 us (0.930)
  local copies, waits for them, and re-layouts: 14.6 us -> 6.5 us
    unnamed x42 -> x30, local copies, waits for them, and re-layouts: 7.6 us -> 3.4 us
    broadcast_in_dim x2 -> x0, local copies, waits for them, and re-layouts: 2.5 us -> none  [the longest x1 1.75 us: per_device(): jnp.broadcast_to(window, (NM, *window.shape))]
    reshape x3 -> x0, local copies, waits for them, and re-layouts: 2.07 us -> none  [the longest x1 0.7 us: denoise(): b_in.reshape(chans, 1)]
    pallas_call x1 -> x2, Pallas kernels: 1.83 us -> 3.1 us  [the longest x1 1.61 us: per_device(): pl.pallas_call(window_kernel, out_shape=jax.ShapeDtypeStruct((NM, 2, PATC...]
  transfers between devices with their start and end apart: 11 -> 11, of which waited for: 4 -> 4; matrix products, arithmetic and copies ran while one was open for 5% -> 5% of each run, Pallas kernels for 10% -> 8%
where the time goes in v3:
time: 133 us; the launch traced here: 132 us
  starting transfers between devices  51.9 us (39%)
  waiting for transfers between devices  29.3 us (22%)
  Pallas kernels  23.5 us (18%)
  blocking collectives  16.1 us (12%)
  local copies, waits for them, and re-layouts  6.5 us (5%)
  other arithmetic  2.89 us (2%)
    all_to_all x1, blocking collectives, per_device(): got = lax.all_to_all(packed, ('x', 'core'), 0, 0, tiled=True)  16.1 us
    all_to_all x1, waiting for transfers between devices, per_device(): near = lax.all_to_all(spread, 'z', 0, 0, tiled=True)  15.9 us
    all_to_all x1, starting transfers between devices, per_device(): near = lax.all_to_all(spread, 'z', 0, 0, tiled=True)  15.2 us
    ppermute x4, starting transfers between devices, shifted(): return lax.ppermute(value, axes, pairs)  11.4 us
    ppermute x3, starting transfers between devices, per_device(): lax.ppermute(probe0, 'mode', [(i, (i + k) % NM) for i in range(NM)])  10.4 us
    ppermute x3, waiting for transfers between devices, per_device(): lax.ppermute(probe0, 'mode', [(i, (i + k) % NM) for i in range(NM)])  8.92 us
    pallas_call x1, Pallas kernels, denoise(): pl.pallas_call(denoise_kernel, out_shape=jax.ShapeDtypeStruct((2, ROWS, C...  6.64 us
    all_to_all x1, starting transfers between devices, per_device(): pieces = lax.all_to_all(partial, 'z', 0, 0, tiled=True)  6.25 us
  transfers between devices with their start and end apart: 11, of which 4 were waited for; matrix products, arithmetic and copies ran while one was open for 5% of the time, Pallas kernels for 8%

profile of v3, /device:TPU:40, one launch (start us, length us, event | category | flops | bytes accessed | tf_op | source)
XLA Modules:
  0.0 132.0 jit_solution(18118703848919391054)
XLA Ops:
  0.6 1.5 %spread.1 = bf16[16,64,128]{2,1,0:T(8,128)(2,1)} custom-call(f32[2,32,128]{2,1,0:T(8,128)} %obj.1), custom_call_target="tpu_custom_call" | custom-call | tf_op jit(solution)/shard_map/spread/pallas_call | solution.py:421
  2.1 15.2 %all-to-all-start = ((bf16[16,64,128]{2,1,0:T(8,128)(2,1)}), bf16[16,64,128]{2,1,0:T(8,128)(2,1)S(1)}, u32[]{:S(2)}, u32[]{:S(2)}) async-start(bf16[16,64,128]{2,1,0:T(8,128)(2,1)} %spread.1), calls=%async_computation | async-start | bytes 524288 | tf_op jit(solution)/shard_map/all_to_all | solution.py:428
  17.3 0.6 copy-done.11
  18.0 0.7 copy-done.10
  18.7 0.1 select_reduce_fusion
  18.8 0.6 pad_add_fusion.meta
  19.4 15.9 %all-to-all-done.near = bf16[16,64,128]{2,1,0:T(8,128)(2,1)S(1)} async-done(((bf16[16,64,128]{2,1,0:T(8,128)(2,1)}), bf16[16,64,128]{2,1,0:T(8,128)(2,1)S(1)}, u32[]{:S(2)}, u32[]{:S(2)}) %all-to-all-start) | async-done | bytes 262176 | tf_op jit(solution)/shard_map/all_to_all | solution.py:428
  35.2 1.9 %pack.1 = bf16[8,5,64,128]{3,2,1,0:T(8,128)(2,1)} custom-call(s32[3,128]{1,0:T(4,128)} %pad_add_fusion.meta, bf16[16,64,128]{2,1,0:T(8,128)(2,1)S(1)} %all-to-all-done.near), custom_call_target="tpu_custom_call" | custom-call | tf_op jit(solution)/shard_map/pack/pallas_call | solution.py:435
  37.1 16.1 %all_to_all.25.got = bf16[8,5,64,128]{3,2,1,0:T(8,128)(2,1)S(1)} all-to-all(bf16[8,5,64,128]{3,2,1,0:T(8,128)(2,1)} %pack.1), channel_id=1, replica_groups=mesh['x'=4,'z'=16,'core'=2,'mode'=4] {'x','core'}, dimensions={0} | all-to-all | bytes 1310720 | tf_op jit(solution)/shard_map/all_to_all | solution.py:442
  53.2 1.6 %window.1 = bf16[4,2,256,128]{3,2,1,0:T(8,128)(2,1)} custom-call(s32[3,128]{1,0:T(4,128)} %pad_add_fusion.meta, bf16[8,5,64,128]{3,2,1,0:T(8,128)(2,1)S(1)} %all_to_all.25.got), custom_call_target="tpu_custom_call" | custom-call | tf_op jit(solution)/shard_map/window/pallas_call | solution.py:443
  54.8 5.0 %all-to-all-start.2 = ((bf16[4,2,256,128]{3,2,1,0:T(8,128)(2,1)}), bf16[4,2,256,128]{3,2,1,0:T(8,128)(2,1)S(1)}, u32[]{:S(2)}, u32[]{:S(2)}) async-start(bf16[4,2,256,128]{3,2,1,0:T(8,128)(2,1)} %window.1), calls=%async_computation.2 | async-start | bytes 1048576 | tf_op jit(solution)/shard_map/all_to_all | solution.py:451
  59.8 0.0 copy-done
  59.9 3.4 %collective-permute-start = (bf16[2,256,256]{2,1,0:T(8,128)(2,1)S(1)}, bf16[2,256,256]{2,1,0:T(8,128)(2,1)S(1)}, u32[]{:S(2)}, u32[]{:S(2)}) collective-permute-start(bf16[2,256,256]{2,1,0:T(8,128)(2,1)S(1)} %convert_bitcast_fusion.probe0), channel_id=1, source_target_pairs={{0,1},{1,2},{2,3},{3,0},{4,5},{5,6},{6,7},{7,4},{8,9},{9,10},{10,1... | collective-permute-start | bytes 786440 | tf_op jit(solution)/shard_map/ppermute | solution.py:431
  63.2 2.5 %collective-permute-start.1 = (bf16[2,256,256]{2,1,0:T(8,128)(2,1)S(1)}, bf16[2,256,256]{2,1,0:T(8,128)(2,1)S(1)}, u32[]{:S(2)}, u32[]{:S(2)}) collective-permute-start(bf16[2,256,256]{2,1,0:T(8,128)(2,1)S(1)} %convert_bitcast_fusion.probe0), channel_id=1, source_target_pairs={{0,2},{1,3},{2,0},{3,1},{4,6},{5,7},{6,4},{7,5},{8,10},{9,11},{10,... | collective-permute-start | bytes 786440 | tf_op jit(solution)/shard_map/ppermute | solution.py:431
  65.8 4.5 %collective-permute-start.2 = (bf16[2,256,256]{2,1,0:T(8,128)(2,1)S(1)}, bf16[2,256,256]{2,1,0:T(8,128)(2,1)S(1)}, u32[]{:S(2)}, u32[]{:S(2)}) collective-permute-start(bf16[2,256,256]{2,1,0:T(8,128)(2,1)S(1)} %convert_bitcast_fusion.probe0), channel_id=1, source_target_pairs={{0,3},{1,0},{2,1},{3,2},{4,7},{5,4},{6,5},{7,6},{8,11},{9,8},{10,9... | collective-permute-start | bytes 786440 | tf_op jit(solution)/shard_map/ppermute | solution.py:431
  70.3 0.0 copy-done.1
  70.3 0.0 copy-done.2
  70.4 6.0 %collective-permute-done.probe1 = bf16[2,256,256]{2,1,0:T(8,128)(2,1)S(1)} collective-permute-done((bf16[2,256,256]{2,1,0:T(8,128)(2,1)S(1)}, bf16[2,256,256]{2,1,0:T(8,128)(2,1)S(1)}, u32[]{:S(2)}, u32[]{:S(2)}) %collective-permute-start) | collective-permute-done | bytes 262176 | tf_op jit(solution)/shard_map/ppermute | solution.py:431
  76.4 0.0 collective-permute-done.1.probe2
  76.4 2.9 %collective-permute-done.2.probe3 = bf16[2,256,256]{2,1,0:T(8,128)(2,1)S(1)} collective-permute-done((bf16[2,256,256]{2,1,0:T(8,128)(2,1)S(1)}, bf16[2,256,256]{2,1,0:T(8,128)(2,1)S(1)}, u32[]{:S(2)}, u32[]{:S(2)}) %collective-permute-start.2) | collective-permute-done | bytes 262176 | tf_op jit(solution)/shard_map/ppermute | solution.py:431
  79.3 0.0 all-to-all-done.2.wins
  79.3 5.9 %wave.1 = (bf16[8,5,64,128]{3,2,1,0:T(8,128)(2,1)}, f32[1,1]{1,0:T(1,128)}) custom-call(s32[3,128]{1,0:T(4,128)} %pad_add_fusion.meta, bf16[4,2,256,128]{3,2,1,0:T(8,128)(2,1)S(1)} %all-to-all-done.2.wins, bf16[2,256,256]{2,1,0:T(8,128)(2,1)S(1)} %convert_bitcast_fusion.probe0, bf16[2,256,256]{2,1,0:T(8,128)(2,1)S(1)} %collective-permute-done.probe1, ...), custom_call_target="tpu_custom_call" | custom-call | tf_op jit(solution)/shard_map/wave/pallas_call | solution.py:452
  85.2 3.5 %all-to-all-start.3 = ((bf16[8,5,64,128]{3,2,1,0:T(8,128)(2,1)}), bf16[8,5,64,128]{3,2,1,0:T(8,128)(2,1)S(1)}, u32[]{:S(2)}, u32[]{:S(2)}) async-start(bf16[8,5,64,128]{3,2,1,0:T(8,128)(2,1)} %get-tuple-element.6), calls=%async_computation.3 | async-start | bytes 1310720 | tf_op jit(solution)/shard_map/all_to_all | solution.py:466
  88.7 0.0 copy-start.7
  88.7 0.0 copy-start.8
  88.8 2.4 %collective-permute-start.3 = (bf16[2,6,128]{2,1,0:T(8,128)(2,1)S(1)}, bf16[2,6,128]{2,1,0:T(8,128)(2,1)S(1)}, u32[]{:S(2)}, u32[]{:S(2)}) collective-permute-start(bf16[2,6,128]{2,1,0:T(8,128)(2,1)S(1)} %get-tuple-element.15), channel_id=1, source_target_pairs={{0,4},{4,8},{8,12},{12,16},{16,20},{20,24},{24,28},{28,32},{32,36}... | collective-permute-start | bytes 9224 | tf_op jit(solution)/shard_map/ppermute | solution.py:29
  91.2 0.0 copy-start.6
  91.2 3.1 %collective-permute-start.4 = (bf16[2,6,128]{2,1,0:T(8,128)(2,1)S(1)}, bf16[2,6,128]{2,1,0:T(8,128)(2,1)S(1)}, u32[]{:S(2)}, u32[]{:S(2)}) collective-permute-start(bf16[2,6,128]{2,1,0:T(8,128)(2,1)S(1)} %get-tuple-element.16), channel_id=1, source_target_pairs={{4,0},{8,4},{12,8},{16,12},{20,16},{24,20},{28,24},{32,28},{36,32}... | collective-permute-start | bytes 9224 | tf_op jit(solution)/shard_map/ppermute | solution.py:29
  94.4 0.0 copy-start.9
  94.4 0.2 convolution_bitcast_fusion
  94.6 0.5 copy-done.9
  95.1 0.8 fusion.1
  95.9 0.0 collective-permute-done.3
  95.9 0.0 collective-permute-done.4
  95.9 4.5 %all-to-all-done.3.got = bf16[8,5,64,128]{3,2,1,0:T(8,128)(2,1)S(1)} async-done(((bf16[8,5,64,128]{3,2,1,0:T(8,128)(2,1)}), bf16[8,5,64,128]{3,2,1,0:T(8,128)(2,1)S(1)}, u32[]{:S(2)}, u32[]{:S(2)}) %all-to-all-start.3) | async-done | bytes 655392 | tf_op jit(solution)/shard_map/all_to_all | solution.py:466
  100.4 1.8 %gather.1 = bf16[16,64,128]{2,1,0:T(8,128)(2,1)} custom-call(s32[3,128]{1,0:T(4,128)} %pad_add_fusion.meta, bf16[8,5,64,128]{3,2,1,0:T(8,128)(2,1)S(1)} %all-to-all-done.3.got), custom_call_target="tpu_custom_call" | custom-call | tf_op jit(solution)/shard_map/gather/pallas_call | solution.py:467
  102.1 6.2 %all-to-all-start.4 = ((bf16[16,64,128]{2,1,0:T(8,128)(2,1)}), bf16[16,64,128]{2,1,0:T(8,128)(2,1)S(1)}, u32[]{:S(2)}, u32[]{:S(2)}) async-start(bf16[16,64,128]{2,1,0:T(8,128)(2,1)} %gather.1), calls=%async_computation.4 | async-start | bytes 524288 | tf_op jit(solution)/shard_map/all_to_all | solution.py:475
  108.4 0.1 fusion.6
  108.5 2.5 %collective-permute-start.5 = (bf16[2,44,6]{2,1,0:T(8,128)(2,1)S(1)}, bf16[2,44,6]{2,1,0:T(8,128)(2,1)S(1)}, u32[]{:S(2)}, u32[]{:S(2)}) collective-permute-start(bf16[2,44,6]{2,1,0:T(8,128)(2,1)S(1)} %get-tuple-element.13), channel_id=1, source_target_pairs={{0,1},{1,2},{2,3},{4,5},{5,6},{6,7},{8,9},{9,10},{10,11},{12,13},{... | collective-permute-start | bytes 3176 | tf_op jit(solution)/shard_map/ppermute | solution.py:29
  110.9 3.4 %collective-permute-start.6 = (bf16[2,44,6]{2,1,0:T(8,128)(2,1)S(1)}, bf16[2,44,6]{2,1,0:T(8,128)(2,1)S(1)}, u32[]{:S(2)}, u32[]{:S(2)}) collective-permute-start(bf16[2,44,6]{2,1,0:T(8,128)(2,1)S(1)} %get-tuple-element.14), channel_id=1, source_target_pairs={{1,0},{2,1},{3,2},{5,4},{6,5},{7,6},{9,8},{10,9},{11,10},{13,12},{... | collective-permute-start | bytes 3176 | tf_op jit(solution)/shard_map/ppermute | solution.py:29
  114.3 0.0 copy-start.12
  114.3 0.0 copy-start.13
  114.3 0.0 copy-start.14
  114.3 0.6 copy-done.12
  115.0 0.0 copy-done.13
  115.0 0.0 copy-done.14
  115.0 0.0 copy-start.3
  115.1 0.7 reshape.82.last_w
  115.8 0.1 copy-done.3
  115.9 0.1 copy.47
  116.0 0.0 copy-start.4
  116.0 0.7 copy.50.mid_w
  116.8 0.1 copy-done.4
  116.9 0.7 reshape.80.down_w
  117.6 0.7 copy.51.biases
  118.3 0.0 collective-permute-done.5
  118.3 0.0 collective-permute-done.6
  118.3 0.7 pad_maximum_fusion.ext
  119.0 6.6 %denoise.1 = f32[2,32,128]{2,1,0:T(8,128)} custom-call(s32[3,128]{1,0:T(4,128)} %pad_add_fusion.meta, f32[2]{0:T(128)} %b_out.1, bf16[2,44,140]{2,1,0:T(8,128)(2,1)} %pad_maximum_fusion.ext, bf16[192,72]{1,0:T(8,128)(2,1)} %bitcast.33, bf16[48,192]{1,0:T(8,128)(2,1)} %reshape.80.down_w, bf16[48,432]{1,0:T(8,128)(2,1)} %copy.50.mid_w, ...), custom_call_target="tpu_custom_call" | custom-call | flops 4000000000 | bytes 20000000 | tf_op jit(solution)/shard_map/denoise/pallas_call | solution.py:362
  125.6 4.2 %weight.1 = f32[32,128]{1,0:T(8,128)} custom-call(s32[3,128]{1,0:T(4,128)} %pad_add_fusion.meta, bf16[2,256,256]{2,1,0:T(8,128)(2,1)S(1)} %convert_bitcast_fusion.probe0, bf16[2,256,256]{2,1,0:T(8,128)(2,1)S(1)} %collective-permute-done.probe1, bf16[2,256,256]{2,1,0:T(8,128)(2,1)S(1)} %collective-permute-done.1.probe2, ...), custom_call_target="tpu_custom_call" | custom-call | tf_op jit(solution)/shard_map/weight/pallas_call | solution.py:476
  129.9 0.7 broadcast_add_fusion
  130.6 0.0 all-to-all-done.4
  130.6 0.7 copy-done.5
  131.3 0.6 add_subtract_fusion
  (19 shorter events, 0.2 us)
Async XLA Ops:
  2.1 33.1 %all-to-all-start = ((bf16[16,64,128]{2,1,0:T(8,128)(2,1)}), bf16[16,64,128]{2,1,0:T(8,128)(2,1)S(1)}, u32[]{:S(2)}, u32[]{:S(2)}) async-start(bf16[16,64,128]{2,1,0:T(8,128)(2,1)} %spread.1), calls=%async_computation | async-start | bytes 524288 | tf_op jit(solution)/shard_map/all_to_all | solution.py:428
  17.3 0.7 copy-start.11
  18.0 0.7 copy-start.10
  54.8 5.0 %copy-start = (f32[1,2,256,256]{3,2,1,0:T(8,128)S(1)}, f32[1,2,256,256]{3,2,1,0:T(8,128)}, u32[]{:S(2)}) copy-start(f32[1,2,256,256]{3,2,1,0:T(8,128)} %param.19) | copy-start | bytes 1572868
  54.8 24.5 %all-to-all-start.2 = ((bf16[4,2,256,128]{3,2,1,0:T(8,128)(2,1)}), bf16[4,2,256,128]{3,2,1,0:T(8,128)(2,1)S(1)}, u32[]{:S(2)}, u32[]{:S(2)}) async-start(bf16[4,2,256,128]{3,2,1,0:T(8,128)(2,1)} %window.1), calls=%async_computation.2 | async-start | bytes 1048576 | tf_op jit(solution)/shard_map/all_to_all | solution.py:451
  59.8 10.5 %copy-start.1 = (f32[2,32,128]{2,1,0:T(8,128)S(1)}, f32[2,32,128]{2,1,0:T(8,128)}, u32[]{:S(2)}) copy-start(f32[2,32,128]{2,1,0:T(8,128)} %obj.1) | copy-start | bytes 98308
  59.8 10.5 %copy-start.2 = (f32[2,32,128]{2,1,0:T(8,128)S(1)}, f32[2,32,128]{2,1,0:T(8,128)}, u32[]{:S(2)}) copy-start(f32[2,32,128]{2,1,0:T(8,128)} %param.18) | copy-start | bytes 98308
  59.9 16.5 %collective-permute-start = (bf16[2,256,256]{2,1,0:T(8,128)(2,1)S(1)}, bf16[2,256,256]{2,1,0:T(8,128)(2,1)S(1)}, u32[]{:S(2)}, u32[]{:S(2)}) collective-permute-start(bf16[2,256,256]{2,1,0:T(8,128)(2,1)S(1)} %convert_bitcast_fusion.probe0), channel_id=1, source_target_pairs={{0,1},{1,2},{2,3},{3,0},{4,5},{5,6},{6,7},{7,4},{8,9},{9,10},{10,1... | collective-permute-start | bytes 786440 | tf_op jit(solution)/shard_map/ppermute | solution.py:431
  63.2 13.2 %collective-permute-start.1 = (bf16[2,256,256]{2,1,0:T(8,128)(2,1)S(1)}, bf16[2,256,256]{2,1,0:T(8,128)(2,1)S(1)}, u32[]{:S(2)}, u32[]{:S(2)}) collective-permute-start(bf16[2,256,256]{2,1,0:T(8,128)(2,1)S(1)} %convert_bitcast_fusion.probe0), channel_id=1, source_target_pairs={{0,2},{1,3},{2,0},{3,1},{4,6},{5,7},{6,4},{7,5},{8,10},{9,11},{10,... | collective-permute-start | bytes 786440 | tf_op jit(solution)/shard_map/ppermute | solution.py:431
  65.8 13.5 %collective-permute-start.2 = (bf16[2,256,256]{2,1,0:T(8,128)(2,1)S(1)}, bf16[2,256,256]{2,1,0:T(8,128)(2,1)S(1)}, u32[]{:S(2)}, u32[]{:S(2)}) collective-permute-start(bf16[2,256,256]{2,1,0:T(8,128)(2,1)S(1)} %convert_bitcast_fusion.probe0), channel_id=1, source_target_pairs={{0,3},{1,0},{2,1},{3,2},{4,7},{5,4},{6,5},{7,6},{8,11},{9,8},{10,9... | collective-permute-start | bytes 786440 | tf_op jit(solution)/shard_map/ppermute | solution.py:431
  85.2 15.2 %all-to-all-start.3 = ((bf16[8,5,64,128]{3,2,1,0:T(8,128)(2,1)}), bf16[8,5,64,128]{3,2,1,0:T(8,128)(2,1)S(1)}, u32[]{:S(2)}, u32[]{:S(2)}) async-start(bf16[8,5,64,128]{3,2,1,0:T(8,128)(2,1)} %get-tuple-element.6), calls=%async_computation.3 | async-start | bytes 1310720 | tf_op jit(solution)/shard_map/all_to_all | solution.py:466
  88.7 5.6 %copy-start.7 = (bf16[9,36,4,1]{1,0,3,2:T(8,128)(2,1)S(1)}, bf16[9,36,4,1]{1,0,3,2:T(8,128)(2,1)}, u32[]{:S(2)}) copy-start(bf16[9,36,4,1]{1,0,3,2:T(8,128)(2,1)} %constant.46) | copy-start | bytes 7780
  88.7 5.6 %copy-start.8 = (bf16[9,2,48]{2,1,0:T(2,128)(2,1)S(1)}, bf16[9,2,48]{2,1,0:T(2,128)(2,1)}, u32[]{:S(2)}) copy-start(bf16[9,2,48]{2,1,0:T(2,128)(2,1)} %param.29) | copy-start | bytes 5188
  88.8 7.1 %collective-permute-start.3 = (bf16[2,6,128]{2,1,0:T(8,128)(2,1)S(1)}, bf16[2,6,128]{2,1,0:T(8,128)(2,1)S(1)}, u32[]{:S(2)}, u32[]{:S(2)}) collective-permute-start(bf16[2,6,128]{2,1,0:T(8,128)(2,1)S(1)} %get-tuple-element.15), channel_id=1, source_target_pairs={{0,4},{4,8},{8,12},{12,16},{16,20},{20,24},{24,28},{28,32},{32,36}... | collective-permute-start | bytes 9224 | tf_op jit(solution)/shard_map/ppermute | solution.py:29
  91.2 3.4 %copy-start.6 = (bf16[9,2,4,72]{3,0,1,2:T(8,128)(2,1)S(1)}, bf16[9,2,4,72]{3,0,1,2:T(8,128)(2,1)}, u32[]{:S(2)}) copy-start(bf16[9,2,4,72]{3,0,1,2:T(8,128)(2,1)} %constant.44) | copy-start | bytes 31108
  91.2 4.7 %collective-permute-start.4 = (bf16[2,6,128]{2,1,0:T(8,128)(2,1)S(1)}, bf16[2,6,128]{2,1,0:T(8,128)(2,1)S(1)}, u32[]{:S(2)}, u32[]{:S(2)}) collective-permute-start(bf16[2,6,128]{2,1,0:T(8,128)(2,1)S(1)} %get-tuple-element.16), channel_id=1, source_target_pairs={{4,0},{8,4},{12,8},{16,12},{20,16},{24,20},{28,24},{32,28},{36,32}... | collective-permute-start | bytes 9224 | tf_op jit(solution)/shard_map/ppermute | solution.py:29
  94.4 0.7 copy-start.9
  102.1 28.4 %all-to-all-start.4 = ((bf16[16,64,128]{2,1,0:T(8,128)(2,1)}), bf16[16,64,128]{2,1,0:T(8,128)(2,1)S(1)}, u32[]{:S(2)}, u32[]{:S(2)}) async-start(bf16[16,64,128]{2,1,0:T(8,128)(2,1)} %gather.1), calls=%async_computation.4 | async-start | bytes 524288 | tf_op jit(solution)/shard_map/all_to_all | solution.py:475
  108.5 9.8 %collective-permute-start.5 = (bf16[2,44,6]{2,1,0:T(8,128)(2,1)S(1)}, bf16[2,44,6]{2,1,0:T(8,128)(2,1)S(1)}, u32[]{:S(2)}, u32[]{:S(2)}) collective-permute-start(bf16[2,44,6]{2,1,0:T(8,128)(2,1)S(1)} %get-tuple-element.13), channel_id=1, source_target_pairs={{0,1},{1,2},{2,3},{4,5},{5,6},{6,7},{8,9},{9,10},{10,11},{12,13},{... | collective-permute-start | bytes 3176 | tf_op jit(solution)/shard_map/ppermute | solution.py:29
  110.9 7.3 %collective-permute-start.6 = (bf16[2,44,6]{2,1,0:T(8,128)(2,1)S(1)}, bf16[2,44,6]{2,1,0:T(8,128)(2,1)S(1)}, u32[]{:S(2)}, u32[]{:S(2)}) collective-permute-start(bf16[2,44,6]{2,1,0:T(8,128)(2,1)S(1)} %get-tuple-element.14), channel_id=1, source_target_pairs={{1,0},{2,1},{3,2},{5,4},{6,5},{7,6},{9,8},{10,9},{11,10},{13,12},{... | collective-permute-start | bytes 3176 | tf_op jit(solution)/shard_map/ppermute | solution.py:29
  114.3 0.7 copy-start.12
  114.3 0.7 copy-start.13
  114.3 0.7 copy-start.14
  115.0 0.9 copy-start.3
  116.0 0.8 copy-start.4
  130.6 0.8 copy-start.5

commit v4 on v3

--- a/solution.py
+++ b/solution.py
@@ -14,7 +14,7 @@
 ROWS = 32
 COLS = 128
 STRIPS = PATCH // ROWS + 1
-HALF = (STRIPS + 1) // 2
+HALF = PATCH // ROWS // 2
 
 rho_weight = 2.0
 floor_level = 0.25
@@ -48,6 +48,10 @@
     return [pltpu.with_memory_space_constraint(a, pltpu.VMEM) for a in arrays]
 
 
+def any_spec():
+    return pl.BlockSpec(memory_space=pl.ANY)
+
+
 def smem_spec():
     return pl.BlockSpec(memory_space=pltpu.SMEM)
 
@@ -60,38 +64,70 @@
     return s0 + ((s0 + core) & 1)
 
 
-def spread_kernel(obj, out):
-    rows = jnp.concatenate([obj[0], obj[1]], axis=0).astype(bf16)
-    for slot in range(NZ):
-        out[slot] = rows
-
-
-def pack_kernel(meta, near, out):
+def copy_out(held, out, sems, count, same):
+    copies = [
+        pltpu.make_async_copy(held if same else held.at[n], out.at[n], sems.at[n])
+        for n in range(count)
+    ]
+    for copy in copies:
+        copy.start()
+    return copies
+
+
+def spread_kernel(obj, out, held, sems):
+    held[...] = jnp.concatenate([obj[0], obj[1]], axis=0).astype(bf16)
+    for copy in copy_out(held, out, sems, NZ, True):
+        copy.wait()
+
+
+def row_in_strip():
+    return lax.broadcasted_iota(jnp.int32, (2 * ROWS, COLS), 0) & (ROWS - 1)
+
+
+def z_slot(strip):
+    return (strip % (NZ * NC)) // NC
+
+
+def strips_of(row, core):
+    s0 = row // ROWS
+    begin = first_strip(s0, core)
+    return begin, jnp.where(begin == s0, row - s0 * ROWS, 0)
+
+
+def pack_kernel(meta, near, out, held, sems):
     _, z, core, _ = ids(meta)
+    rows = row_in_strip()
+    copies = []
     for target in range(NX * NC):
         tx, tc = target // NC, target % NC
-        tile = tx * (NZ * NC) + z * NC + tc
-        begin = first_strip(meta[0, tile] // ROWS, core)
-        for j in range(HALF):
-            slot = ((begin + 2 * j) % (NZ * NC)) // NC
-            out[target, j] = near[slot]
-
-
-def window_kernel(meta, got, out, tall):
+        begin, cut = strips_of(meta[0, tx * (NZ * NC) + z * NC + tc], core)
+        late = near[z_slot(begin + 2 * HALF)].astype(f32)
+        early = near[z_slot(begin)].astype(f32)
+        held[target, 0] = jnp.where(rows < cut, late, early).astype(bf16)
+        for j in range(1, HALF):
+            held[target, j] = near[z_slot(begin + 2 * j)]
+        copy = pltpu.make_async_copy(held.at[target], out.at[target], sems.at[target])
+        copy.start()
+        copies.append(copy)
+    for copy in copies:
+        copy.wait()
+
+
+def window_kernel(meta, got, out, tall, held, sems):
     x, z, core, _ = ids(meta)
     row = meta[0, x * (NZ * NC) + z * NC + core]
     s0 = row // ROWS
     for i in range(STRIPS):
         strip = s0 + i
         source = jnp.minimum(strip // (NZ * NC), NX - 1) * NC + (strip & 1)
-        block = got[source, i // 2].astype(f32)
+        block = got[source, (i // 2) % HALF].astype(f32)
         tall[0, pl.ds(i * ROWS, ROWS)] = block[:ROWS]
         tall[1, pl.ds(i * ROWS, ROWS)] = block[ROWS:]
     offset = row - s0 * ROWS
     for plane in range(2):
-        rows = tall[plane, pl.ds(offset, PATCH)].astype(bf16)
-        for peer in range(NM):
-            out[peer, plane] = rows
+        held[plane] = tall[plane, pl.ds(offset, PATCH)].astype(bf16)
+    for copy in copy_out(held, out, sems, NM, True):
+        copy.wait()
 
 
 def dot(a, b):
@@ -170,18 +206,26 @@
     for i in range(STRIPS):
         strip = s0 + i
         target = jnp.minimum(strip // (NZ * NC), NX - 1) * NC + (strip & 1)
-        piece = [tall[p, pl.ds(i * ROWS, ROWS)] for p in range(2)]
-        out[target, i // 2] = jnp.concatenate(piece, axis=0).astype(bf16)
+        piece = jnp.concatenate([tall[p, pl.ds(i * ROWS, ROWS)] for p in range(2)], axis=0)
+        if i < 2 * HALF:
+            out[target, i // 2] = piece.astype(bf16)
+        else:
+            out[target, 0] = (out[target, 0].astype(f32) + piece).astype(bf16)
 
 
 def gather_kernel(meta, got, out, acc):
     _, z, core, _ = ids(meta)
+    rows = row_in_strip()
     acc[...] = jnp.zeros(acc.shape, f32)
     for source in range(NX * NC):
         sx, sc = source // NC, source % NC
-        begin = first_strip(meta[0, sx * (NZ * NC) + z * NC + sc] // ROWS, core)
-        for j in range(HALF):
-            slot = ((begin + 2 * j) % (NZ * NC)) // NC
+        begin, cut = strips_of(meta[0, sx * (NZ * NC) + z * NC + sc], core)
+        both = got[source, 0].astype(f32)
+        late, early = z_slot(begin + 2 * HALF), z_slot(begin)
+        acc[late] = acc[late] + jnp.where(rows < cut, both, 0.0)
+        acc[early] = acc[early] + jnp.where(rows < cut, 0.0, both)
+        for j in range(1, HALF):
+            slot = z_slot(begin + 2 * j)
             acc[slot] = acc[slot] + got[source, j].astype(f32)
     out[...] = acc[...].astype(bf16)
 
@@ -422,7 +466,8 @@
         spread_kernel,
         out_shape=jax.ShapeDtypeStruct((NZ, 2 * ROWS, COLS), bf16),
         in_specs=[vmem_spec()],
-        out_specs=vmem_spec(),
+        out_specs=any_spec(),
+        scratch_shapes=[pltpu.VMEM((2 * ROWS, COLS), bf16), pltpu.SemaphoreType.DMA((NZ,))],
         name="spread",
     )(obj_x)
     near = lax.all_to_all(spread, "z", 0, 0, tiled=True)
@@ -436,7 +481,11 @@
         pack_kernel,
         out_shape=jax.ShapeDtypeStruct((NX * NC, HALF, 2 * ROWS, COLS), bf16),
         in_specs=[smem_spec(), vmem_spec()],
-        out_specs=vmem_spec(),
+        out_specs=any_spec(),
+        scratch_shapes=[
+            pltpu.VMEM((NX * NC, HALF, 2 * ROWS, COLS), bf16),
+            pltpu.SemaphoreType.DMA((NX * NC,)),
+        ],
         name="pack",
     )(meta, *near_core(near))
     got = lax.all_to_all(packed, ("x", "core"), 0, 0, tiled=True)
@@ -444,8 +493,12 @@
         window_kernel,
         out_shape=jax.ShapeDtypeStruct((NM, 2, PATCH, COLS), bf16),
         in_specs=[smem_spec(), vmem_spec()],
-        out_specs=vmem_spec(),
-        scratch_shapes=[pltpu.VMEM((2, STRIPS * ROWS, COLS), f32)],
+        out_specs=any_spec(),
+        scratch_shapes=[
+            pltpu.VMEM((2, STRIPS * ROWS, COLS), f32),
+            pltpu.VMEM((2, PATCH, COLS), bf16),
+            pltpu.SemaphoreType.DMA((NM,)),
+        ],
         name="window",
     )(meta, *near_core(got))
     wins = lax.all_to_all(window, "mode", 0, 0, tiled=True)

time: 133 us -> 122 us (0.917)
  blocking collectives: 16.1 us -> 0 us
  starting transfers between devices: 51.9 us -> 57.3 us
    all_to_all x1 -> x0, blocking collectives: 16.1 us -> none  [per_device(): got = lax.all_to_all(packed, ('x', 'core'), 0, 0, tiled=True)]
    ppermute x3, waiting for transfers between devices: 8.92 us -> 0.01 us  [per_device(): lax.ppermute(probe0, 'mode', [(i, (i + k) % NM) for i in range(NM)])]
    all_to_all x0 -> x1, starting transfers between devices: none -> 4.44 us  [per_device(): got = lax.all_to_all(packed, ('x', 'core'), 0, 0, tiled=True)]
    all_to_all x1, waiting for transfers between devices: 4.47 us -> 8.7 us  [per_device(): back = lax.all_to_all(updates, ('x', 'core'), 0, 0, tiled=True)]
    all_to_all x1, waiting for transfers between devices: 0.01 us -> 3.82 us  [per_device(): wins = lax.all_to_all(window, 'mode', 0, 0, tiled=True)]
  transfers between devices with their start and end apart: 11 -> 12, of which waited for: 4 -> 3; matrix products, arithmetic and copies ran while one was open for 5% -> 5% of each run, Pallas kernels for 8% -> 15%
where the time goes in v4:
time: 122 us; the launch traced here: 121 us
  starting transfers between devices  57.3 us (47%)
  waiting for transfers between devices  28.4 us (23%)
  Pallas kernels  23.5 us (19%)
  local copies, waits for them, and re-layouts  6.57 us (5%)
  other arithmetic  2.9 us (2%)
    all_to_all x1, waiting for transfers between devices, per_device(): near = lax.all_to_all(spread, 'z', 0, 0, tiled=True)  15.9 us
    all_to_all x1, starting transfers between devices, per_device(): near = lax.all_to_all(spread, 'z', 0, 0, tiled=True)  15.2 us
    ppermute x4, starting transfers between devices, shifted(): return lax.ppermute(value, axes, pairs)  11.4 us
    ppermute x3, starting transfers between devices, per_device(): lax.ppermute(probe0, 'mode', [(i, (i + k) % NM) for i in range(NM)])  10.7 us
    all_to_all x1, waiting for transfers between devices, per_device(): back = lax.all_to_all(updates, ('x', 'core'), 0, 0, tiled=True)  8.7 us
    pallas_call x1, Pallas kernels, denoise(): pl.pallas_call(denoise_kernel, out_shape=jax.ShapeDtypeStruct((2, ROWS, C...  6.64 us
    all_to_all x1, starting transfers between devices, per_device(): pieces = lax.all_to_all(partial, 'z', 0, 0, tiled=True)  6.24 us
    pallas_call x1, Pallas kernels, per_device(): pl.pallas_call(wave_kernel, out_shape=(jax.ShapeDtypeStruct((NX * NC, HAL...  5.85 us
  transfers between devices with their start and end apart: 12, of which 3 were waited for; matrix products, arithmetic and copies ran while one was open for 5% of the time, Pallas kernels for 15%

profile of v4, /device:TPU:40, one launch (start us, length us, event | category | flops | bytes accessed | tf_op | source)
XLA Modules:
  0.0 120.6 jit_solution(6827551912932674727)
XLA Ops:
  0.6 1.6 %spread.1 = bf16[16,64,128]{2,1,0:T(8,128)(2,1)} custom-call(f32[2,32,128]{2,1,0:T(8,128)} %obj.1), custom_call_target="tpu_custom_call" | custom-call | tf_op jit(solution)/shard_map/spread/pallas_call | solution.py:465
  2.2 15.2 %all-to-all-start = ((bf16[16,64,128]{2,1,0:T(8,128)(2,1)}), bf16[16,64,128]{2,1,0:T(8,128)(2,1)S(1)}, u32[]{:S(2)}, u32[]{:S(2)}) async-start(bf16[16,64,128]{2,1,0:T(8,128)(2,1)} %spread.1), calls=%async_computation | async-start | bytes 524288 | tf_op jit(solution)/shard_map/all_to_all | solution.py:473
  17.5 0.6 copy-done.11
  18.1 0.7 copy-done.10
  18.8 0.1 select_reduce_fusion
  18.9 0.6 pad_add_fusion.meta
  19.5 15.9 %all-to-all-done.near = bf16[16,64,128]{2,1,0:T(8,128)(2,1)S(1)} async-done(((bf16[16,64,128]{2,1,0:T(8,128)(2,1)}), bf16[16,64,128]{2,1,0:T(8,128)(2,1)S(1)}, u32[]{:S(2)}, u32[]{:S(2)}) %all-to-all-start) | async-done | bytes 262176 | tf_op jit(solution)/shard_map/all_to_all | solution.py:473
  35.4 1.8 %pack.1 = bf16[8,4,64,128]{3,2,1,0:T(8,128)(2,1)} custom-call(s32[3,128]{1,0:T(4,128)} %pad_add_fusion.meta, bf16[16,64,128]{2,1,0:T(8,128)(2,1)S(1)} %all-to-all-done.near), custom_call_target="tpu_custom_call" | custom-call | tf_op jit(solution)/shard_map/pack/pallas_call | solution.py:480
  37.2 0.0 copy-start
  37.2 4.4 %all-to-all-start.1 = ((bf16[8,4,64,128]{3,2,1,0:T(8,128)(2,1)}), bf16[8,4,64,128]{3,2,1,0:T(8,128)(2,1)S(1)}, u32[]{:S(2)}, u32[]{:S(2)}) async-start(bf16[8,4,64,128]{3,2,1,0:T(8,128)(2,1)} %pack.1), calls=%async_computation.1 | async-start | bytes 1048576 | tf_op jit(solution)/shard_map/all_to_all | solution.py:491
  41.6 3.5 %collective-permute-start = (bf16[2,256,256]{2,1,0:T(8,128)(2,1)S(1)}, bf16[2,256,256]{2,1,0:T(8,128)(2,1)S(1)}, u32[]{:S(2)}, u32[]{:S(2)}) collective-permute-start(bf16[2,256,256]{2,1,0:T(8,128)(2,1)S(1)} %convert_bitcast_fusion.probe0), channel_id=1, source_target_pairs={{0,1},{1,2},{2,3},{3,0},{4,5},{5,6},{6,7},{7,4},{8,9},{9,10},{10,1... | collective-permute-start | bytes 786440 | tf_op jit(solution)/shard_map/ppermute | solution.py:476
  45.1 2.8 %collective-permute-start.1 = (bf16[2,256,256]{2,1,0:T(8,128)(2,1)S(1)}, bf16[2,256,256]{2,1,0:T(8,128)(2,1)S(1)}, u32[]{:S(2)}, u32[]{:S(2)}) collective-permute-start(bf16[2,256,256]{2,1,0:T(8,128)(2,1)S(1)} %convert_bitcast_fusion.probe0), channel_id=1, source_target_pairs={{0,2},{1,3},{2,0},{3,1},{4,6},{5,7},{6,4},{7,5},{8,10},{9,11},{10,... | collective-permute-start | bytes 786440 | tf_op jit(solution)/shard_map/ppermute | solution.py:476
  48.0 4.3 %collective-permute-start.2 = (bf16[2,256,256]{2,1,0:T(8,128)(2,1)S(1)}, bf16[2,256,256]{2,1,0:T(8,128)(2,1)S(1)}, u32[]{:S(2)}, u32[]{:S(2)}) collective-permute-start(bf16[2,256,256]{2,1,0:T(8,128)(2,1)S(1)} %convert_bitcast_fusion.probe0), channel_id=1, source_target_pairs={{0,3},{1,0},{2,1},{3,2},{4,7},{5,4},{6,5},{7,6},{8,11},{9,8},{10,9... | collective-permute-start | bytes 786440 | tf_op jit(solution)/shard_map/ppermute | solution.py:476
  52.3 0.0 all-to-all-done.1.got
  52.3 1.6 %window.1 = bf16[4,2,256,128]{3,2,1,0:T(8,128)(2,1)} custom-call(s32[3,128]{1,0:T(4,128)} %pad_add_fusion.meta, bf16[8,4,64,128]{3,2,1,0:T(8,128)(2,1)S(1)} %all-to-all-done.1.got), custom_call_target="tpu_custom_call" | custom-call | tf_op jit(solution)/shard_map/window/pallas_call | solution.py:492
  54.0 0.0 copy-start.1
  54.0 0.0 copy-start.2
  54.0 4.8 %all-to-all-start.2 = ((bf16[4,2,256,128]{3,2,1,0:T(8,128)(2,1)}), bf16[4,2,256,128]{3,2,1,0:T(8,128)(2,1)S(1)}, u32[]{:S(2)}, u32[]{:S(2)}) async-start(bf16[4,2,256,128]{3,2,1,0:T(8,128)(2,1)} %window.1), calls=%async_computation.2 | async-start | bytes 1048576 | tf_op jit(solution)/shard_map/all_to_all | solution.py:504
  58.8 0.0 copy-done.1
  58.8 1.9 %collective-permute-start.3 = (bf16[2,6,128]{2,1,0:T(8,128)(2,1)S(1)}, bf16[2,6,128]{2,1,0:T(8,128)(2,1)S(1)}, u32[]{:S(2)}, u32[]{:S(2)}) collective-permute-start(bf16[2,6,128]{2,1,0:T(8,128)(2,1)S(1)} %get-tuple-element.15), channel_id=1, source_target_pairs={{0,4},{4,8},{8,12},{12,16},{16,20},{20,24},{24,28},{28,32},{32,36}... | collective-permute-start | bytes 9224 | tf_op jit(solution)/shard_map/ppermute | solution.py:29
  60.7 3.6 %collective-permute-start.4 = (bf16[2,6,128]{2,1,0:T(8,128)(2,1)S(1)}, bf16[2,6,128]{2,1,0:T(8,128)(2,1)S(1)}, u32[]{:S(2)}, u32[]{:S(2)}) collective-permute-start(bf16[2,6,128]{2,1,0:T(8,128)(2,1)S(1)} %get-tuple-element.16), channel_id=1, source_target_pairs={{4,0},{8,4},{12,8},{16,12},{20,16},{24,20},{28,24},{32,28},{36,32}... | collective-permute-start | bytes 9224 | tf_op jit(solution)/shard_map/ppermute | solution.py:29
  64.4 0.0 collective-permute-done.probe1
  64.4 0.0 collective-permute-done.1.probe2
  64.4 0.0 collective-permute-done.2.probe3
  64.4 3.8 %all-to-all-done.2.wins = bf16[4,2,256,128]{3,2,1,0:T(8,128)(2,1)S(1)} async-done(((bf16[4,2,256,128]{3,2,1,0:T(8,128)(2,1)}), bf16[4,2,256,128]{3,2,1,0:T(8,128)(2,1)S(1)}, u32[]{:S(2)}, u32[]{:S(2)}) %all-to-all-start.2) | async-done | bytes 524320 | tf_op jit(solution)/shard_map/all_to_all | solution.py:504
  68.2 5.8 %wave.1 = (bf16[8,4,64,128]{3,2,1,0:T(8,128)(2,1)}, f32[1,1]{1,0:T(1,128)}) custom-call(s32[3,128]{1,0:T(4,128)} %pad_add_fusion.meta, bf16[4,2,256,128]{3,2,1,0:T(8,128)(2,1)S(1)} %all-to-all-done.2.wins, bf16[2,256,256]{2,1,0:T(8,128)(2,1)S(1)} %convert_bitcast_fusion.probe0, bf16[2,256,256]{2,1,0:T(8,128)(2,1)S(1)} %collective-permute-done.probe1, ...), custom_call_target="tpu_custom_call" | custom-call | tf_op jit(solution)/shard_map/wave/pallas_call | solution.py:505
  74.1 4.5 %all-to-all-start.3 = ((bf16[8,4,64,128]{3,2,1,0:T(8,128)(2,1)}), bf16[8,4,64,128]{3,2,1,0:T(8,128)(2,1)S(1)}, u32[]{:S(2)}, u32[]{:S(2)}) async-start(bf16[8,4,64,128]{3,2,1,0:T(8,128)(2,1)} %get-tuple-element.6), calls=%async_computation.3 | async-start | bytes 1048576 | tf_op jit(solution)/shard_map/all_to_all | solution.py:519
  78.7 0.0 copy-start.6
  78.7 0.0 copy-start.9
  78.7 0.2 convolution_bitcast_fusion
  78.9 0.5 copy-done.6
  79.4 0.8 fusion.1
  80.2 0.0 collective-permute-done.3
  80.2 0.0 collective-permute-done.4
  80.3 8.7 %all-to-all-done.3.got = bf16[8,4,64,128]{3,2,1,0:T(8,128)(2,1)S(1)} async-done(((bf16[8,4,64,128]{3,2,1,0:T(8,128)(2,1)}), bf16[8,4,64,128]{3,2,1,0:T(8,128)(2,1)S(1)}, u32[]{:S(2)}, u32[]{:S(2)}) %all-to-all-start.3) | async-done | bytes 524320 | tf_op jit(solution)/shard_map/all_to_all | solution.py:519
  89.0 1.8 %gather.1 = bf16[16,64,128]{2,1,0:T(8,128)(2,1)} custom-call(s32[3,128]{1,0:T(4,128)} %pad_add_fusion.meta, bf16[8,4,64,128]{3,2,1,0:T(8,128)(2,1)S(1)} %all-to-all-done.3.got), custom_call_target="tpu_custom_call" | custom-call | tf_op jit(solution)/shard_map/gather/pallas_call | solution.py:520
  90.7 6.2 %all-to-all-start.4 = ((bf16[16,64,128]{2,1,0:T(8,128)(2,1)}), bf16[16,64,128]{2,1,0:T(8,128)(2,1)S(1)}, u32[]{:S(2)}, u32[]{:S(2)}) async-start(bf16[16,64,128]{2,1,0:T(8,128)(2,1)} %gather.1), calls=%async_computation.4 | async-start | bytes 524288 | tf_op jit(solution)/shard_map/all_to_all | solution.py:528
  97.0 0.1 fusion.6
  97.1 1.9 %collective-permute-start.5 = (bf16[2,44,6]{2,1,0:T(8,128)(2,1)S(1)}, bf16[2,44,6]{2,1,0:T(8,128)(2,1)S(1)}, u32[]{:S(2)}, u32[]{:S(2)}) collective-permute-start(bf16[2,44,6]{2,1,0:T(8,128)(2,1)S(1)} %get-tuple-element.13), channel_id=1, source_target_pairs={{0,1},{1,2},{2,3},{4,5},{5,6},{6,7},{8,9},{9,10},{10,11},{12,13},{... | collective-permute-start | bytes 3176 | tf_op jit(solution)/shard_map/ppermute | solution.py:29
  99.0 3.9 %collective-permute-start.6 = (bf16[2,44,6]{2,1,0:T(8,128)(2,1)S(1)}, bf16[2,44,6]{2,1,0:T(8,128)(2,1)S(1)}, u32[]{:S(2)}, u32[]{:S(2)}) collective-permute-start(bf16[2,44,6]{2,1,0:T(8,128)(2,1)S(1)} %get-tuple-element.14), channel_id=1, source_target_pairs={{1,0},{2,1},{3,2},{5,4},{6,5},{7,6},{9,8},{10,9},{11,10},{13,12},{... | collective-permute-start | bytes 3176 | tf_op jit(solution)/shard_map/ppermute | solution.py:29
  102.9 0.0 copy-start.12
  102.9 0.0 copy-start.13
  102.9 0.0 copy-start.14
  102.9 0.6 copy-done.12
  103.6 0.0 copy-done.13
  103.6 0.0 copy-done.14
  103.6 0.0 copy-start.3
  103.7 0.7 reshape.82.last_w
  104.4 0.1 copy-done.3
  104.5 0.1 copy.47
  104.6 0.0 copy-start.4
  104.7 0.7 copy.50.mid_w
  105.4 0.1 copy-done.4
  105.5 0.7 reshape.80.down_w
  106.2 0.7 copy.51.biases
  106.9 0.0 collective-permute-done.5
  106.9 0.0 collective-permute-done.6
  106.9 0.7 pad_maximum_fusion.ext
  107.6 6.6 %denoise.1 = f32[2,32,128]{2,1,0:T(8,128)} custom-call(s32[3,128]{1,0:T(4,128)} %pad_add_fusion.meta, f32[2]{0:T(128)} %b_out.1, bf16[2,44,140]{2,1,0:T(8,128)(2,1)} %pad_maximum_fusion.ext, bf16[192,72]{1,0:T(8,128)(2,1)} %bitcast.33, bf16[48,192]{1,0:T(8,128)(2,1)} %reshape.80.down_w, bf16[48,432]{1,0:T(8,128)(2,1)} %copy.50.mid_w, ...), custom_call_target="tpu_custom_call" | custom-call | flops 4000000000 | bytes 20000000 | tf_op jit(solution)/shard_map/denoise/pallas_call | solution.py:406
  114.2 4.2 %weight.1 = f32[32,128]{1,0:T(8,128)} custom-call(s32[3,128]{1,0:T(4,128)} %pad_add_fusion.meta, bf16[2,256,256]{2,1,0:T(8,128)(2,1)S(1)} %convert_bitcast_fusion.probe0, bf16[2,256,256]{2,1,0:T(8,128)(2,1)S(1)} %collective-permute-done.probe1, bf16[2,256,256]{2,1,0:T(8,128)(2,1)S(1)} %collective-permute-done.1.probe2, ...), custom_call_target="tpu_custom_call" | custom-call | tf_op jit(solution)/shard_map/weight/pallas_call | solution.py:529
  118.5 0.7 broadcast_add_fusion
  119.2 0.0 all-to-all-done.4
  119.2 0.7 copy-done.5
  119.9 0.6 add_subtract_fusion
  (20 shorter events, 0.2 us)
Async XLA Ops:
  2.2 33.1 %all-to-all-start = ((bf16[16,64,128]{2,1,0:T(8,128)(2,1)}), bf16[16,64,128]{2,1,0:T(8,128)(2,1)S(1)}, u32[]{:S(2)}, u32[]{:S(2)}) async-start(bf16[16,64,128]{2,1,0:T(8,128)(2,1)} %spread.1), calls=%async_computation | async-start | bytes 524288 | tf_op jit(solution)/shard_map/all_to_all | solution.py:473
  17.5 0.7 copy-start.11
  18.1 0.7 copy-start.10
  37.2 4.5 %copy-start = (f32[1,2,256,256]{3,2,1,0:T(8,128)S(1)}, f32[1,2,256,256]{3,2,1,0:T(8,128)}, u32[]{:S(2)}) copy-start(f32[1,2,256,256]{3,2,1,0:T(8,128)} %param.19) | copy-start | bytes 1572868
  37.2 15.2 %all-to-all-start.1 = ((bf16[8,4,64,128]{3,2,1,0:T(8,128)(2,1)}), bf16[8,4,64,128]{3,2,1,0:T(8,128)(2,1)S(1)}, u32[]{:S(2)}, u32[]{:S(2)}) async-start(bf16[8,4,64,128]{3,2,1,0:T(8,128)(2,1)} %pack.1), calls=%async_computation.1 | async-start | bytes 1048576 | tf_op jit(solution)/shard_map/all_to_all | solution.py:491
  41.6 22.8 %collective-permute-start = (bf16[2,256,256]{2,1,0:T(8,128)(2,1)S(1)}, bf16[2,256,256]{2,1,0:T(8,128)(2,1)S(1)}, u32[]{:S(2)}, u32[]{:S(2)}) collective-permute-start(bf16[2,256,256]{2,1,0:T(8,128)(2,1)S(1)} %convert_bitcast_fusion.probe0), channel_id=1, source_target_pairs={{0,1},{1,2},{2,3},{3,0},{4,5},{5,6},{6,7},{7,4},{8,9},{9,10},{10,1... | collective-permute-start | bytes 786440 | tf_op jit(solution)/shard_map/ppermute | solution.py:476
  45.1 19.3 %collective-permute-start.1 = (bf16[2,256,256]{2,1,0:T(8,128)(2,1)S(1)}, bf16[2,256,256]{2,1,0:T(8,128)(2,1)S(1)}, u32[]{:S(2)}, u32[]{:S(2)}) collective-permute-start(bf16[2,256,256]{2,1,0:T(8,128)(2,1)S(1)} %convert_bitcast_fusion.probe0), channel_id=1, source_target_pairs={{0,2},{1,3},{2,0},{3,1},{4,6},{5,7},{6,4},{7,5},{8,10},{9,11},{10,... | collective-permute-start | bytes 786440 | tf_op jit(solution)/shard_map/ppermute | solution.py:476
  48.0 16.4 %collective-permute-start.2 = (bf16[2,256,256]{2,1,0:T(8,128)(2,1)S(1)}, bf16[2,256,256]{2,1,0:T(8,128)(2,1)S(1)}, u32[]{:S(2)}, u32[]{:S(2)}) collective-permute-start(bf16[2,256,256]{2,1,0:T(8,128)(2,1)S(1)} %convert_bitcast_fusion.probe0), channel_id=1, source_target_pairs={{0,3},{1,0},{2,1},{3,2},{4,7},{5,4},{6,5},{7,6},{8,11},{9,8},{10,9... | collective-permute-start | bytes 786440 | tf_op jit(solution)/shard_map/ppermute | solution.py:476
  54.0 4.8 %copy-start.1 = (f32[2,32,128]{2,1,0:T(8,128)S(1)}, f32[2,32,128]{2,1,0:T(8,128)}, u32[]{:S(2)}) copy-start(f32[2,32,128]{2,1,0:T(8,128)} %obj.1) | copy-start | bytes 98308
  54.0 4.8 %copy-start.2 = (f32[2,32,128]{2,1,0:T(8,128)S(1)}, f32[2,32,128]{2,1,0:T(8,128)}, u32[]{:S(2)}) copy-start(f32[2,32,128]{2,1,0:T(8,128)} %param.18) | copy-start | bytes 98308
  54.0 14.3 %all-to-all-start.2 = ((bf16[4,2,256,128]{3,2,1,0:T(8,128)(2,1)}), bf16[4,2,256,128]{3,2,1,0:T(8,128)(2,1)S(1)}, u32[]{:S(2)}, u32[]{:S(2)}) async-start(bf16[4,2,256,128]{3,2,1,0:T(8,128)(2,1)} %window.1), calls=%async_computation.2 | async-start | bytes 1048576 | tf_op jit(solution)/shard_map/all_to_all | solution.py:504
  58.8 21.4 %collective-permute-start.3 = (bf16[2,6,128]{2,1,0:T(8,128)(2,1)S(1)}, bf16[2,6,128]{2,1,0:T(8,128)(2,1)S(1)}, u32[]{:S(2)}, u32[]{:S(2)}) collective-permute-start(bf16[2,6,128]{2,1,0:T(8,128)(2,1)S(1)} %get-tuple-element.15), channel_id=1, source_target_pairs={{0,4},{4,8},{8,12},{12,16},{16,20},{20,24},{24,28},{28,32},{32,36}... | collective-permute-start | bytes 9224 | tf_op jit(solution)/shard_map/ppermute | solution.py:29
  60.7 19.5 %collective-permute-start.4 = (bf16[2,6,128]{2,1,0:T(8,128)(2,1)S(1)}, bf16[2,6,128]{2,1,0:T(8,128)(2,1)S(1)}, u32[]{:S(2)}, u32[]{:S(2)}) collective-permute-start(bf16[2,6,128]{2,1,0:T(8,128)(2,1)S(1)} %get-tuple-element.16), channel_id=1, source_target_pairs={{4,0},{8,4},{12,8},{16,12},{20,16},{24,20},{28,24},{32,28},{36,32}... | collective-permute-start | bytes 9224 | tf_op jit(solution)/shard_map/ppermute | solution.py:29
  74.1 4.6 %copy-start.7 = (bf16[9,36,4,1]{1,0,3,2:T(8,128)(2,1)S(1)}, bf16[9,36,4,1]{1,0,3,2:T(8,128)(2,1)}, u32[]{:S(2)}) copy-start(bf16[9,36,4,1]{1,0,3,2:T(8,128)(2,1)} %constant.46) | copy-start | bytes 7780
  74.1 4.6 %copy-start.8 = (bf16[9,2,48]{2,1,0:T(2,128)(2,1)S(1)}, bf16[9,2,48]{2,1,0:T(2,128)(2,1)}, u32[]{:S(2)}) copy-start(bf16[9,2,48]{2,1,0:T(2,128)(2,1)} %param.29) | copy-start | bytes 5188
  74.1 14.9 %all-to-all-start.3 = ((bf16[8,4,64,128]{3,2,1,0:T(8,128)(2,1)}), bf16[8,4,64,128]{3,2,1,0:T(8,128)(2,1)S(1)}, u32[]{:S(2)}, u32[]{:S(2)}) async-start(bf16[8,4,64,128]{3,2,1,0:T(8,128)(2,1)} %get-tuple-element.6), calls=%async_computation.3 | async-start | bytes 1048576 | tf_op jit(solution)/shard_map/all_to_all | solution.py:519
  78.7 0.8 copy-start.6
  78.7 0.8 copy-start.9
  90.7 28.4 %all-to-all-start.4 = ((bf16[16,64,128]{2,1,0:T(8,128)(2,1)}), bf16[16,64,128]{2,1,0:T(8,128)(2,1)S(1)}, u32[]{:S(2)}, u32[]{:S(2)}) async-start(bf16[16,64,128]{2,1,0:T(8,128)(2,1)} %gather.1), calls=%async_computation.4 | async-start | bytes 524288 | tf_op jit(solution)/shard_map/all_to_all | solution.py:528
  97.1 9.8 %collective-permute-start.5 = (bf16[2,44,6]{2,1,0:T(8,128)(2,1)S(1)}, bf16[2,44,6]{2,1,0:T(8,128)(2,1)S(1)}, u32[]{:S(2)}, u32[]{:S(2)}) collective-permute-start(bf16[2,44,6]{2,1,0:T(8,128)(2,1)S(1)} %get-tuple-element.13), channel_id=1, source_target_pairs={{0,1},{1,2},{2,3},{4,5},{5,6},{6,7},{8,9},{9,10},{10,11},{12,13},{... | collective-permute-start | bytes 3176 | tf_op jit(solution)/shard_map/ppermute | solution.py:29
  99.0 7.9 %collective-permute-start.6 = (bf16[2,44,6]{2,1,0:T(8,128)(2,1)S(1)}, bf16[2,44,6]{2,1,0:T(8,128)(2,1)S(1)}, u32[]{:S(2)}, u32[]{:S(2)}) collective-permute-start(bf16[2,44,6]{2,1,0:T(8,128)(2,1)S(1)} %get-tuple-element.14), channel_id=1, source_target_pairs={{1,0},{2,1},{3,2},{5,4},{6,5},{7,6},{9,8},{10,9},{11,10},{13,12},{... | collective-permute-start | bytes 3176 | tf_op jit(solution)/shard_map/ppermute | solution.py:29
  102.9 0.7 copy-start.12
  102.9 0.7 copy-start.13
  102.9 0.7 copy-start.14
  103.6 0.9 copy-start.3
  104.6 0.8 copy-start.4
  119.2 0.8 copy-start.5

commit v5 on v4

--- a/solution.py
+++ b/solution.py
@@ -72,12 +72,6 @@
     for copy in copies:
         copy.start()
     return copies
-
-
-def spread_kernel(obj, out, held, sems):
-    held[...] = jnp.concatenate([obj[0], obj[1]], axis=0).astype(bf16)
-    for copy in copy_out(held, out, sems, NZ, True):
-        copy.wait()
 
 
 def row_in_strip():
@@ -134,8 +128,10 @@
     return jnp.dot(a, b, preferred_element_type=f32)
 
 
-def wave_kernel(meta, wins, probe0, probe1, probe2, probe3, intensity, table, out, err, far_all, tall):
-    x, z, core, mode = ids(meta)
+def wave_kernel(
+    meta, wins, probe0, probe1, probe2, probe3, side, turn, intensity, table, out, err, far_all, tall
+):
+    x, z, core, _ = ids(meta)
     mine = x * (NZ * NC) + z * NC + core
     row = meta[0, mine]
     col = meta[1, mine]
@@ -176,29 +172,28 @@
     gap = jnp.sqrt(power) - measured
     err[...] = jnp.sum(gap * gap, keepdims=True) * (1.0 / (PATCH * PATCH))
     scale = measured / jnp.sqrt(jnp.maximum(power, floor_level))
-    b_src = lax.broadcasted_iota(jnp.int32, (PATCH, COLS), 0)
-    b_dst = lax.broadcasted_iota(jnp.int32, (PATCH, COLS), 1)
-    keep = jnp.where(b_src == b_dst + (mode * COLS - col), 1.0, 0.0).astype(bf16)
-    k_re = dot(t_re, keep).astype(bf16)
-    k_im = dot(t_im, keep).astype(bf16)
-    back_right = jnp.concatenate(
-        [jnp.concatenate([k_re, -k_im], axis=1), jnp.concatenate([k_im, k_re], axis=1)], axis=0
-    )
-    sum_re = jnp.zeros((PATCH, COLS), f32)
-    sum_im = jnp.zeros((PATCH, COLS), f32)
-    for m in range(NM):
-        far = far_all[m]
-        scaled = jnp.concatenate(
-            [(far[:, :PATCH] * scale).astype(bf16), (far[:, PATCH:] * scale).astype(bf16)], axis=1
-        )
-        half = dot(scaled, back_right).astype(bf16)
-        back = dot(right, jnp.concatenate([half[:, :COLS], half[:, COLS:]], axis=0))
+    sums = [jnp.zeros((PATCH, 2 * COLS), f32) for _ in range(2)]
+    for pair in range(NM // 2):
+        halves = []
+        for m in (2 * pair, 2 * pair + 1):
+            far = far_all[m]
+            scaled = jnp.concatenate(
+                [(far[:, :PATCH] * scale).astype(bf16), (far[:, PATCH:] * scale).astype(bf16)],
+                axis=1,
+            )
+            halves.append(dot(scaled, turn[...]).astype(bf16))
+        stacked = [
+            jnp.concatenate([h[:, p * COLS : (p + 1) * COLS] for h in halves], axis=1)
+            for p in range(2)
+        ]
+        back = dot(right, jnp.concatenate(stacked, axis=0))
         back_re = back[:PATCH]
         back_im = back[PATCH:]
-        q_re = dot(probes[m][0], keep)
-        q_im = dot(probes[m][1], keep)
-        sum_re = sum_re + (q_re * back_re + q_im * back_im)
-        sum_im = sum_im + (q_re * back_im - q_im * back_re)
+        q_re = side[pair, 0].astype(f32)
+        q_im = side[pair, 1].astype(f32)
+        sums[0] = sums[0] + (q_re * back_re + q_im * back_im)
+        sums[1] = sums[1] + (q_re * back_im - q_im * back_re)
+    sum_re, sum_im = [v[:, :COLS] + v[:, COLS:] for v in sums]
     tall[...] = jnp.zeros(tall.shape, f32)
     tall[0, pl.ds(offset, PATCH)] = sum_re
     tall[1, pl.ds(offset, PATCH)] = sum_im
@@ -230,12 +225,26 @@
     out[...] = acc[...].astype(bf16)
 
 
-def weight_kernel(meta, probe0, probe1, probe2, probe3, out, padded):
+def weight_kernel(meta, probe0, probe1, probe2, probe3, table, out, side, turn, padded):
     x, z, core, mode = ids(meta)
     row0 = (x * (NZ * NC) + z * NC + core) * ROWS
     col0 = mode * COLS
+    probes = (probe0, probe1, probe2, probe3)
+    mine = x * (NZ * NC) + z * NC + core
+    src = lax.broadcasted_iota(jnp.int32, (PATCH, COLS), 0)
+    dst = lax.broadcasted_iota(jnp.int32, (PATCH, COLS), 1)
+    keep = jnp.where(src == dst + (col0 - meta[1, mine]), 1.0, 0.0).astype(bf16)
+    for m in range(NM):
+        for plane in range(2):
+            moved_probe = dot(probes[m][plane], keep).astype(bf16)
+            side[m // 2, plane, :, pl.ds(m % 2 * COLS, COLS)] = moved_probe
+    k_re = dot(table[0], keep).astype(bf16)
+    k_im = dot(table[1], keep).astype(bf16)
+    turn[...] = jnp.concatenate(
+        [jnp.concatenate([k_re, -k_im], axis=1), jnp.concatenate([k_im, k_re], axis=1)], axis=0
+    )
     total = jnp.zeros((PATCH, PATCH), f32)
-    for probe in (probe0, probe1, probe2, probe3):
+    for probe in probes:
         p_re = probe[0].astype(f32)
         p_im = probe[1].astype(f32)
         total = total + p_re * p_re + p_im * p_im
@@ -422,6 +431,7 @@
         cost_estimate=pl.CostEstimate(
             flops=4 * 10**9, bytes_accessed=2 * 10**7, transcendentals=0
         ),
+        compiler_params=pltpu.CompilerParams(vmem_limit_bytes=24 * 2**20),
         name="denoise",
     )(
         meta,
@@ -462,14 +472,8 @@
     place = jnp.where(lanes == 0, x, jnp.where(lanes == 1, z, jnp.where(lanes == 2, core, mode)))
     meta = jnp.concatenate([by_owner, place[None]], axis=0).astype(jnp.int32)
 
-    spread = pl.pallas_call(
-        spread_kernel,
-        out_shape=jax.ShapeDtypeStruct((NZ, 2 * ROWS, COLS), bf16),
-        in_specs=[vmem_spec()],
-        out_specs=any_spec(),
-        scratch_shapes=[pltpu.VMEM((2 * ROWS, COLS), bf16), pltpu.SemaphoreType.DMA((NZ,))],
-        name="spread",
-    )(obj_x)
+    rows = jnp.broadcast_to(obj_x.reshape(1, 2 * ROWS, COLS), (NZ, 2 * ROWS, COLS))
+    spread = rows.astype(bf16)
     near = lax.all_to_all(spread, "z", 0, 0, tiled=True)
     probe0 = probes[0].astype(bf16)
     others = [
@@ -477,6 +481,20 @@
         for k in range(1, NM)
     ]
     all_probes = (probe0, *others)
+    table = dft_table()
+    denom, side, turn = pl.pallas_call(
+        weight_kernel,
+        out_shape=(
+            jax.ShapeDtypeStruct((ROWS, COLS), f32),
+            pltpu.VMEM((NM // 2, 2, PATCH, 2 * COLS), bf16),
+            pltpu.VMEM((2 * PATCH, 2 * COLS), bf16),
+        ),
+        in_specs=[smem_spec()] + [vmem_spec()] * (NM + 1),
+        out_specs=(vmem_spec(),) * 3,
+        scratch_shapes=[pltpu.VMEM((PATCH // COLS + 2, PATCH + 2 * ROWS, COLS), f32)],
+        compiler_params=pltpu.CompilerParams(vmem_limit_bytes=12 * 2**20),
+        name="weight",
+    )(meta, *near_core(*all_probes), table)
     packed = pl.pallas_call(
         pack_kernel,
         out_shape=jax.ShapeDtypeStruct((NX * NC, HALF, 2 * ROWS, COLS), bf16),
@@ -486,6 +504,7 @@
             pltpu.VMEM((NX * NC, HALF, 2 * ROWS, COLS), bf16),
             pltpu.SemaphoreType.DMA((NX * NC,)),
         ],
+        compiler_params=pltpu.CompilerParams(vmem_limit_bytes=8 * 2**20),
         name="pack",
     )(meta, *near_core(near))
     got = lax.all_to_all(packed, ("x", "core"), 0, 0, tiled=True)
@@ -499,6 +518,7 @@
             pltpu.VMEM((2, PATCH, COLS), bf16),
             pltpu.SemaphoreType.DMA((NM,)),
         ],
+        compiler_params=pltpu.CompilerParams(vmem_limit_bytes=8 * 2**20),
         name="window",
     )(meta, *near_core(got))
     wins = lax.all_to_all(window, "mode", 0, 0, tiled=True)
@@ -508,14 +528,15 @@
             jax.ShapeDtypeStruct((NX * NC, HALF, 2 * ROWS, COLS), bf16),
             jax.ShapeDtypeStruct((1, 1), f32),
         ),
-        in_specs=[smem_spec()] + [vmem_spec()] * 7,
+        in_specs=[smem_spec()] + [vmem_spec()] * 9,
         out_specs=(vmem_spec(), vmem_spec()),
         scratch_shapes=[
             pltpu.VMEM((NM, PATCH, 2 * PATCH), f32),
             pltpu.VMEM((2, STRIPS * ROWS, COLS), f32),
         ],
+        compiler_params=pltpu.CompilerParams(vmem_limit_bytes=24 * 2**20),
         name="wave",
-    )(meta, *near_core(wins, *all_probes), intensity, dft_table())
+    )(meta, *near_core(wins, *all_probes, side, turn, intensity, table))
     back = lax.all_to_all(updates, ("x", "core"), 0, 0, tiled=True)
     partial = pl.pallas_call(
         gather_kernel,
@@ -523,18 +544,12 @@
         in_specs=[smem_spec(), vmem_spec()],
         out_specs=vmem_spec(),
         scratch_shapes=[pltpu.VMEM((NZ, 2 * ROWS, COLS), f32)],
+        compiler_params=pltpu.CompilerParams(vmem_limit_bytes=8 * 2**20),
         name="gather",
     )(meta, *near_core(back))
     pieces = lax.all_to_all(partial, "z", 0, 0, tiled=True)
-    denom = pl.pallas_call(
-        weight_kernel,
-        out_shape=jax.ShapeDtypeStruct((ROWS, COLS), f32),
-        in_specs=[smem_spec()] + [vmem_spec()] * NM,
-        out_specs=vmem_spec(),
-        scratch_shapes=[pltpu.VMEM((PATCH // COLS + 2, PATCH + 2 * ROWS, COLS), f32)],
-        name="weight",
-    )(meta, *near_core(*all_probes))
-    base = obj_x + dual_u
+    obj_later = lax.optimization_barrier(obj_x)
+    base = obj_later + dual_u
     center = denoise(base, meta, w_in, b_in, w_down, b_down, w_mid, b_mid, w_out, b_out)
     aux_next = base - center
     numer = jnp.sum(pieces.astype(f32), axis=0).reshape(2, ROWS, COLS)

time: 122 us -> 118 us (0.967)
  the two profiles are of different devices: /device:TPU:40 before, /device:TPU:8 now
where the time goes in v5:
time: 118 us; the launch traced here: 117 us
  starting transfers between devices  56.8 us (48%)
  waiting for transfers between devices  32.2 us (27%)
  Pallas kernels  18.8 us (16%)
  local copies, waits for them, and re-layouts  6.03 us (5%)
  other arithmetic  1.75 us (1%)
    all_to_all x1, waiting for transfers between devices, per_device(): near = lax.all_to_all(spread, 'z', 0, 0, tiled=True)  16.9 us
    all_to_all x1, starting transfers between devices, per_device(): near = lax.all_to_all(spread, 'z', 0, 0, tiled=True)  15.2 us
    ppermute x3, starting transfers between devices, per_device(): lax.ppermute(probe0, 'mode', [(i, (i + k) % NM) for i in range(NM)])  10.7 us
    all_to_all x1, waiting for transfers between devices, per_device(): back = lax.all_to_all(updates, ('x', 'core'), 0, 0, tiled=True)  9.3 us
    ppermute x4, starting transfers between devices, shifted(): return lax.ppermute(value, axes, pairs)  8.54 us
    all_to_all x1, starting transfers between devices, per_device(): back = lax.all_to_all(updates, ('x', 'core'), 0, 0, tiled=True)  7.91 us
    pallas_call x1, Pallas kernels, denoise(): pl.pallas_call(denoise_kernel, out_shape=jax.ShapeDtypeStruct((2, ROWS, C...  5.72 us
    all_to_all x1, starting transfers between devices, per_device(): pieces = lax.all_to_all(partial, 'z', 0, 0, tiled=True)  5.09 us
  transfers between devices with their start and end apart: 12, of which 6 were waited for; matrix products, arithmetic and copies ran while one was open for 1% of the time, Pallas kernels for 13%

profile of v5, /device:TPU:8, one launch (start us, length us, event | category | flops | bytes accessed | tf_op | source)
XLA Modules:
  0.0 117.0 jit_solution(15878039384003756533)
XLA Ops:
  0.6 0.8 convert_element_type.27
  1.4 0.7 broadcast_in_dim.53
  2.1 15.2 %all-to-all-start = ((bf16[16,64,128]{2,1,0:T(8,128)(2,1)}), bf16[16,64,128]{2,1,0:T(8,128)(2,1)S(1)}, u32[]{:S(2)}, u32[]{:S(2)}) async-start(bf16[16,64,128]{2,1,0:T(8,128)(2,1)} %broadcast_in_dim.53), calls=%async_computation | async-start | bytes 524288 | tf_op jit(solution)/shard_map/all_to_all | solution.py:477
  17.3 0.0 copy-start.13
  17.4 0.6 copy-done.13
  18.0 0.7 copy-done.12
  18.7 0.1 select_reduce_fusion
  18.8 16.9 %all-to-all-done.near = bf16[16,64,128]{2,1,0:T(8,128)(2,1)S(1)} async-done(((bf16[16,64,128]{2,1,0:T(8,128)(2,1)}), bf16[16,64,128]{2,1,0:T(8,128)(2,1)S(1)}, u32[]{:S(2)}, u32[]{:S(2)}) %all-to-all-start) | async-done | bytes 262176 | tf_op jit(solution)/shard_map/all_to_all | solution.py:477
  35.7 1.6 %pack.1 = bf16[8,4,64,128]{3,2,1,0:T(8,128)(2,1)} custom-call(s32[3,128]{1,0:T(4,128)S(1)} %pad_add_fusion.meta, bf16[16,64,128]{2,1,0:T(8,128)(2,1)S(1)} %all-to-all-done.near), custom_call_target="tpu_custom_call" | custom-call | tf_op jit(solution)/shard_map/pack/pallas_call | solution.py:498
  37.4 0.0 copy-start.3
  37.4 4.4 %all-to-all-start.1 = ((bf16[8,4,64,128]{3,2,1,0:T(8,128)(2,1)}), bf16[8,4,64,128]{3,2,1,0:T(8,128)(2,1)S(1)}, u32[]{:S(2)}, u32[]{:S(2)}) async-start(bf16[8,4,64,128]{3,2,1,0:T(8,128)(2,1)} %pack.1), calls=%async_computation.1 | async-start | bytes 1048576 | tf_op jit(solution)/shard_map/all_to_all | solution.py:510
  41.9 3.5 %collective-permute-start = (bf16[2,256,256]{2,1,0:T(8,128)(2,1)S(1)}, bf16[2,256,256]{2,1,0:T(8,128)(2,1)S(1)}, u32[]{:S(2)}, u32[]{:S(2)}) collective-permute-start(bf16[2,256,256]{2,1,0:T(8,128)(2,1)S(1)} %convert_bitcast_fusion.probe0), channel_id=1, source_target_pairs={{0,1},{1,2},{2,3},{3,0},{4,5},{5,6},{6,7},{7,4},{8,9},{9,10},{10,1... | collective-permute-start | bytes 786440 | tf_op jit(solution)/shard_map/ppermute | solution.py:480
  45.4 2.8 %collective-permute-start.1 = (bf16[2,256,256]{2,1,0:T(8,128)(2,1)S(1)}, bf16[2,256,256]{2,1,0:T(8,128)(2,1)S(1)}, u32[]{:S(2)}, u32[]{:S(2)}) collective-permute-start(bf16[2,256,256]{2,1,0:T(8,128)(2,1)S(1)} %convert_bitcast_fusion.probe0), channel_id=1, source_target_pairs={{0,2},{1,3},{2,0},{3,1},{4,6},{5,7},{6,4},{7,5},{8,10},{9,11},{10,... | collective-permute-start | bytes 786440 | tf_op jit(solution)/shard_map/ppermute | solution.py:480
  48.2 4.3 %collective-permute-start.2 = (bf16[2,256,256]{2,1,0:T(8,128)(2,1)S(1)}, bf16[2,256,256]{2,1,0:T(8,128)(2,1)S(1)}, u32[]{:S(2)}, u32[]{:S(2)}) collective-permute-start(bf16[2,256,256]{2,1,0:T(8,128)(2,1)S(1)} %convert_bitcast_fusion.probe0), channel_id=1, source_target_pairs={{0,3},{1,0},{2,1},{3,2},{4,7},{5,4},{6,5},{7,6},{8,11},{9,8},{10,9... | collective-permute-start | bytes 786440 | tf_op jit(solution)/shard_map/ppermute | solution.py:480
  52.5 0.0 all-to-all-done.1.got
  52.5 1.5 %window.1 = bf16[4,2,256,128]{3,2,1,0:T(8,128)(2,1)} custom-call(s32[3,128]{1,0:T(4,128)S(1)} %pad_add_fusion.meta, bf16[8,4,64,128]{3,2,1,0:T(8,128)(2,1)S(1)} %all-to-all-done.1.got), custom_call_target="tpu_custom_call" | custom-call | tf_op jit(solution)/shard_map/window/pallas_call | solution.py:511
  54.0 0.0 copy-start.4
  54.0 0.0 copy-start.5
  54.1 0.0 copy-start
  54.1 4.9 %all-to-all-start.2 = ((bf16[4,2,256,128]{3,2,1,0:T(8,128)(2,1)}), bf16[4,2,256,128]{3,2,1,0:T(8,128)(2,1)S(1)}, u32[]{:S(2)}, u32[]{:S(2)}) async-start(bf16[4,2,256,128]{3,2,1,0:T(8,128)(2,1)} %window.1), calls=%async_computation.2 | async-start | bytes 1048576 | tf_op jit(solution)/shard_map/all_to_all | solution.py:524
  59.0 1.3 %collective-permute-start.3 = (bf16[2,6,128]{2,1,0:T(8,128)(2,1)S(1)}, bf16[2,6,128]{2,1,0:T(8,128)(2,1)S(1)}, u32[]{:S(2)}, u32[]{:S(2)}) collective-permute-start(bf16[2,6,128]{2,1,0:T(8,128)(2,1)S(1)} %get-tuple-element.21), channel_id=1, source_target_pairs={{0,4},{4,8},{8,12},{12,16},{16,20},{20,24},{24,28},{28,32},{32,36}... | collective-permute-start | bytes 9224 | tf_op jit(solution)/shard_map/ppermute | solution.py:29
  60.3 0.0 copy-start.1
  60.3 1.4 %collective-permute-start.4 = (bf16[2,6,128]{2,1,0:T(8,128)(2,1)S(1)}, bf16[2,6,128]{2,1,0:T(8,128)(2,1)S(1)}, u32[]{:S(2)}, u32[]{:S(2)}) collective-permute-start(bf16[2,6,128]{2,1,0:T(8,128)(2,1)S(1)} %get-tuple-element.22), channel_id=1, source_target_pairs={{4,0},{8,4},{12,8},{16,12},{20,16},{24,20},{28,24},{32,28},{36,32}... | collective-permute-start | bytes 9224 | tf_op jit(solution)/shard_map/ppermute | solution.py:29
  61.8 0.0 collective-permute-done.probe1
  61.8 0.0 collective-permute-done.1.probe2
  61.8 1.1 collective-permute-done.2.probe3
  62.9 3.7 %weight.1 = (f32[32,128]{1,0:T(8,128)S(1)}, bf16[2,2,256,256]{3,2,1,0:T(8,128)(2,1)S(1)}, bf16[512,256]{1,0:T(8,128)(2,1)S(1)}) custom-call(s32[3,128]{1,0:T(4,128)S(1)} %pad_add_fusion.meta, bf16[2,256,256]{2,1,0:T(8,128)(2,1)S(1)} %convert_bitcast_fusion.probe0, bf16[2,256,256]{2,1,0:T(8,128)(2,1)S(1)} %collective-permute-done.probe1, ...), custom_call_target="tpu_custom_call" | custom-call | tf_op jit(solution)/shard_map/weight/pallas_call | solution.py:485
  66.6 1.8 %all-to-all-done.2.wins = bf16[4,2,256,128]{3,2,1,0:T(8,128)(2,1)S(1)} async-done(((bf16[4,2,256,128]{3,2,1,0:T(8,128)(2,1)}), bf16[4,2,256,128]{3,2,1,0:T(8,128)(2,1)S(1)}, u32[]{:S(2)}, u32[]{:S(2)}) %all-to-all-start.2) | async-done | bytes 524320 | tf_op jit(solution)/shard_map/all_to_all | solution.py:524
  68.5 4.6 %wave.1 = (bf16[8,4,64,128]{3,2,1,0:T(8,128)(2,1)}, f32[1,1]{1,0:T(1,128)}) custom-call(s32[3,128]{1,0:T(4,128)S(1)} %pad_add_fusion.meta, bf16[4,2,256,128]{3,2,1,0:T(8,128)(2,1)S(1)} %all-to-all-done.2.wins, bf16[2,256,256]{2,1,0:T(8,128)(2,1)S(1)} %convert_bitcast_fusion.probe0, bf16[2,256,256]{2,1,0:T(8,128)(2,1)S(1)} %collective-permute-done.probe1, ...), custom_call_target="tpu_custom_call" | custom-call | tf_op jit(solution)/shard_map/wave/pallas_call | solution.py:525
  73.0 7.9 %all-to-all-start.3 = ((bf16[8,4,64,128]{3,2,1,0:T(8,128)(2,1)}), bf16[8,4,64,128]{3,2,1,0:T(8,128)(2,1)S(1)}, u32[]{:S(2)}, u32[]{:S(2)}) async-start(bf16[8,4,64,128]{3,2,1,0:T(8,128)(2,1)} %get-tuple-element.11), calls=%async_computation.3 | async-start | bytes 1048576 | tf_op jit(solution)/shard_map/all_to_all | solution.py:540
  81.0 0.0 copy-start.8
  81.0 0.2 convolution_bitcast_fusion
  81.2 0.5 copy-done.8
  81.7 0.2 fusion.1
  81.9 0.0 collective-permute-done.3
  81.9 0.0 collective-permute-done.4
  82.0 9.3 %all-to-all-done.3.got = bf16[8,4,64,128]{3,2,1,0:T(8,128)(2,1)S(1)} async-done(((bf16[8,4,64,128]{3,2,1,0:T(8,128)(2,1)}), bf16[8,4,64,128]{3,2,1,0:T(8,128)(2,1)S(1)}, u32[]{:S(2)}, u32[]{:S(2)}) %all-to-all-start.3) | async-done | bytes 524320 | tf_op jit(solution)/shard_map/all_to_all | solution.py:540
  91.3 1.6 %gather.1 = bf16[16,64,128]{2,1,0:T(8,128)(2,1)} custom-call(s32[3,128]{1,0:T(4,128)S(1)} %pad_add_fusion.meta, bf16[8,4,64,128]{3,2,1,0:T(8,128)(2,1)S(1)} %all-to-all-done.3.got), custom_call_target="tpu_custom_call" | custom-call | tf_op jit(solution)/shard_map/gather/pallas_call | solution.py:541
  92.9 5.1 %all-to-all-start.4 = ((bf16[16,64,128]{2,1,0:T(8,128)(2,1)}), bf16[16,64,128]{2,1,0:T(8,128)(2,1)S(1)}, u32[]{:S(2)}, u32[]{:S(2)}) async-start(bf16[16,64,128]{2,1,0:T(8,128)(2,1)} %gather.1), calls=%async_computation.4 | async-start | bytes 524288 | tf_op jit(solution)/shard_map/all_to_all | solution.py:550
  98.0 0.1 fusion.6
  98.1 3.4 %collective-permute-start.5 = (bf16[2,44,6]{2,1,0:T(8,128)(2,1)S(1)}, bf16[2,44,6]{2,1,0:T(8,128)(2,1)S(1)}, u32[]{:S(2)}, u32[]{:S(2)}) collective-permute-start(bf16[2,44,6]{2,1,0:T(8,128)(2,1)S(1)} %get-tuple-element.19), channel_id=1, source_target_pairs={{0,1},{1,2},{2,3},{4,5},{5,6},{6,7},{8,9},{9,10},{10,11},{12,13},{... | collective-permute-start | bytes 3176 | tf_op jit(solution)/shard_map/ppermute | solution.py:29
  101.5 2.5 %collective-permute-start.6 = (bf16[2,44,6]{2,1,0:T(8,128)(2,1)S(1)}, bf16[2,44,6]{2,1,0:T(8,128)(2,1)S(1)}, u32[]{:S(2)}, u32[]{:S(2)}) collective-permute-start(bf16[2,44,6]{2,1,0:T(8,128)(2,1)S(1)} %get-tuple-element.20), channel_id=1, source_target_pairs={{1,0},{2,1},{3,2},{5,4},{6,5},{7,6},{9,8},{10,9},{11,10},{13,12},{... | collective-permute-start | bytes 3176 | tf_op jit(solution)/shard_map/ppermute | solution.py:29
  103.9 0.0 copy-start.14
  103.9 0.0 copy-start.15
  104.0 0.0 copy-start.16
  104.0 0.6 copy-done.14
  104.6 0.0 copy-done.15
  104.6 0.0 copy-done.16
  104.6 0.0 copy-start.6
  104.7 0.1 reshape.85.last_w
  104.8 0.7 copy-done.6
  105.5 0.1 copy.47
  105.7 0.0 copy-start.7
  105.7 0.1 copy.50.mid_w
  105.8 0.7 copy-done.7
  106.5 0.1 reshape.83.down_w
  106.6 0.1 copy.51.biases
  106.7 0.5 collective-permute-done.6
  107.2 0.1 pad_maximum_fusion.ext
  107.3 0.0 copy-start.2
  107.3 0.6 copy-done.2
  108.0 5.7 %denoise.1 = f32[2,32,128]{2,1,0:T(8,128)S(1)} custom-call(s32[3,128]{1,0:T(4,128)S(1)} %pad_add_fusion.meta, f32[2]{0:T(128)S(1)} %copy-done.2, bf16[2,44,140]{2,1,0:T(8,128)(2,1)S(1)} %pad_maximum_fusion.ext, bf16[192,72]{1,0:T(8,128)(2,1)S(1)} %bitcast.30, bf16[48,192]{1,0:T(8,128)(2,1)S(1)} %reshape.83.down_w, bf16[48,432]{1,0:T(8,128)(2,1)S(1)} %copy.50.mid_w, ...), custom_call_target="tpu_custom_call" | custom-call | flops 4000000000 | bytes 20000000 | tf_op jit(solution)/shard_map/denoise/pallas_call | solution.py:415
  113.7 2.6 %all-to-all-done.4 = bf16[16,64,128]{2,1,0:T(8,128)(2,1)S(1)} async-done(((bf16[16,64,128]{2,1,0:T(8,128)(2,1)}), bf16[16,64,128]{2,1,0:T(8,128)(2,1)S(1)}, u32[]{:S(2)}, u32[]{:S(2)}) %all-to-all-start.4) | async-done | bytes 262176 | tf_op jit(solution)/shard_map/all_to_all | solution.py:550
  116.3 0.6 add_subtract_fusion
  (25 shorter events, 0.2 us)
Async XLA Ops:
  2.1 33.6 %all-to-all-start = ((bf16[16,64,128]{2,1,0:T(8,128)(2,1)}), bf16[16,64,128]{2,1,0:T(8,128)(2,1)S(1)}, u32[]{:S(2)}, u32[]{:S(2)}) async-start(bf16[16,64,128]{2,1,0:T(8,128)(2,1)} %broadcast_in_dim.53), calls=%async_computation | async-start | bytes 524288 | tf_op jit(solution)/shard_map/all_to_all | solution.py:477
  17.3 0.7 copy-start.13
  18.0 0.7 copy-start.12
  37.4 4.5 %copy-start.3 = (f32[1,2,256,256]{3,2,1,0:T(8,128)S(1)}, f32[1,2,256,256]{3,2,1,0:T(8,128)}, u32[]{:S(2)}) copy-start(f32[1,2,256,256]{3,2,1,0:T(8,128)} %param.19) | copy-start | bytes 1572868
  37.4 15.2 %all-to-all-start.1 = ((bf16[8,4,64,128]{3,2,1,0:T(8,128)(2,1)}), bf16[8,4,64,128]{3,2,1,0:T(8,128)(2,1)S(1)}, u32[]{:S(2)}, u32[]{:S(2)}) async-start(bf16[8,4,64,128]{3,2,1,0:T(8,128)(2,1)} %pack.1), calls=%async_computation.1 | async-start | bytes 1048576 | tf_op jit(solution)/shard_map/all_to_all | solution.py:510
  41.9 19.9 %collective-permute-start = (bf16[2,256,256]{2,1,0:T(8,128)(2,1)S(1)}, bf16[2,256,256]{2,1,0:T(8,128)(2,1)S(1)}, u32[]{:S(2)}, u32[]{:S(2)}) collective-permute-start(bf16[2,256,256]{2,1,0:T(8,128)(2,1)S(1)} %convert_bitcast_fusion.probe0), channel_id=1, source_target_pairs={{0,1},{1,2},{2,3},{3,0},{4,5},{5,6},{6,7},{7,4},{8,9},{9,10},{10,1... | collective-permute-start | bytes 786440 | tf_op jit(solution)/shard_map/ppermute | solution.py:480
  45.4 16.4 %collective-permute-start.1 = (bf16[2,256,256]{2,1,0:T(8,128)(2,1)S(1)}, bf16[2,256,256]{2,1,0:T(8,128)(2,1)S(1)}, u32[]{:S(2)}, u32[]{:S(2)}) collective-permute-start(bf16[2,256,256]{2,1,0:T(8,128)(2,1)S(1)} %convert_bitcast_fusion.probe0), channel_id=1, source_target_pairs={{0,2},{1,3},{2,0},{3,1},{4,6},{5,7},{6,4},{7,5},{8,10},{9,11},{10,... | collective-permute-start | bytes 786440 | tf_op jit(solution)/shard_map/ppermute | solution.py:480
  48.2 14.7 %collective-permute-start.2 = (bf16[2,256,256]{2,1,0:T(8,128)(2,1)S(1)}, bf16[2,256,256]{2,1,0:T(8,128)(2,1)S(1)}, u32[]{:S(2)}, u32[]{:S(2)}) collective-permute-start(bf16[2,256,256]{2,1,0:T(8,128)(2,1)S(1)} %convert_bitcast_fusion.probe0), channel_id=1, source_target_pairs={{0,3},{1,0},{2,1},{3,2},{4,7},{5,4},{6,5},{7,6},{8,11},{9,8},{10,9... | collective-permute-start | bytes 786440 | tf_op jit(solution)/shard_map/ppermute | solution.py:480
  54.0 5.0 %copy-start.4 = (f32[2,32,128]{2,1,0:T(8,128)S(1)}, f32[2,32,128]{2,1,0:T(8,128)}, u32[]{:S(2)}) copy-start(f32[2,32,128]{2,1,0:T(8,128)} %param.18) | copy-start | bytes 98308
  54.0 5.0 %copy-start.5 = (f32[2,32,128]{2,1,0:T(8,128)S(1)}, f32[2,32,128]{2,1,0:T(8,128)}, u32[]{:S(2)}) copy-start(f32[2,32,128]{2,1,0:T(8,128)} %param.17) | copy-start | bytes 98308
  54.1 8.8 %copy-start = (bf16[2,256,256]{2,1,0:T(8,128)(2,1)S(1)}, bf16[2,256,256]{2,1,0:T(8,128)(2,1)}, u32[]{:S(2)}) copy-start(bf16[2,256,256]{2,1,0:T(8,128)(2,1)} %constant.43.table) | copy-start | bytes 786436
  54.1 14.4 %all-to-all-start.2 = ((bf16[4,2,256,128]{3,2,1,0:T(8,128)(2,1)}), bf16[4,2,256,128]{3,2,1,0:T(8,128)(2,1)S(1)}, u32[]{:S(2)}, u32[]{:S(2)}) async-start(bf16[4,2,256,128]{3,2,1,0:T(8,128)(2,1)} %window.1), calls=%async_computation.2 | async-start | bytes 1048576 | tf_op jit(solution)/shard_map/all_to_all | solution.py:524
  59.0 22.9 %collective-permute-start.3 = (bf16[2,6,128]{2,1,0:T(8,128)(2,1)S(1)}, bf16[2,6,128]{2,1,0:T(8,128)(2,1)S(1)}, u32[]{:S(2)}, u32[]{:S(2)}) collective-permute-start(bf16[2,6,128]{2,1,0:T(8,128)(2,1)S(1)} %get-tuple-element.21), channel_id=1, source_target_pairs={{0,4},{4,8},{8,12},{12,16},{16,20},{20,24},{24,28},{28,32},{32,36}... | collective-permute-start | bytes 9224 | tf_op jit(solution)/shard_map/ppermute | solution.py:29
  60.3 8.1 %copy-start.1 = (f32[1,256,256]{2,1,0:T(8,128)S(1)}, f32[1,256,256]{2,1,0:T(8,128)}, u32[]{:S(2)}) copy-start(f32[1,256,256]{2,1,0:T(8,128)} %intensity.1) | copy-start | bytes 786436
  60.3 21.6 %collective-permute-start.4 = (bf16[2,6,128]{2,1,0:T(8,128)(2,1)S(1)}, bf16[2,6,128]{2,1,0:T(8,128)(2,1)S(1)}, u32[]{:S(2)}, u32[]{:S(2)}) collective-permute-start(bf16[2,6,128]{2,1,0:T(8,128)(2,1)S(1)} %get-tuple-element.22), channel_id=1, source_target_pairs={{4,0},{8,4},{12,8},{16,12},{20,16},{24,20},{28,24},{32,28},{36,32}... | collective-permute-start | bytes 9224 | tf_op jit(solution)/shard_map/ppermute | solution.py:29
  73.0 7.9 %copy-start.9 = (bf16[9,36,4,1]{1,0,3,2:T(8,128)(2,1)S(1)}, bf16[9,36,4,1]{1,0,3,2:T(8,128)(2,1)}, u32[]{:S(2)}) copy-start(bf16[9,36,4,1]{1,0,3,2:T(8,128)(2,1)} %constant.46) | copy-start | bytes 7780
  73.0 7.9 %copy-start.10 = (bf16[9,2,48]{2,1,0:T(2,128)(2,1)S(1)}, bf16[9,2,48]{2,1,0:T(2,128)(2,1)}, u32[]{:S(2)}) copy-start(bf16[9,2,48]{2,1,0:T(2,128)(2,1)} %param.29) | copy-start | bytes 5188
  73.0 8.1 %copy-start.11 = (bf16[9,48,2]{1,2,0:T(2,128)(2,1)S(1)}, bf16[9,48,2]{1,2,0:T(2,128)(2,1)}, u32[]{:S(2)}) copy-start(bf16[9,48,2]{1,2,0:T(2,128)(2,1)} %param.23) | copy-start | bytes 5188
  73.0 18.2 %all-to-all-start.3 = ((bf16[8,4,64,128]{3,2,1,0:T(8,128)(2,1)}), bf16[8,4,64,128]{3,2,1,0:T(8,128)(2,1)S(1)}, u32[]{:S(2)}, u32[]{:S(2)}) async-start(bf16[8,4,64,128]{3,2,1,0:T(8,128)(2,1)} %get-tuple-element.11), calls=%async_computation.3 | async-start | bytes 1048576 | tf_op jit(solution)/shard_map/all_to_all | solution.py:540
  81.0 0.8 copy-start.8
  92.9 23.4 %all-to-all-start.4 = ((bf16[16,64,128]{2,1,0:T(8,128)(2,1)}), bf16[16,64,128]{2,1,0:T(8,128)(2,1)S(1)}, u32[]{:S(2)}, u32[]{:S(2)}) async-start(bf16[16,64,128]{2,1,0:T(8,128)(2,1)} %gather.1), calls=%async_computation.4 | async-start | bytes 524288 | tf_op jit(solution)/shard_map/all_to_all | solution.py:550
  98.1 8.6 %collective-permute-start.5 = (bf16[2,44,6]{2,1,0:T(8,128)(2,1)S(1)}, bf16[2,44,6]{2,1,0:T(8,128)(2,1)S(1)}, u32[]{:S(2)}, u32[]{:S(2)}) collective-permute-start(bf16[2,44,6]{2,1,0:T(8,128)(2,1)S(1)} %get-tuple-element.19), channel_id=1, source_target_pairs={{0,1},{1,2},{2,3},{4,5},{5,6},{6,7},{8,9},{9,10},{10,11},{12,13},{... | collective-permute-start | bytes 3176 | tf_op jit(solution)/shard_map/ppermute | solution.py:29
  101.5 5.7 %collective-permute-start.6 = (bf16[2,44,6]{2,1,0:T(8,128)(2,1)S(1)}, bf16[2,44,6]{2,1,0:T(8,128)(2,1)S(1)}, u32[]{:S(2)}, u32[]{:S(2)}) collective-permute-start(bf16[2,44,6]{2,1,0:T(8,128)(2,1)S(1)} %get-tuple-element.20), channel_id=1, source_target_pairs={{1,0},{2,1},{3,2},{5,4},{6,5},{7,6},{9,8},{10,9},{11,10},{13,12},{... | collective-permute-start | bytes 3176 | tf_op jit(solution)/shard_map/ppermute | solution.py:29
  103.9 0.7 copy-start.14
  103.9 0.7 copy-start.15
  104.0 0.7 copy-start.16
  104.6 0.9 copy-start.6
  105.7 0.8 copy-start.7
  107.3 0.7 copy-start.2

commit v6 on v5

--- a/solution.py
+++ b/solution.py
@@ -129,12 +129,11 @@
 
 
 def wave_kernel(
-    meta, wins, probe0, probe1, probe2, probe3, side, turn, intensity, table, out, err, far_all, tall
+    meta, wins, probe0, probe1, probe2, probe3, side, turn, take, intensity, table, out, err, far_all, tall
 ):
     x, z, core, _ = ids(meta)
     mine = x * (NZ * NC) + z * NC + core
     row = meta[0, mine]
-    col = meta[1, mine]
     s0 = row // ROWS
     offset = row - s0 * ROWS
     t_re = table[0]
@@ -149,10 +148,7 @@
     full = jnp.concatenate(
         [jnp.concatenate([wins[m, p] for m in range(NM)], axis=1) for p in range(2)], axis=0
     )
-    src = lax.broadcasted_iota(jnp.int32, (NM * COLS, PATCH), 0)
-    dst = lax.broadcasted_iota(jnp.int32, (NM * COLS, PATCH), 1)
-    take = jnp.where(src == dst + col, 1.0, 0.0).astype(bf16)
-    patch = dot(full, take)
+    patch = dot(full, take[...])
     obj_re = patch[:PATCH]
     obj_im = patch[PATCH:]
     probes = (probe0, probe1, probe2, probe3)
@@ -225,12 +221,15 @@
     out[...] = acc[...].astype(bf16)
 
 
-def weight_kernel(meta, probe0, probe1, probe2, probe3, table, out, side, turn, padded):
+def weight_kernel(meta, probe0, probe1, probe2, probe3, table, out, side, turn, take, padded):
     x, z, core, mode = ids(meta)
     row0 = (x * (NZ * NC) + z * NC + core) * ROWS
     col0 = mode * COLS
     probes = (probe0, probe1, probe2, probe3)
     mine = x * (NZ * NC) + z * NC + core
+    src = lax.broadcasted_iota(jnp.int32, (NM * COLS, PATCH), 0)
+    dst = lax.broadcasted_iota(jnp.int32, (NM * COLS, PATCH), 1)
+    take[...] = jnp.where(src == dst + meta[1, mine], 1.0, 0.0).astype(bf16)
     src = lax.broadcasted_iota(jnp.int32, (PATCH, COLS), 0)
     dst = lax.broadcasted_iota(jnp.int32, (PATCH, COLS), 1)
     keep = jnp.where(src == dst + (col0 - meta[1, mine]), 1.0, 0.0).astype(bf16)
@@ -473,7 +472,8 @@
     meta = jnp.concatenate([by_owner, place[None]], axis=0).astype(jnp.int32)
 
     rows = jnp.broadcast_to(obj_x.reshape(1, 2 * ROWS, COLS), (NZ, 2 * ROWS, COLS))
-    spread = rows.astype(bf16)
+    slots = lax.broadcasted_iota(jnp.int32, rows.shape, 0)
+    spread = jnp.where(slots + z >= 0, rows, 0.0).astype(bf16)
     near = lax.all_to_all(spread, "z", 0, 0, tiled=True)
     probe0 = probes[0].astype(bf16)
     others = [
@@ -482,15 +482,16 @@
     ]
     all_probes = (probe0, *others)
     table = dft_table()
-    denom, side, turn = pl.pallas_call(
+    denom, side, turn, take = pl.pallas_call(
         weight_kernel,
         out_shape=(
             jax.ShapeDtypeStruct((ROWS, COLS), f32),
             pltpu.VMEM((NM // 2, 2, PATCH, 2 * COLS), bf16),
             pltpu.VMEM((2 * PATCH, 2 * COLS), bf16),
+            pltpu.VMEM((NM * COLS, PATCH), bf16),
         ),
         in_specs=[smem_spec()] + [vmem_spec()] * (NM + 1),
-        out_specs=(vmem_spec(),) * 3,
+        out_specs=(vmem_spec(),) * 4,
         scratch_shapes=[pltpu.VMEM((PATCH // COLS + 2, PATCH + 2 * ROWS, COLS), f32)],
         compiler_params=pltpu.CompilerParams(vmem_limit_bytes=12 * 2**20),
         name="weight",
@@ -528,7 +529,7 @@
             jax.ShapeDtypeStruct((NX * NC, HALF, 2 * ROWS, COLS), bf16),
             jax.ShapeDtypeStruct((1, 1), f32),
         ),
-        in_specs=[smem_spec()] + [vmem_spec()] * 9,
+        in_specs=[smem_spec()] + [vmem_spec()] * 10,
         out_specs=(vmem_spec(), vmem_spec()),
         scratch_shapes=[
             pltpu.VMEM((NM, PATCH, 2 * PATCH), f32),
@@ -536,7 +537,7 @@
         ],
         compiler_params=pltpu.CompilerParams(vmem_limit_bytes=24 * 2**20),
         name="wave",
-    )(meta, *near_core(wins, *all_probes, side, turn, intensity, table))
+    )(meta, *near_core(wins, *all_probes, side, turn, take, intensity, table))
     back = lax.all_to_all(updates, ("x", "core"), 0, 0, tiled=True)
     partial = pl.pallas_call(
         gather_kernel,

time: 118 us -> 118 us (level)
  no operation moved by 1% of the time
where the time goes in v6:
time: 118 us; the launch traced here: 117 us
  starting transfers between devices  56.8 us (48%)
  waiting for transfers between devices  32.2 us (27%)
  Pallas kernels  18.8 us (16%)
  local copies, waits for them, and re-layouts  5.29 us (4%)
  other arithmetic  2.55 us (2%)
    all_to_all x1, waiting for transfers between devices, per_device(): near = lax.all_to_all(spread, 'z', 0, 0, tiled=True)  16.9 us
    all_to_all x1, starting transfers between devices, per_device(): near = lax.all_to_all(spread, 'z', 0, 0, tiled=True)  15.2 us
    ppermute x3, starting transfers between devices, per_device(): lax.ppermute(probe0, 'mode', [(i, (i + k) % NM) for i in range(NM)])  10.7 us
    all_to_all x1, waiting for transfers between devices, per_device(): back = lax.all_to_all(updates, ('x', 'core'), 0, 0, tiled=True)  9.3 us
    ppermute x4, starting transfers between devices, shifted(): return lax.ppermute(value, axes, pairs)  8.54 us
    all_to_all x1, starting transfers between devices, per_device(): back = lax.all_to_all(updates, ('x', 'core'), 0, 0, tiled=True)  7.96 us
    pallas_call x1, Pallas kernels, denoise(): pl.pallas_call(denoise_kernel, out_shape=jax.ShapeDtypeStruct((2, ROWS, C...  5.72 us
    all_to_all x1, starting transfers between devices, per_device(): pieces = lax.all_to_all(partial, 'z', 0, 0, tiled=True)  5.09 us
  transfers between devices with their start and end apart: 12, of which 6 were waited for; matrix products, arithmetic and copies ran while one was open for 1% of the time, Pallas kernels for 13%

profile of v6, /device:TPU:8, one launch (start us, length us, event | category | flops | bytes accessed | tf_op | source)
XLA Modules:
  0.0 117.1 jit_solution(11123232963647646100)
XLA Ops:
  0.6 1.6 %select_convert_fusion = bf16[16,64,128]{2,1,0:T(8,128)(2,1)} fusion(f32[64,128]{1,0:T(8,128)} %bitcast.32, pred[16]{0:T(512)(128)(4,1)S(1)} %add_compare_fusion), kind=kLoop, calls=%fused_computation.2 | loop fusion | flops 131072 | bytes 294928 | tf_op jit(solution)/shard_map/convert_element_type | solution.py:476
  2.2 15.2 %all-to-all-start = ((bf16[16,64,128]{2,1,0:T(8,128)(2,1)}), bf16[16,64,128]{2,1,0:T(8,128)(2,1)S(1)}, u32[]{:S(2)}, u32[]{:S(2)}) async-start(bf16[16,64,128]{2,1,0:T(8,128)(2,1)} %select_convert_fusion), calls=%async_computation | async-start | bytes 524288 | tf_op jit(solution)/shard_map/all_to_all | solution.py:477
  17.4 0.0 copy-start.13
  17.4 0.6 copy-done.13
  18.1 0.7 copy-done.12
  18.8 0.1 select_reduce_fusion
  18.9 16.9 %all-to-all-done.near = bf16[16,64,128]{2,1,0:T(8,128)(2,1)S(1)} async-done(((bf16[16,64,128]{2,1,0:T(8,128)(2,1)}), bf16[16,64,128]{2,1,0:T(8,128)(2,1)S(1)}, u32[]{:S(2)}, u32[]{:S(2)}) %all-to-all-start) | async-done | bytes 262176 | tf_op jit(solution)/shard_map/all_to_all | solution.py:477
  35.8 1.6 %pack.1 = bf16[8,4,64,128]{3,2,1,0:T(8,128)(2,1)} custom-call(s32[3,128]{1,0:T(4,128)S(1)} %pad_add_fusion.meta, bf16[16,64,128]{2,1,0:T(8,128)(2,1)S(1)} %all-to-all-done.near), custom_call_target="tpu_custom_call" | custom-call | tf_op jit(solution)/shard_map/pack/pallas_call | solution.py:499
  37.4 0.0 copy-start.3
  37.4 4.4 %all-to-all-start.1 = ((bf16[8,4,64,128]{3,2,1,0:T(8,128)(2,1)}), bf16[8,4,64,128]{3,2,1,0:T(8,128)(2,1)S(1)}, u32[]{:S(2)}, u32[]{:S(2)}) async-start(bf16[8,4,64,128]{3,2,1,0:T(8,128)(2,1)} %pack.1), calls=%async_computation.1 | async-start | bytes 1048576 | tf_op jit(solution)/shard_map/all_to_all | solution.py:511
  41.9 3.5 %collective-permute-start = (bf16[2,256,256]{2,1,0:T(8,128)(2,1)S(1)}, bf16[2,256,256]{2,1,0:T(8,128)(2,1)S(1)}, u32[]{:S(2)}, u32[]{:S(2)}) collective-permute-start(bf16[2,256,256]{2,1,0:T(8,128)(2,1)S(1)} %convert_bitcast_fusion.probe0), channel_id=1, source_target_pairs={{0,1},{1,2},{2,3},{3,0},{4,5},{5,6},{6,7},{7,4},{8,9},{9,10},{10,1... | collective-permute-start | bytes 786440 | tf_op jit(solution)/shard_map/ppermute | solution.py:480
  45.4 2.8 %collective-permute-start.1 = (bf16[2,256,256]{2,1,0:T(8,128)(2,1)S(1)}, bf16[2,256,256]{2,1,0:T(8,128)(2,1)S(1)}, u32[]{:S(2)}, u32[]{:S(2)}) collective-permute-start(bf16[2,256,256]{2,1,0:T(8,128)(2,1)S(1)} %convert_bitcast_fusion.probe0), channel_id=1, source_target_pairs={{0,2},{1,3},{2,0},{3,1},{4,6},{5,7},{6,4},{7,5},{8,10},{9,11},{10,... | collective-permute-start | bytes 786440 | tf_op jit(solution)/shard_map/ppermute | solution.py:480
  48.3 4.3 %collective-permute-start.2 = (bf16[2,256,256]{2,1,0:T(8,128)(2,1)S(1)}, bf16[2,256,256]{2,1,0:T(8,128)(2,1)S(1)}, u32[]{:S(2)}, u32[]{:S(2)}) collective-permute-start(bf16[2,256,256]{2,1,0:T(8,128)(2,1)S(1)} %convert_bitcast_fusion.probe0), channel_id=1, source_target_pairs={{0,3},{1,0},{2,1},{3,2},{4,7},{5,4},{6,5},{7,6},{8,11},{9,8},{10,9... | collective-permute-start | bytes 786440 | tf_op jit(solution)/shard_map/ppermute | solution.py:480
  52.6 0.0 all-to-all-done.1.got
  52.6 1.5 %window.1 = bf16[4,2,256,128]{3,2,1,0:T(8,128)(2,1)} custom-call(s32[3,128]{1,0:T(4,128)S(1)} %pad_add_fusion.meta, bf16[8,4,64,128]{3,2,1,0:T(8,128)(2,1)S(1)} %all-to-all-done.1.got), custom_call_target="tpu_custom_call" | custom-call | tf_op jit(solution)/shard_map/window/pallas_call | solution.py:512
  54.1 0.0 copy-start.4
  54.1 0.0 copy-start.5
  54.1 0.0 copy-start
  54.1 4.9 %all-to-all-start.2 = ((bf16[4,2,256,128]{3,2,1,0:T(8,128)(2,1)}), bf16[4,2,256,128]{3,2,1,0:T(8,128)(2,1)S(1)}, u32[]{:S(2)}, u32[]{:S(2)}) async-start(bf16[4,2,256,128]{3,2,1,0:T(8,128)(2,1)} %window.1), calls=%async_computation.2 | async-start | bytes 1048576 | tf_op jit(solution)/shard_map/all_to_all | solution.py:525
  59.1 1.3 %collective-permute-start.3 = (bf16[2,6,128]{2,1,0:T(8,128)(2,1)S(1)}, bf16[2,6,128]{2,1,0:T(8,128)(2,1)S(1)}, u32[]{:S(2)}, u32[]{:S(2)}) collective-permute-start(bf16[2,6,128]{2,1,0:T(8,128)(2,1)S(1)} %get-tuple-element.23), channel_id=1, source_target_pairs={{0,4},{4,8},{8,12},{12,16},{16,20},{20,24},{24,28},{28,32},{32,36}... | collective-permute-start | bytes 9224 | tf_op jit(solution)/shard_map/ppermute | solution.py:29
  60.4 0.0 copy-start.1
  60.4 1.4 %collective-permute-start.4 = (bf16[2,6,128]{2,1,0:T(8,128)(2,1)S(1)}, bf16[2,6,128]{2,1,0:T(8,128)(2,1)S(1)}, u32[]{:S(2)}, u32[]{:S(2)}) collective-permute-start(bf16[2,6,128]{2,1,0:T(8,128)(2,1)S(1)} %get-tuple-element.24), channel_id=1, source_target_pairs={{4,0},{8,4},{12,8},{16,12},{20,16},{24,20},{28,24},{32,28},{36,32}... | collective-permute-start | bytes 9224 | tf_op jit(solution)/shard_map/ppermute | solution.py:29
  61.8 0.0 collective-permute-done.probe1
  61.9 0.0 collective-permute-done.1.probe2
  61.9 1.1 collective-permute-done.2.probe3
  63.0 3.8 %weight.1 = (f32[32,128]{1,0:T(8,128)S(1)}, bf16[2,2,256,256]{3,2,1,0:T(8,128)(2,1)S(1)}, bf16[512,256]{1,0:T(8,128)(2,1)S(1)}, bf16[512,256]{1,0:T(8,128)(2,1)S(1)}) custom-call(s32[3,128]{1,0:T(4,128)S(1)} %pad_add_fusion.meta, bf16[2,256,256]{2,1,0:T(8,128)(2,1)S(1)} %convert_bitcast_fusion.probe0, bf16[2,256,256]{2,1,0:T(8,128)(2,1)S(1)} %collective-permute-done.probe1, ...), custom_call_target="tpu_custom_call" | custom-call | tf_op jit(solution)/shard_map/weight/pallas_call | solution.py:485
  66.7 1.8 %all-to-all-done.2.wins = bf16[4,2,256,128]{3,2,1,0:T(8,128)(2,1)S(1)} async-done(((bf16[4,2,256,128]{3,2,1,0:T(8,128)(2,1)}), bf16[4,2,256,128]{3,2,1,0:T(8,128)(2,1)S(1)}, u32[]{:S(2)}, u32[]{:S(2)}) %all-to-all-start.2) | async-done | bytes 524320 | tf_op jit(solution)/shard_map/all_to_all | solution.py:525
  68.5 4.5 %wave.1 = (bf16[8,4,64,128]{3,2,1,0:T(8,128)(2,1)}, f32[1,1]{1,0:T(1,128)}) custom-call(s32[3,128]{1,0:T(4,128)S(1)} %pad_add_fusion.meta, bf16[4,2,256,128]{3,2,1,0:T(8,128)(2,1)S(1)} %all-to-all-done.2.wins, bf16[2,256,256]{2,1,0:T(8,128)(2,1)S(1)} %convert_bitcast_fusion.probe0, bf16[2,256,256]{2,1,0:T(8,128)(2,1)S(1)} %collective-permute-done.probe1, ...), custom_call_target="tpu_custom_call" | custom-call | tf_op jit(solution)/shard_map/wave/pallas_call | solution.py:526
  73.1 8.0 %all-to-all-start.3 = ((bf16[8,4,64,128]{3,2,1,0:T(8,128)(2,1)}), bf16[8,4,64,128]{3,2,1,0:T(8,128)(2,1)S(1)}, u32[]{:S(2)}, u32[]{:S(2)}) async-start(bf16[8,4,64,128]{3,2,1,0:T(8,128)(2,1)} %get-tuple-element.13), calls=%async_computation.3 | async-start | bytes 1048576 | tf_op jit(solution)/shard_map/all_to_all | solution.py:541
  81.1 0.0 copy-start.8
  81.1 0.2 convolution_bitcast_fusion
  81.3 0.5 copy-done.8
  81.8 0.2 fusion.1
  82.0 0.0 collective-permute-done.3
  82.0 0.0 collective-permute-done.4
  82.1 9.3 %all-to-all-done.3.got = bf16[8,4,64,128]{3,2,1,0:T(8,128)(2,1)S(1)} async-done(((bf16[8,4,64,128]{3,2,1,0:T(8,128)(2,1)}), bf16[8,4,64,128]{3,2,1,0:T(8,128)(2,1)S(1)}, u32[]{:S(2)}, u32[]{:S(2)}) %all-to-all-start.3) | async-done | bytes 524320 | tf_op jit(solution)/shard_map/all_to_all | solution.py:541
  91.4 1.6 %gather.1 = bf16[16,64,128]{2,1,0:T(8,128)(2,1)} custom-call(s32[3,128]{1,0:T(4,128)S(1)} %pad_add_fusion.meta, bf16[8,4,64,128]{3,2,1,0:T(8,128)(2,1)S(1)} %all-to-all-done.3.got), custom_call_target="tpu_custom_call" | custom-call | tf_op jit(solution)/shard_map/gather/pallas_call | solution.py:542
  93.0 5.1 %all-to-all-start.4 = ((bf16[16,64,128]{2,1,0:T(8,128)(2,1)}), bf16[16,64,128]{2,1,0:T(8,128)(2,1)S(1)}, u32[]{:S(2)}, u32[]{:S(2)}) async-start(bf16[16,64,128]{2,1,0:T(8,128)(2,1)} %gather.1), calls=%async_computation.4 | async-start | bytes 524288 | tf_op jit(solution)/shard_map/all_to_all | solution.py:551
  98.1 0.1 fusion.6
  98.2 3.4 %collective-permute-start.5 = (bf16[2,44,6]{2,1,0:T(8,128)(2,1)S(1)}, bf16[2,44,6]{2,1,0:T(8,128)(2,1)S(1)}, u32[]{:S(2)}, u32[]{:S(2)}) collective-permute-start(bf16[2,44,6]{2,1,0:T(8,128)(2,1)S(1)} %get-tuple-element.21), channel_id=1, source_target_pairs={{0,1},{1,2},{2,3},{4,5},{5,6},{6,7},{8,9},{9,10},{10,11},{12,13},{... | collective-permute-start | bytes 3176 | tf_op jit(solution)/shard_map/ppermute | solution.py:29
  101.6 2.5 %collective-permute-start.6 = (bf16[2,44,6]{2,1,0:T(8,128)(2,1)S(1)}, bf16[2,44,6]{2,1,0:T(8,128)(2,1)S(1)}, u32[]{:S(2)}, u32[]{:S(2)}) collective-permute-start(bf16[2,44,6]{2,1,0:T(8,128)(2,1)S(1)} %get-tuple-element.22), channel_id=1, source_target_pairs={{1,0},{2,1},{3,2},{5,4},{6,5},{7,6},{9,8},{10,9},{11,10},{13,12},{... | collective-permute-start | bytes 3176 | tf_op jit(solution)/shard_map/ppermute | solution.py:29
  104.0 0.0 copy-start.14
  104.0 0.0 copy-start.15
  104.1 0.0 copy-start.16
  104.1 0.6 copy-done.14
  104.7 0.0 copy-done.15
  104.7 0.0 copy-done.16
  104.7 0.0 copy-start.6
  104.8 0.1 reshape.84.last_w
  104.9 0.7 copy-done.6
  105.6 0.1 copy.47
  105.8 0.0 copy-start.7
  105.8 0.1 copy.50.mid_w
  105.9 0.7 copy-done.7
  106.6 0.1 reshape.82.down_w
  106.7 0.1 copy.51.biases
  106.8 0.0 collective-permute-done.5
  106.8 0.5 collective-permute-done.6
  107.3 0.1 pad_maximum_fusion.ext
  107.4 0.0 copy-start.2
  107.4 0.6 copy-done.2
  108.1 5.7 %denoise.1 = f32[2,32,128]{2,1,0:T(8,128)S(1)} custom-call(s32[3,128]{1,0:T(4,128)S(1)} %pad_add_fusion.meta, f32[2]{0:T(128)S(1)} %copy-done.2, bf16[2,44,140]{2,1,0:T(8,128)(2,1)S(1)} %pad_maximum_fusion.ext, bf16[192,72]{1,0:T(8,128)(2,1)S(1)} %bitcast.30, bf16[48,192]{1,0:T(8,128)(2,1)S(1)} %reshape.82.down_w, bf16[48,432]{1,0:T(8,128)(2,1)S(1)} %copy.50.mid_w, ...), custom_call_target="tpu_custom_call" | custom-call | flops 4000000000 | bytes 20000000 | tf_op jit(solution)/shard_map/denoise/pallas_call | solution.py:414
  113.8 2.6 %all-to-all-done.4 = bf16[16,64,128]{2,1,0:T(8,128)(2,1)S(1)} async-done(((bf16[16,64,128]{2,1,0:T(8,128)(2,1)}), bf16[16,64,128]{2,1,0:T(8,128)(2,1)S(1)}, u32[]{:S(2)}, u32[]{:S(2)}) %all-to-all-start.4) | async-done | bytes 262176 | tf_op jit(solution)/shard_map/all_to_all | solution.py:551
  116.4 0.6 add_subtract_fusion
  (25 shorter events, 0.2 us)
Async XLA Ops:
  2.2 33.6 %all-to-all-start = ((bf16[16,64,128]{2,1,0:T(8,128)(2,1)}), bf16[16,64,128]{2,1,0:T(8,128)(2,1)S(1)}, u32[]{:S(2)}, u32[]{:S(2)}) async-start(bf16[16,64,128]{2,1,0:T(8,128)(2,1)} %select_convert_fusion), calls=%async_computation | async-start | bytes 524288 | tf_op jit(solution)/shard_map/all_to_all | solution.py:477
  17.4 0.7 copy-start.13
  18.1 0.7 copy-start.12
  37.4 4.5 %copy-start.3 = (f32[1,2,256,256]{3,2,1,0:T(8,128)S(1)}, f32[1,2,256,256]{3,2,1,0:T(8,128)}, u32[]{:S(2)}) copy-start(f32[1,2,256,256]{3,2,1,0:T(8,128)} %param.19) | copy-start | bytes 1572868
  37.4 15.2 %all-to-all-start.1 = ((bf16[8,4,64,128]{3,2,1,0:T(8,128)(2,1)}), bf16[8,4,64,128]{3,2,1,0:T(8,128)(2,1)S(1)}, u32[]{:S(2)}, u32[]{:S(2)}) async-start(bf16[8,4,64,128]{3,2,1,0:T(8,128)(2,1)} %pack.1), calls=%async_computation.1 | async-start | bytes 1048576 | tf_op jit(solution)/shard_map/all_to_all | solution.py:511
  41.9 19.9 %collective-permute-start = (bf16[2,256,256]{2,1,0:T(8,128)(2,1)S(1)}, bf16[2,256,256]{2,1,0:T(8,128)(2,1)S(1)}, u32[]{:S(2)}, u32[]{:S(2)}) collective-permute-start(bf16[2,256,256]{2,1,0:T(8,128)(2,1)S(1)} %convert_bitcast_fusion.probe0), channel_id=1, source_target_pairs={{0,1},{1,2},{2,3},{3,0},{4,5},{5,6},{6,7},{7,4},{8,9},{9,10},{10,1... | collective-permute-start | bytes 786440 | tf_op jit(solution)/shard_map/ppermute | solution.py:480
  45.4 16.4 %collective-permute-start.1 = (bf16[2,256,256]{2,1,0:T(8,128)(2,1)S(1)}, bf16[2,256,256]{2,1,0:T(8,128)(2,1)S(1)}, u32[]{:S(2)}, u32[]{:S(2)}) collective-permute-start(bf16[2,256,256]{2,1,0:T(8,128)(2,1)S(1)} %convert_bitcast_fusion.probe0), channel_id=1, source_target_pairs={{0,2},{1,3},{2,0},{3,1},{4,6},{5,7},{6,4},{7,5},{8,10},{9,11},{10,... | collective-permute-start | bytes 786440 | tf_op jit(solution)/shard_map/ppermute | solution.py:480
  48.3 14.7 %collective-permute-start.2 = (bf16[2,256,256]{2,1,0:T(8,128)(2,1)S(1)}, bf16[2,256,256]{2,1,0:T(8,128)(2,1)S(1)}, u32[]{:S(2)}, u32[]{:S(2)}) collective-permute-start(bf16[2,256,256]{2,1,0:T(8,128)(2,1)S(1)} %convert_bitcast_fusion.probe0), channel_id=1, source_target_pairs={{0,3},{1,0},{2,1},{3,2},{4,7},{5,4},{6,5},{7,6},{8,11},{9,8},{10,9... | collective-permute-start | bytes 786440 | tf_op jit(solution)/shard_map/ppermute | solution.py:480
  54.1 5.0 %copy-start.4 = (f32[2,32,128]{2,1,0:T(8,128)S(1)}, f32[2,32,128]{2,1,0:T(8,128)}, u32[]{:S(2)}) copy-start(f32[2,32,128]{2,1,0:T(8,128)} %param.17) | copy-start | bytes 98308
  54.1 5.0 %copy-start.5 = (f32[2,32,128]{2,1,0:T(8,128)S(1)}, f32[2,32,128]{2,1,0:T(8,128)}, u32[]{:S(2)}) copy-start(f32[2,32,128]{2,1,0:T(8,128)} %param.18) | copy-start | bytes 98308
  54.1 8.8 %copy-start = (bf16[2,256,256]{2,1,0:T(8,128)(2,1)S(1)}, bf16[2,256,256]{2,1,0:T(8,128)(2,1)}, u32[]{:S(2)}) copy-start(bf16[2,256,256]{2,1,0:T(8,128)(2,1)} %constant.44.table) | copy-start | bytes 786436
  54.1 14.4 %all-to-all-start.2 = ((bf16[4,2,256,128]{3,2,1,0:T(8,128)(2,1)}), bf16[4,2,256,128]{3,2,1,0:T(8,128)(2,1)S(1)}, u32[]{:S(2)}, u32[]{:S(2)}) async-start(bf16[4,2,256,128]{3,2,1,0:T(8,128)(2,1)} %window.1), calls=%async_computation.2 | async-start | bytes 1048576 | tf_op jit(solution)/shard_map/all_to_all | solution.py:525
  59.1 22.9 %collective-permute-start.3 = (bf16[2,6,128]{2,1,0:T(8,128)(2,1)S(1)}, bf16[2,6,128]{2,1,0:T(8,128)(2,1)S(1)}, u32[]{:S(2)}, u32[]{:S(2)}) collective-permute-start(bf16[2,6,128]{2,1,0:T(8,128)(2,1)S(1)} %get-tuple-element.23), channel_id=1, source_target_pairs={{0,4},{4,8},{8,12},{12,16},{16,20},{20,24},{24,28},{28,32},{32,36}... | collective-permute-start | bytes 9224 | tf_op jit(solution)/shard_map/ppermute | solution.py:29
  60.4 8.1 %copy-start.1 = (f32[1,256,256]{2,1,0:T(8,128)S(1)}, f32[1,256,256]{2,1,0:T(8,128)}, u32[]{:S(2)}) copy-start(f32[1,256,256]{2,1,0:T(8,128)} %intensity.1) | copy-start | bytes 786436
  60.4 21.6 %collective-permute-start.4 = (bf16[2,6,128]{2,1,0:T(8,128)(2,1)S(1)}, bf16[2,6,128]{2,1,0:T(8,128)(2,1)S(1)}, u32[]{:S(2)}, u32[]{:S(2)}) collective-permute-start(bf16[2,6,128]{2,1,0:T(8,128)(2,1)S(1)} %get-tuple-element.24), channel_id=1, source_target_pairs={{4,0},{8,4},{12,8},{16,12},{20,16},{24,20},{28,24},{32,28},{36,32}... | collective-permute-start | bytes 9224 | tf_op jit(solution)/shard_map/ppermute | solution.py:29
  73.1 8.0 %copy-start.9 = (bf16[9,36,4,1]{1,0,3,2:T(8,128)(2,1)S(1)}, bf16[9,36,4,1]{1,0,3,2:T(8,128)(2,1)}, u32[]{:S(2)}) copy-start(bf16[9,36,4,1]{1,0,3,2:T(8,128)(2,1)} %constant.47) | copy-start | bytes 7780
  73.1 8.0 %copy-start.10 = (bf16[9,2,48]{2,1,0:T(2,128)(2,1)S(1)}, bf16[9,2,48]{2,1,0:T(2,128)(2,1)}, u32[]{:S(2)}) copy-start(bf16[9,2,48]{2,1,0:T(2,128)(2,1)} %param.29) | copy-start | bytes 5188
  73.1 8.2 %copy-start.11 = (bf16[9,48,2]{1,2,0:T(2,128)(2,1)S(1)}, bf16[9,48,2]{1,2,0:T(2,128)(2,1)}, u32[]{:S(2)}) copy-start(bf16[9,48,2]{1,2,0:T(2,128)(2,1)} %param.23) | copy-start | bytes 5188
  73.1 18.3 %all-to-all-start.3 = ((bf16[8,4,64,128]{3,2,1,0:T(8,128)(2,1)}), bf16[8,4,64,128]{3,2,1,0:T(8,128)(2,1)S(1)}, u32[]{:S(2)}, u32[]{:S(2)}) async-start(bf16[8,4,64,128]{3,2,1,0:T(8,128)(2,1)} %get-tuple-element.13), calls=%async_computation.3 | async-start | bytes 1048576 | tf_op jit(solution)/shard_map/all_to_all | solution.py:541
  81.1 0.8 copy-start.8
  93.0 23.4 %all-to-all-start.4 = ((bf16[16,64,128]{2,1,0:T(8,128)(2,1)}), bf16[16,64,128]{2,1,0:T(8,128)(2,1)S(1)}, u32[]{:S(2)}, u32[]{:S(2)}) async-start(bf16[16,64,128]{2,1,0:T(8,128)(2,1)} %gather.1), calls=%async_computation.4 | async-start | bytes 524288 | tf_op jit(solution)/shard_map/all_to_all | solution.py:551
  98.2 8.6 %collective-permute-start.5 = (bf16[2,44,6]{2,1,0:T(8,128)(2,1)S(1)}, bf16[2,44,6]{2,1,0:T(8,128)(2,1)S(1)}, u32[]{:S(2)}, u32[]{:S(2)}) collective-permute-start(bf16[2,44,6]{2,1,0:T(8,128)(2,1)S(1)} %get-tuple-element.21), channel_id=1, source_target_pairs={{0,1},{1,2},{2,3},{4,5},{5,6},{6,7},{8,9},{9,10},{10,11},{12,13},{... | collective-permute-start | bytes 3176 | tf_op jit(solution)/shard_map/ppermute | solution.py:29
  101.6 5.7 %collective-permute-start.6 = (bf16[2,44,6]{2,1,0:T(8,128)(2,1)S(1)}, bf16[2,44,6]{2,1,0:T(8,128)(2,1)S(1)}, u32[]{:S(2)}, u32[]{:S(2)}) collective-permute-start(bf16[2,44,6]{2,1,0:T(8,128)(2,1)S(1)} %get-tuple-element.22), channel_id=1, source_target_pairs={{1,0},{2,1},{3,2},{5,4},{6,5},{7,6},{9,8},{10,9},{11,10},{13,12},{... | collective-permute-start | bytes 3176 | tf_op jit(solution)/shard_map/ppermute | solution.py:29
  104.0 0.7 copy-start.14
  104.0 0.7 copy-start.15
  104.1 0.7 copy-start.16
  104.7 0.9 copy-start.6
  105.8 0.8 copy-start.7
  107.4 0.7 copy-start.2

commit v7 on v6

--- a/solution.py
+++ b/solution.py
@@ -9,12 +9,12 @@
 from jax.sharding import Mesh, PartitionSpec as P
 
 HALO = 6
-NX, NZ, NC, NM = 4, 16, 2, 4
+NX, NZ, NC, NM = 4, 8, 4, 4
 PATCH = 256
 ROWS = 32
 COLS = 128
 STRIPS = PATCH // ROWS + 1
-HALF = PATCH // ROWS // 2
+HALF = PATCH // ROWS // NC
 
 rho_weight = 2.0
 floor_level = 0.25
@@ -61,7 +61,7 @@
 
 
 def first_strip(s0, core):
-    return s0 + ((s0 + core) & 1)
+    return s0 + ((core - s0) & (NC - 1))
 
 
 def copy_out(held, out, sems, count, same):
@@ -95,11 +95,11 @@
     for target in range(NX * NC):
         tx, tc = target // NC, target % NC
         begin, cut = strips_of(meta[0, tx * (NZ * NC) + z * NC + tc], core)
-        late = near[z_slot(begin + 2 * HALF)].astype(f32)
+        late = near[z_slot(begin + NC * HALF)].astype(f32)
         early = near[z_slot(begin)].astype(f32)
         held[target, 0] = jnp.where(rows < cut, late, early).astype(bf16)
         for j in range(1, HALF):
-            held[target, j] = near[z_slot(begin + 2 * j)]
+            held[target, j] = near[z_slot(begin + NC * j)]
         copy = pltpu.make_async_copy(held.at[target], out.at[target], sems.at[target])
         copy.start()
         copies.append(copy)
@@ -113,8 +113,8 @@
     s0 = row // ROWS
     for i in range(STRIPS):
         strip = s0 + i
-        source = jnp.minimum(strip // (NZ * NC), NX - 1) * NC + (strip & 1)
-        block = got[source, (i // 2) % HALF].astype(f32)
+        source = jnp.minimum(strip // (NZ * NC), NX - 1) * NC + (strip & (NC - 1))
+        block = got[source, (i // NC) % HALF].astype(f32)
         tall[0, pl.ds(i * ROWS, ROWS)] = block[:ROWS]
         tall[1, pl.ds(i * ROWS, ROWS)] = block[ROWS:]
     offset = row - s0 * ROWS
@@ -196,10 +196,10 @@
     out[...] = jnp.zeros(out.shape, bf16)
     for i in range(STRIPS):
         strip = s0 + i
-        target = jnp.minimum(strip // (NZ * NC), NX - 1) * NC + (strip & 1)
+        target = jnp.minimum(strip // (NZ * NC), NX - 1) * NC + (strip & (NC - 1))
         piece = jnp.concatenate([tall[p, pl.ds(i * ROWS, ROWS)] for p in range(2)], axis=0)
-        if i < 2 * HALF:
-            out[target, i // 2] = piece.astype(bf16)
+        if i < NC * HALF:
+            out[target, i // NC] = piece.astype(bf16)
         else:
             out[target, 0] = (out[target, 0].astype(f32) + piece).astype(bf16)
 
@@ -212,11 +212,11 @@
         sx, sc = source // NC, source % NC
         begin, cut = strips_of(meta[0, sx * (NZ * NC) + z * NC + sc], core)
         both = got[source, 0].astype(f32)
-        late, early = z_slot(begin + 2 * HALF), z_slot(begin)
+        late, early = z_slot(begin + NC * HALF), z_slot(begin)
         acc[late] = acc[late] + jnp.where(rows < cut, both, 0.0)
         acc[early] = acc[early] + jnp.where(rows < cut, 0.0, both)
         for j in range(1, HALF):
-            slot = z_slot(begin + 2 * j)
+            slot = z_slot(begin + NC * j)
             acc[slot] = acc[slot] + got[source, j].astype(f32)
     out[...] = acc[...].astype(bf16)
 
@@ -472,8 +472,7 @@
     meta = jnp.concatenate([by_owner, place[None]], axis=0).astype(jnp.int32)
 
     rows = jnp.broadcast_to(obj_x.reshape(1, 2 * ROWS, COLS), (NZ, 2 * ROWS, COLS))
-    slots = lax.broadcasted_iota(jnp.int32, rows.shape, 0)
-    spread = jnp.where(slots + z >= 0, rows, 0.0).astype(bf16)
+    spread = rows.astype(bf16)
     near = lax.all_to_all(spread, "z", 0, 0, tiled=True)
     probe0 = probes[0].astype(bf16)
     others = [

time: 118 us -> 130 us (1.10)
  the two profiles are of different devices: /device:TPU:8 before, /device:TPU:10 now
where the time goes in v7:
time: 130 us; the launch traced here: 129 us
  starting transfers between devices  52.8 us (41%)
  waiting for transfers between devices  34.3 us (26%)
  Pallas kernels  20 us (15%)
  blocking collectives  13.2 us (10%)
  local copies, waits for them, and re-layouts  5.43 us (4%)
  other arithmetic  1.73 us (1%)
    all_to_all x1, starting transfers between devices, per_device(): near = lax.all_to_all(spread, 'z', 0, 0, tiled=True)  15.1 us
    all_to_all x1, waiting for transfers between devices, per_device(): near = lax.all_to_all(spread, 'z', 0, 0, tiled=True)  14.5 us
    ppermute x4, starting transfers between devices, shifted(): return lax.ppermute(value, axes, pairs)  13.5 us
    all_to_all x1, blocking collectives, per_device(): got = lax.all_to_all(packed, ('x', 'core'), 0, 0, tiled=True)  13.2 us
    ppermute x3, starting transfers between devices, per_device(): lax.ppermute(probe0, 'mode', [(i, (i + k) % NM) for i in range(NM)])  10.6 us
    all_to_all x1, waiting for transfers between devices, per_device(): pieces = lax.all_to_all(partial, 'z', 0, 0, tiled=True)  9.52 us
    ppermute x3, waiting for transfers between devices, per_device(): lax.ppermute(probe0, 'mode', [(i, (i + k) % NM) for i in range(NM)])  9.43 us
    pallas_call x1, Pallas kernels, denoise(): pl.pallas_call(denoise_kernel, out_shape=jax.ShapeDtypeStruct((2, ROWS, C...  5.72 us
  transfers between devices with their start and end apart: 11, of which 6 were waited for; matrix products, arithmetic and copies ran while one was open for 1% of the time, Pallas kernels for 8%

profile of v7, /device:TPU:10, one launch (start us, length us, event | category | flops | bytes accessed | tf_op | source)
XLA Modules:
  0.0 128.8 jit_solution(10002663057786726436)
XLA Ops:
  0.6 0.8 convert_element_type.27
  1.4 0.7 broadcast_in_dim.53
  2.1 15.1 %all-to-all-start = ((bf16[8,64,128]{2,1,0:T(8,128)(2,1)}), bf16[8,64,128]{2,1,0:T(8,128)(2,1)S(1)}, u32[]{:S(2)}, u32[]{:S(2)}) async-start(bf16[8,64,128]{2,1,0:T(8,128)(2,1)} %broadcast_in_dim.53), calls=%async_computation | async-start | bytes 262144 | tf_op jit(solution)/shard_map/all_to_all | solution.py:476
  17.2 0.6 copy-done.13
  17.8 0.7 copy-done.12
  18.5 0.1 select_reduce_fusion
  18.6 14.5 %all-to-all-done.near = bf16[8,64,128]{2,1,0:T(8,128)(2,1)S(1)} async-done(((bf16[8,64,128]{2,1,0:T(8,128)(2,1)}), bf16[8,64,128]{2,1,0:T(8,128)(2,1)S(1)}, u32[]{:S(2)}, u32[]{:S(2)}) %all-to-all-start) | async-done | bytes 131104 | tf_op jit(solution)/shard_map/all_to_all | solution.py:476
  33.1 2.0 %pack.1 = bf16[16,2,64,128]{3,2,1,0:T(8,128)(2,1)S(1)} custom-call(s32[3,128]{1,0:T(4,128)S(1)} %pad_add_fusion.meta, bf16[8,64,128]{2,1,0:T(8,128)(2,1)S(1)} %all-to-all-done.near), custom_call_target="tpu_custom_call" | custom-call | tf_op jit(solution)/shard_map/pack/pallas_call | solution.py:498
  35.2 13.2 %all_to_all.25.got = bf16[16,2,64,128]{3,2,1,0:T(8,128)(2,1)S(1)} all-to-all(bf16[16,2,64,128]{3,2,1,0:T(8,128)(2,1)S(1)} %pack.1), channel_id=1, replica_groups=mesh['x'=4,'z'=8,'core'=4,'mode'=4] {'x','core'}, dimensions={0} | all-to-all | bytes 1048576 | tf_op jit(solution)/shard_map/all_to_all | solution.py:510
  48.3 1.5 %window.1 = bf16[4,2,256,128]{3,2,1,0:T(8,128)(2,1)} custom-call(s32[3,128]{1,0:T(4,128)S(1)} %pad_add_fusion.meta, bf16[16,2,64,128]{3,2,1,0:T(8,128)(2,1)S(1)} %all_to_all.25.got), custom_call_target="tpu_custom_call" | custom-call | tf_op jit(solution)/shard_map/window/pallas_call | solution.py:511
  49.8 0.0 copy-start.3
  49.8 5.1 %all-to-all-start.2 = ((bf16[4,2,256,128]{3,2,1,0:T(8,128)(2,1)}), bf16[4,2,256,128]{3,2,1,0:T(8,128)(2,1)S(1)}, u32[]{:S(2)}, u32[]{:S(2)}) async-start(bf16[4,2,256,128]{3,2,1,0:T(8,128)(2,1)} %window.1), calls=%async_computation.2 | async-start | bytes 1048576 | tf_op jit(solution)/shard_map/all_to_all | solution.py:524
  54.9 0.0 copy-done.3
  54.9 0.0 copy-start.1
  54.9 3.5 %collective-permute-start = (bf16[2,256,256]{2,1,0:T(8,128)(2,1)S(1)}, bf16[2,256,256]{2,1,0:T(8,128)(2,1)S(1)}, u32[]{:S(2)}, u32[]{:S(2)}) collective-permute-start(bf16[2,256,256]{2,1,0:T(8,128)(2,1)S(1)} %convert_bitcast_fusion.probe0), channel_id=1, source_target_pairs={{0,1},{1,2},{2,3},{3,0},{4,5},{5,6},{6,7},{7,4},{8,9},{9,10},{10,1... | collective-permute-start | bytes 786440 | tf_op jit(solution)/shard_map/ppermute | solution.py:479
  58.5 2.5 %collective-permute-start.1 = (bf16[2,256,256]{2,1,0:T(8,128)(2,1)S(1)}, bf16[2,256,256]{2,1,0:T(8,128)(2,1)S(1)}, u32[]{:S(2)}, u32[]{:S(2)}) collective-permute-start(bf16[2,256,256]{2,1,0:T(8,128)(2,1)S(1)} %convert_bitcast_fusion.probe0), channel_id=1, source_target_pairs={{0,2},{1,3},{2,0},{3,1},{4,6},{5,7},{6,4},{7,5},{8,10},{9,11},{10,... | collective-permute-start | bytes 786440 | tf_op jit(solution)/shard_map/ppermute | solution.py:479
  61.0 4.5 %collective-permute-start.2 = (bf16[2,256,256]{2,1,0:T(8,128)(2,1)S(1)}, bf16[2,256,256]{2,1,0:T(8,128)(2,1)S(1)}, u32[]{:S(2)}, u32[]{:S(2)}) collective-permute-start(bf16[2,256,256]{2,1,0:T(8,128)(2,1)S(1)} %convert_bitcast_fusion.probe0), channel_id=1, source_target_pairs={{0,3},{1,0},{2,1},{3,2},{4,7},{5,4},{6,5},{7,6},{8,11},{9,8},{10,9... | collective-permute-start | bytes 786440 | tf_op jit(solution)/shard_map/ppermute | solution.py:479
  65.5 2.4 %collective-permute-done.probe1 = bf16[2,256,256]{2,1,0:T(8,128)(2,1)S(1)} collective-permute-done((bf16[2,256,256]{2,1,0:T(8,128)(2,1)S(1)}, bf16[2,256,256]{2,1,0:T(8,128)(2,1)S(1)}, u32[]{:S(2)}, u32[]{:S(2)}) %collective-permute-start) | collective-permute-done | bytes 262176 | tf_op jit(solution)/shard_map/ppermute | solution.py:479
  67.9 3.2 %collective-permute-done.1.probe2 = bf16[2,256,256]{2,1,0:T(8,128)(2,1)S(1)} collective-permute-done((bf16[2,256,256]{2,1,0:T(8,128)(2,1)S(1)}, bf16[2,256,256]{2,1,0:T(8,128)(2,1)S(1)}, u32[]{:S(2)}, u32[]{:S(2)}) %collective-permute-start.1) | collective-permute-done | bytes 262176 | tf_op jit(solution)/shard_map/ppermute | solution.py:479
  71.1 3.9 %collective-permute-done.2.probe3 = bf16[2,256,256]{2,1,0:T(8,128)(2,1)S(1)} collective-permute-done((bf16[2,256,256]{2,1,0:T(8,128)(2,1)S(1)}, bf16[2,256,256]{2,1,0:T(8,128)(2,1)S(1)}, u32[]{:S(2)}, u32[]{:S(2)}) %collective-permute-start.2) | collective-permute-done | bytes 262176 | tf_op jit(solution)/shard_map/ppermute | solution.py:479
  75.0 0.0 copy-done
  75.0 4.5 %weight.1 = (f32[32,128]{1,0:T(8,128)S(1)}, bf16[2,2,256,256]{3,2,1,0:T(8,128)(2,1)S(1)}, bf16[512,256]{1,0:T(8,128)(2,1)S(1)}, bf16[512,256]{1,0:T(8,128)(2,1)S(1)}) custom-call(s32[3,128]{1,0:T(4,128)S(1)} %pad_add_fusion.meta, bf16[2,256,256]{2,1,0:T(8,128)(2,1)S(1)} %convert_bitcast_fusion.probe0, bf16[2,256,256]{2,1,0:T(8,128)(2,1)S(1)} %collective-permute-done.probe1, ...), custom_call_target="tpu_custom_call" | custom-call | tf_op jit(solution)/shard_map/weight/pallas_call | solution.py:484
  79.4 0.0 all-to-all-done.2.wins
  79.4 4.6 %wave.1 = (bf16[16,2,64,128]{3,2,1,0:T(8,128)(2,1)}, f32[1,1]{1,0:T(1,128)}) custom-call(s32[3,128]{1,0:T(4,128)S(1)} %pad_add_fusion.meta, bf16[4,2,256,128]{3,2,1,0:T(8,128)(2,1)S(1)} %all-to-all-done.2.wins, bf16[2,256,256]{2,1,0:T(8,128)(2,1)S(1)} %convert_bitcast_fusion.probe0, bf16[2,256,256]{2,1,0:T(8,128)(2,1)S(1)} %collective-permute-done.probe1, ...), custom_call_target="tpu_custom_call" | custom-call | tf_op jit(solution)/shard_map/wave/pallas_call | solution.py:525
  84.0 5.2 %all-to-all-start.3 = ((bf16[16,2,64,128]{3,2,1,0:T(8,128)(2,1)}), bf16[16,2,64,128]{3,2,1,0:T(8,128)(2,1)S(1)}, u32[]{:S(2)}, u32[]{:S(2)}) async-start(bf16[16,2,64,128]{3,2,1,0:T(8,128)(2,1)} %get-tuple-element.13), calls=%async_computation.3 | async-start | bytes 1048576 | tf_op jit(solution)/shard_map/all_to_all | solution.py:540
  89.2 0.0 copy-start.9
  89.3 0.0 copy-start.10
  89.3 0.0 copy-start.11
  89.3 2.0 %collective-permute-start.3 = (bf16[2,6,128]{2,1,0:T(8,128)(2,1)S(1)}, bf16[2,6,128]{2,1,0:T(8,128)(2,1)S(1)}, u32[]{:S(2)}, u32[]{:S(2)}) collective-permute-start(bf16[2,6,128]{2,1,0:T(8,128)(2,1)S(1)} %get-tuple-element.23), channel_id=1, source_target_pairs={{0,4},{4,8},{8,12},{12,16},{16,20},{20,24},{24,28},{28,32},{32,36}... | collective-permute-start | bytes 9224 | tf_op jit(solution)/shard_map/ppermute | solution.py:29
  91.3 0.0 copy-start.8
  91.3 5.6 %collective-permute-start.4 = (bf16[2,6,128]{2,1,0:T(8,128)(2,1)S(1)}, bf16[2,6,128]{2,1,0:T(8,128)(2,1)S(1)}, u32[]{:S(2)}, u32[]{:S(2)}) collective-permute-start(bf16[2,6,128]{2,1,0:T(8,128)(2,1)S(1)} %get-tuple-element.24), channel_id=1, source_target_pairs={{4,0},{8,4},{12,8},{16,12},{20,16},{24,20},{28,24},{32,28},{36,32}... | collective-permute-start | bytes 9224 | tf_op jit(solution)/shard_map/ppermute | solution.py:29
  97.0 0.2 convolution_bitcast_fusion
  97.2 0.2 fusion.1
  97.4 0.0 collective-permute-done.3
  97.5 0.9 collective-permute-done.4
  98.3 0.1 fusion.6
  98.4 2.6 %collective-permute-start.5 = (bf16[2,44,6]{2,1,0:T(8,128)(2,1)S(1)}, bf16[2,44,6]{2,1,0:T(8,128)(2,1)S(1)}, u32[]{:S(2)}, u32[]{:S(2)}) collective-permute-start(bf16[2,44,6]{2,1,0:T(8,128)(2,1)S(1)} %get-tuple-element.21), channel_id=1, source_target_pairs={{0,1},{1,2},{2,3},{4,5},{5,6},{6,7},{8,9},{9,10},{10,11},{12,13},{... | collective-permute-start | bytes 3176 | tf_op jit(solution)/shard_map/ppermute | solution.py:29
  101.0 3.3 %collective-permute-start.6 = (bf16[2,44,6]{2,1,0:T(8,128)(2,1)S(1)}, bf16[2,44,6]{2,1,0:T(8,128)(2,1)S(1)}, u32[]{:S(2)}, u32[]{:S(2)}) collective-permute-start(bf16[2,44,6]{2,1,0:T(8,128)(2,1)S(1)} %get-tuple-element.22), channel_id=1, source_target_pairs={{1,0},{2,1},{3,2},{5,4},{6,5},{7,6},{9,8},{10,9},{11,10},{13,12},{... | collective-permute-start | bytes 3176 | tf_op jit(solution)/shard_map/ppermute | solution.py:29
  104.2 0.0 copy-start.14
  104.3 0.0 copy-start.15
  104.3 0.0 copy-start.16
  104.3 0.6 copy-done.14
  104.9 0.0 copy-done.15
  104.9 0.0 copy-done.16
  104.9 0.0 copy-start.6
  105.0 0.1 reshape.85.last_w
  105.1 0.7 copy-done.6
  105.8 0.1 copy.47
  106.0 0.0 copy-start.7
  106.0 0.1 copy.50.mid_w
  106.1 0.7 copy-done.7
  106.8 0.1 reshape.83.down_w
  106.9 0.1 copy.51.biases
  107.0 0.0 collective-permute-done.5
  107.0 0.0 collective-permute-done.6
  107.0 0.1 pad_maximum_fusion.ext
  107.1 0.0 all-to-all-done.3.got
  107.1 1.7 %gather.1 = bf16[8,64,128]{2,1,0:T(8,128)(2,1)} custom-call(s32[3,128]{1,0:T(4,128)S(1)} %pad_add_fusion.meta, bf16[16,2,64,128]{3,2,1,0:T(8,128)(2,1)S(1)} %all-to-all-done.3.got), custom_call_target="tpu_custom_call" | custom-call | tf_op jit(solution)/shard_map/gather/pallas_call | solution.py:541
  108.8 3.4 %all-to-all-start.4 = ((bf16[8,64,128]{2,1,0:T(8,128)(2,1)}), bf16[8,64,128]{2,1,0:T(8,128)(2,1)S(1)}, u32[]{:S(2)}, u32[]{:S(2)}) async-start(bf16[8,64,128]{2,1,0:T(8,128)(2,1)} %gather.1), calls=%async_computation.4 | async-start | bytes 262144 | tf_op jit(solution)/shard_map/all_to_all | solution.py:550
  112.2 0.0 copy-start.2
  112.2 0.6 copy-done.2
  112.9 5.7 %denoise.1 = f32[2,32,128]{2,1,0:T(8,128)S(1)} custom-call(s32[3,128]{1,0:T(4,128)S(1)} %pad_add_fusion.meta, f32[2]{0:T(128)S(1)} %copy-done.2, bf16[2,44,140]{2,1,0:T(8,128)(2,1)S(1)} %pad_maximum_fusion.ext, bf16[192,72]{1,0:T(8,128)(2,1)S(1)} %bitcast.30, bf16[48,192]{1,0:T(8,128)(2,1)S(1)} %reshape.83.down_w, bf16[48,432]{1,0:T(8,128)(2,1)S(1)} %copy.50.mid_w, ...), custom_call_target="tpu_custom_call" | custom-call | flops 4000000000 | bytes 20000000 | tf_op jit(solution)/shard_map/denoise/pallas_call | solution.py:414
  118.6 9.5 %all-to-all-done.4 = bf16[8,64,128]{2,1,0:T(8,128)(2,1)S(1)} async-done(((bf16[8,64,128]{2,1,0:T(8,128)(2,1)}), bf16[8,64,128]{2,1,0:T(8,128)(2,1)S(1)}, u32[]{:S(2)}, u32[]{:S(2)}) %all-to-all-start.4) | async-done | bytes 131104 | tf_op jit(solution)/shard_map/all_to_all | solution.py:550
  128.1 0.7 add_subtract_fusion
  (24 shorter events, 0.2 us)
Async XLA Ops:
  2.1 31.1 %all-to-all-start = ((bf16[8,64,128]{2,1,0:T(8,128)(2,1)}), bf16[8,64,128]{2,1,0:T(8,128)(2,1)S(1)}, u32[]{:S(2)}, u32[]{:S(2)}) async-start(bf16[8,64,128]{2,1,0:T(8,128)(2,1)} %broadcast_in_dim.53), calls=%async_computation | async-start | bytes 262144 | tf_op jit(solution)/shard_map/all_to_all | solution.py:476
  17.2 0.7 copy-start.13
  17.8 0.7 copy-start.12
  49.8 5.1 %copy-start.3 = (f32[1,2,256,256]{3,2,1,0:T(8,128)S(1)}, f32[1,2,256,256]{3,2,1,0:T(8,128)}, u32[]{:S(2)}) copy-start(f32[1,2,256,256]{3,2,1,0:T(8,128)} %param.19) | copy-start | bytes 1572868
  49.8 29.6 %all-to-all-start.2 = ((bf16[4,2,256,128]{3,2,1,0:T(8,128)(2,1)}), bf16[4,2,256,128]{3,2,1,0:T(8,128)(2,1)S(1)}, u32[]{:S(2)}, u32[]{:S(2)}) async-start(bf16[4,2,256,128]{3,2,1,0:T(8,128)(2,1)} %window.1), calls=%async_computation.2 | async-start | bytes 1048576 | tf_op jit(solution)/shard_map/all_to_all | solution.py:524
  54.9 20.1 %copy-start = (bf16[2,256,256]{2,1,0:T(8,128)(2,1)S(1)}, bf16[2,256,256]{2,1,0:T(8,128)(2,1)}, u32[]{:S(2)}) copy-start(bf16[2,256,256]{2,1,0:T(8,128)(2,1)} %constant.41.table) | copy-start | bytes 786436
  54.9 24.5 %copy-start.1 = (f32[1,256,256]{2,1,0:T(8,128)S(1)}, f32[1,256,256]{2,1,0:T(8,128)}, u32[]{:S(2)}) copy-start(f32[1,256,256]{2,1,0:T(8,128)} %intensity.1) | copy-start | bytes 786436
  54.9 13.0 %collective-permute-start = (bf16[2,256,256]{2,1,0:T(8,128)(2,1)S(1)}, bf16[2,256,256]{2,1,0:T(8,128)(2,1)S(1)}, u32[]{:S(2)}, u32[]{:S(2)}) collective-permute-start(bf16[2,256,256]{2,1,0:T(8,128)(2,1)S(1)} %convert_bitcast_fusion.probe0), channel_id=1, source_target_pairs={{0,1},{1,2},{2,3},{3,0},{4,5},{5,6},{6,7},{7,4},{8,9},{9,10},{10,1... | collective-permute-start | bytes 786440 | tf_op jit(solution)/shard_map/ppermute | solution.py:479
  58.5 12.6 %collective-permute-start.1 = (bf16[2,256,256]{2,1,0:T(8,128)(2,1)S(1)}, bf16[2,256,256]{2,1,0:T(8,128)(2,1)S(1)}, u32[]{:S(2)}, u32[]{:S(2)}) collective-permute-start(bf16[2,256,256]{2,1,0:T(8,128)(2,1)S(1)} %convert_bitcast_fusion.probe0), channel_id=1, source_target_pairs={{0,2},{1,3},{2,0},{3,1},{4,6},{5,7},{6,4},{7,5},{8,10},{9,11},{10,... | collective-permute-start | bytes 786440 | tf_op jit(solution)/shard_map/ppermute | solution.py:479
  61.0 14.0 %collective-permute-start.2 = (bf16[2,256,256]{2,1,0:T(8,128)(2,1)S(1)}, bf16[2,256,256]{2,1,0:T(8,128)(2,1)S(1)}, u32[]{:S(2)}, u32[]{:S(2)}) collective-permute-start(bf16[2,256,256]{2,1,0:T(8,128)(2,1)S(1)} %convert_bitcast_fusion.probe0), channel_id=1, source_target_pairs={{0,3},{1,0},{2,1},{3,2},{4,7},{5,4},{6,5},{7,6},{8,11},{9,8},{10,9... | collective-permute-start | bytes 786440 | tf_op jit(solution)/shard_map/ppermute | solution.py:479
  84.0 5.2 %copy-start.4 = (f32[2,32,128]{2,1,0:T(8,128)S(1)}, f32[2,32,128]{2,1,0:T(8,128)}, u32[]{:S(2)}) copy-start(f32[2,32,128]{2,1,0:T(8,128)} %param.18) | copy-start | bytes 98308
  84.0 5.2 %copy-start.5 = (f32[2,32,128]{2,1,0:T(8,128)S(1)}, f32[2,32,128]{2,1,0:T(8,128)}, u32[]{:S(2)}) copy-start(f32[2,32,128]{2,1,0:T(8,128)} %param.17) | copy-start | bytes 98308
  84.0 23.1 %all-to-all-start.3 = ((bf16[16,2,64,128]{3,2,1,0:T(8,128)(2,1)}), bf16[16,2,64,128]{3,2,1,0:T(8,128)(2,1)S(1)}, u32[]{:S(2)}, u32[]{:S(2)}) async-start(bf16[16,2,64,128]{3,2,1,0:T(8,128)(2,1)} %get-tuple-element.13), calls=%async_computation.3 | async-start | bytes 1048576 | tf_op jit(solution)/shard_map/all_to_all | solution.py:540
  89.2 7.8 %copy-start.9 = (bf16[9,36,4,1]{1,0,3,2:T(8,128)(2,1)S(1)}, bf16[9,36,4,1]{1,0,3,2:T(8,128)(2,1)}, u32[]{:S(2)}) copy-start(bf16[9,36,4,1]{1,0,3,2:T(8,128)(2,1)} %constant.44) | copy-start | bytes 7780
  89.3 7.8 %copy-start.10 = (bf16[9,2,48]{2,1,0:T(2,128)(2,1)S(1)}, bf16[9,2,48]{2,1,0:T(2,128)(2,1)}, u32[]{:S(2)}) copy-start(bf16[9,2,48]{2,1,0:T(2,128)(2,1)} %param.29) | copy-start | bytes 5188
  89.3 7.9 %copy-start.11 = (bf16[9,48,2]{1,2,0:T(2,128)(2,1)S(1)}, bf16[9,48,2]{1,2,0:T(2,128)(2,1)}, u32[]{:S(2)}) copy-start(bf16[9,48,2]{1,2,0:T(2,128)(2,1)} %param.23) | copy-start | bytes 5188
  89.3 8.1 %collective-permute-start.3 = (bf16[2,6,128]{2,1,0:T(8,128)(2,1)S(1)}, bf16[2,6,128]{2,1,0:T(8,128)(2,1)S(1)}, u32[]{:S(2)}, u32[]{:S(2)}) collective-permute-start(bf16[2,6,128]{2,1,0:T(8,128)(2,1)S(1)} %get-tuple-element.23), channel_id=1, source_target_pairs={{0,4},{4,8},{8,12},{12,16},{16,20},{20,24},{24,28},{28,32},{32,36}... | collective-permute-start | bytes 9224 | tf_op jit(solution)/shard_map/ppermute | solution.py:29
  91.3 5.9 %copy-start.8 = (bf16[9,2,4,72]{3,0,1,2:T(8,128)(2,1)S(1)}, bf16[9,2,4,72]{3,0,1,2:T(8,128)(2,1)}, u32[]{:S(2)}) copy-start(bf16[9,2,4,72]{3,0,1,2:T(8,128)(2,1)} %constant.42) | copy-start | bytes 31108
  91.3 7.0 %collective-permute-start.4 = (bf16[2,6,128]{2,1,0:T(8,128)(2,1)S(1)}, bf16[2,6,128]{2,1,0:T(8,128)(2,1)S(1)}, u32[]{:S(2)}, u32[]{:S(2)}) collective-permute-start(bf16[2,6,128]{2,1,0:T(8,128)(2,1)S(1)} %get-tuple-element.24), channel_id=1, source_target_pairs={{4,0},{8,4},{12,8},{16,12},{20,16},{24,20},{28,24},{32,28},{36,32}... | collective-permute-start | bytes 9224 | tf_op jit(solution)/shard_map/ppermute | solution.py:29
  98.4 8.6 %collective-permute-start.5 = (bf16[2,44,6]{2,1,0:T(8,128)(2,1)S(1)}, bf16[2,44,6]{2,1,0:T(8,128)(2,1)S(1)}, u32[]{:S(2)}, u32[]{:S(2)}) collective-permute-start(bf16[2,44,6]{2,1,0:T(8,128)(2,1)S(1)} %get-tuple-element.21), channel_id=1, source_target_pairs={{0,1},{1,2},{2,3},{4,5},{5,6},{6,7},{8,9},{9,10},{10,11},{12,13},{... | collective-permute-start | bytes 3176 | tf_op jit(solution)/shard_map/ppermute | solution.py:29
  101.0 6.0 %collective-permute-start.6 = (bf16[2,44,6]{2,1,0:T(8,128)(2,1)S(1)}, bf16[2,44,6]{2,1,0:T(8,128)(2,1)S(1)}, u32[]{:S(2)}, u32[]{:S(2)}) collective-permute-start(bf16[2,44,6]{2,1,0:T(8,128)(2,1)S(1)} %get-tuple-element.22), channel_id=1, source_target_pairs={{1,0},{2,1},{3,2},{5,4},{6,5},{7,6},{9,8},{10,9},{11,10},{13,12},{... | collective-permute-start | bytes 3176 | tf_op jit(solution)/shard_map/ppermute | solution.py:29
  104.2 0.7 copy-start.14
  104.3 0.7 copy-start.15
  104.3 0.7 copy-start.16
  104.9 0.9 copy-start.6
  106.0 0.8 copy-start.7
  108.8 19.3 %all-to-all-start.4 = ((bf16[8,64,128]{2,1,0:T(8,128)(2,1)}), bf16[8,64,128]{2,1,0:T(8,128)(2,1)S(1)}, u32[]{:S(2)}, u32[]{:S(2)}) async-start(bf16[8,64,128]{2,1,0:T(8,128)(2,1)} %gather.1), calls=%async_computation.4 | async-start | bytes 262144 | tf_op jit(solution)/shard_map/all_to_all | solution.py:550
  112.2 0.7 copy-start.2

commit v8 on v7

--- a/solution.py
+++ b/solution.py
@@ -9,18 +9,19 @@
 from jax.sharding import Mesh, PartitionSpec as P
 
 HALO = 6
-NX, NZ, NC, NM = 4, 8, 4, 4
+NX, PER_X, NM = 4, 32, 4
+OUT, BACK = 4, 2
 PATCH = 256
 ROWS = 32
 COLS = 128
 STRIPS = PATCH // ROWS + 1
-HALF = PATCH // ROWS // NC
+SPAN = PATCH // ROWS
 
 rho_weight = 2.0
 floor_level = 0.25
 f32 = jnp.float32
 bf16 = jnp.bfloat16
-TILE_AXES = ("x", "z", "core")
+TILE_AXES = ("x", "zq", "zp", "core")
 
 
 def shifted(value, axes, step):
@@ -57,11 +58,11 @@
 
 
 def ids(meta):
-    return meta[2, 0], meta[2, 1], meta[2, 2], meta[2, 3]
-
-
-def first_strip(s0, core):
-    return s0 + ((core - s0) & (NC - 1))
+    return meta[2, 0], meta[2, 1], meta[2, 2]
+
+
+def first_strip(s0, core, step):
+    return s0 + ((core - s0) & (step - 1))
 
 
 def copy_out(held, out, sems, count, same):
@@ -78,28 +79,29 @@
     return lax.broadcasted_iota(jnp.int32, (2 * ROWS, COLS), 0) & (ROWS - 1)
 
 
-def z_slot(strip):
-    return (strip % (NZ * NC)) // NC
-
-
-def strips_of(row, core):
+def z_slot(strip, step):
+    return (strip % PER_X) // step
+
+
+def strips_of(row, core, step):
     s0 = row // ROWS
-    begin = first_strip(s0, core)
+    begin = first_strip(s0, core, step)
     return begin, jnp.where(begin == s0, row - s0 * ROWS, 0)
 
 
 def pack_kernel(meta, near, out, held, sems):
-    _, z, core, _ = ids(meta)
+    _, spot, _ = ids(meta)
+    z, core = spot // OUT, spot % OUT
     rows = row_in_strip()
     copies = []
-    for target in range(NX * NC):
-        tx, tc = target // NC, target % NC
-        begin, cut = strips_of(meta[0, tx * (NZ * NC) + z * NC + tc], core)
-        late = near[z_slot(begin + NC * HALF)].astype(f32)
-        early = near[z_slot(begin)].astype(f32)
+    for target in range(NX * OUT):
+        tx, tc = target // OUT, target % OUT
+        begin, cut = strips_of(meta[0, tx * PER_X + z * OUT + tc], core, OUT)
+        late = near[z_slot(begin + SPAN, OUT)].astype(f32)
+        early = near[z_slot(begin, OUT)].astype(f32)
         held[target, 0] = jnp.where(rows < cut, late, early).astype(bf16)
-        for j in range(1, HALF):
-            held[target, j] = near[z_slot(begin + NC * j)]
+        for j in range(1, SPAN // OUT):
+            held[target, j] = near[z_slot(begin + OUT * j, OUT)]
         copy = pltpu.make_async_copy(held.at[target], out.at[target], sems.at[target])
         copy.start()
         copies.append(copy)
@@ -108,13 +110,13 @@
 
 
 def window_kernel(meta, got, out, tall, held, sems):
-    x, z, core, _ = ids(meta)
-    row = meta[0, x * (NZ * NC) + z * NC + core]
+    x, spot, _ = ids(meta)
+    row = meta[0, x * PER_X + spot]
     s0 = row // ROWS
     for i in range(STRIPS):
         strip = s0 + i
-        source = jnp.minimum(strip // (NZ * NC), NX - 1) * NC + (strip & (NC - 1))
-        block = got[source, (i // NC) % HALF].astype(f32)
+        source = jnp.minimum(strip // PER_X, NX - 1) * OUT + (strip & (OUT - 1))
+        block = got[source, i % SPAN // OUT].astype(f32)
         tall[0, pl.ds(i * ROWS, ROWS)] = block[:ROWS]
         tall[1, pl.ds(i * ROWS, ROWS)] = block[ROWS:]
     offset = row - s0 * ROWS
@@ -131,8 +133,8 @@
 def wave_kernel(
     meta, wins, probe0, probe1, probe2, probe3, side, turn, take, intensity, table, out, err, far_all, tall
 ):
-    x, z, core, _ = ids(meta)
-    mine = x * (NZ * NC) + z * NC + core
+    x, spot, _ = ids(meta)
+    mine = x * PER_X + spot
     row = meta[0, mine]
     s0 = row // ROWS
     offset = row - s0 * ROWS
@@ -196,37 +198,38 @@
     out[...] = jnp.zeros(out.shape, bf16)
     for i in range(STRIPS):
         strip = s0 + i
-        target = jnp.minimum(strip // (NZ * NC), NX - 1) * NC + (strip & (NC - 1))
+        target = jnp.minimum(strip // PER_X, NX - 1) * BACK + (strip & (BACK - 1))
         piece = jnp.concatenate([tall[p, pl.ds(i * ROWS, ROWS)] for p in range(2)], axis=0)
-        if i < NC * HALF:
-            out[target, i // NC] = piece.astype(bf16)
+        if i < SPAN:
+            out[target, i // BACK] = piece.astype(bf16)
         else:
             out[target, 0] = (out[target, 0].astype(f32) + piece).astype(bf16)
 
 
 def gather_kernel(meta, got, out, acc):
-    _, z, core, _ = ids(meta)
+    _, spot, _ = ids(meta)
+    z, core = spot // BACK, spot % BACK
     rows = row_in_strip()
     acc[...] = jnp.zeros(acc.shape, f32)
-    for source in range(NX * NC):
-        sx, sc = source // NC, source % NC
-        begin, cut = strips_of(meta[0, sx * (NZ * NC) + z * NC + sc], core)
+    for source in range(NX * BACK):
+        sx, sc = source // BACK, source % BACK
+        begin, cut = strips_of(meta[0, sx * PER_X + z * BACK + sc], core, BACK)
         both = got[source, 0].astype(f32)
-        late, early = z_slot(begin + NC * HALF), z_slot(begin)
+        late, early = z_slot(begin + SPAN, BACK), z_slot(begin, BACK)
         acc[late] = acc[late] + jnp.where(rows < cut, both, 0.0)
         acc[early] = acc[early] + jnp.where(rows < cut, 0.0, both)
-        for j in range(1, HALF):
-            slot = z_slot(begin + NC * j)
+        for j in range(1, SPAN // BACK):
+            slot = z_slot(begin + BACK * j, BACK)
             acc[slot] = acc[slot] + got[source, j].astype(f32)
     out[...] = acc[...].astype(bf16)
 
 
 def weight_kernel(meta, probe0, probe1, probe2, probe3, table, out, side, turn, take, padded):
-    x, z, core, mode = ids(meta)
-    row0 = (x * (NZ * NC) + z * NC + core) * ROWS
+    x, spot, mode = ids(meta)
+    mine = x * PER_X + spot
+    row0 = mine * ROWS
     col0 = mode * COLS
     probes = (probe0, probe1, probe2, probe3)
-    mine = x * (NZ * NC) + z * NC + core
     src = lax.broadcasted_iota(jnp.int32, (NM * COLS, PATCH), 0)
     dst = lax.broadcasted_iota(jnp.int32, (NM * COLS, PATCH), 1)
     take[...] = jnp.where(src == dst + meta[1, mine], 1.0, 0.0).astype(bf16)
@@ -327,7 +330,7 @@
     parts,
     inter,
 ):
-    x, z, core, mode = ids(meta)
+    x, spot, mode = ids(meta)
     chans = coarse.shape[0]
     height = ROWS + 2 * HALO
     width = COLS + 2 * HALO
@@ -347,14 +350,14 @@
     full = planes[...]
     taps1[...] = jnp.concatenate([moved(full, dy, dx) for dy, dx in SHIFTS], axis=0).astype(bf16)
 
-    row0 = (x * (NZ * NC) + z * NC + core) * ROWS - HALO
+    row0 = (x * PER_X + spot) * ROWS - HALO
     col0 = mode * COLS - HALO
-    height_all, width_all = NX * NZ * NC * ROWS, NM * COLS
+    height_all, width_all = NX * PER_X * ROWS, NM * COLS
 
     def masks(start):
-        spot = lax.broadcasted_iota(jnp.int32, (1, CHUNK), 1) + start
-        rows = row0 + 2 * (spot >> 7)
-        cols = col0 + 2 * (spot & 127)
+        cell = lax.broadcasted_iota(jnp.int32, (1, CHUNK), 1) + start
+        rows = row0 + 2 * (cell >> 7)
+        cols = col0 + 2 * (cell & 127)
         found = []
         for p, q in PHASES:
             inside = (rows + p >= 0) & (rows + p < height_all)
@@ -461,25 +464,24 @@
     b_out,
 ):
     x = lax.axis_index("x")
-    z = lax.axis_index("z")
-    core = lax.axis_index("core")
+    spot = lax.axis_index(TILE_AXES[1:])
     mode = lax.axis_index("mode")
-    tiles = NX * NZ * NC
+    tiles = NX * PER_X
     lanes = jnp.arange(tiles, dtype=jnp.int32)
     owned = owner[None, :] == lanes[:, None]
     by_owner = jnp.sum(jnp.where(owned[None], corners[:, None, :], 0), axis=2)
-    place = jnp.where(lanes == 0, x, jnp.where(lanes == 1, z, jnp.where(lanes == 2, core, mode)))
+    place = jnp.where(lanes == 0, x, jnp.where(lanes == 1, spot, mode))
     meta = jnp.concatenate([by_owner, place[None]], axis=0).astype(jnp.int32)
 
-    rows = jnp.broadcast_to(obj_x.reshape(1, 2 * ROWS, COLS), (NZ, 2 * ROWS, COLS))
+    rows = jnp.broadcast_to(obj_x.reshape(1, 2 * ROWS, COLS), (PER_X // OUT, 2 * ROWS, COLS))
     spread = rows.astype(bf16)
-    near = lax.all_to_all(spread, "z", 0, 0, tiled=True)
+    near = lax.all_to_all(spread, "zq", 0, 0, tiled=True)
     probe0 = probes[0].astype(bf16)
-    others = [
-        lax.ppermute(probe0, "mode", [(i, (i + k) % NM) for i in range(NM)])
-        for k in range(1, NM)
+    probe1, probe3 = [
+        lax.ppermute(probe0, "mode", [(i, (i + k) % NM) for i in range(NM)]) for k in (1, 3)
     ]
-    all_probes = (probe0, *others)
+    probe2 = lax.ppermute(probe0, "mode", [(i, (i + 2) % NM) for i in range(NM)])
+    all_probes = (probe0, probe1, probe2, probe3)
     table = dft_table()
     denom, side, turn, take = pl.pallas_call(
         weight_kernel,
@@ -497,17 +499,17 @@
     )(meta, *near_core(*all_probes), table)
     packed = pl.pallas_call(
         pack_kernel,
-        out_shape=jax.ShapeDtypeStruct((NX * NC, HALF, 2 * ROWS, COLS), bf16),
+        out_shape=jax.ShapeDtypeStruct((NX * OUT, SPAN // OUT, 2 * ROWS, COLS), bf16),
         in_specs=[smem_spec(), vmem_spec()],
         out_specs=any_spec(),
         scratch_shapes=[
-            pltpu.VMEM((NX * NC, HALF, 2 * ROWS, COLS), bf16),
-            pltpu.SemaphoreType.DMA((NX * NC,)),
+            pltpu.VMEM((NX * OUT, SPAN // OUT, 2 * ROWS, COLS), bf16),
+            pltpu.SemaphoreType.DMA((NX * OUT,)),
         ],
         compiler_params=pltpu.CompilerParams(vmem_limit_bytes=8 * 2**20),
         name="pack",
     )(meta, *near_core(near))
-    got = lax.all_to_all(packed, ("x", "core"), 0, 0, tiled=True)
+    got = lax.all_to_all(packed, ("x", "zp", "core"), 0, 0, tiled=True)
     window = pl.pallas_call(
         window_kernel,
         out_shape=jax.ShapeDtypeStruct((NM, 2, PATCH, COLS), bf16),
@@ -525,7 +527,7 @@
     updates, misfit = pl.pallas_call(
         wave_kernel,
         out_shape=(
-            jax.ShapeDtypeStruct((NX * NC, HALF, 2 * ROWS, COLS), bf16),
+            jax.ShapeDtypeStruct((NX * BACK, SPAN // BACK, 2 * ROWS, COLS), bf16),
             jax.ShapeDtypeStruct((1, 1), f32),
         ),
         in_specs=[smem_spec()] + [vmem_spec()] * 10,
@@ -540,14 +542,14 @@
     back = lax.all_to_all(updates, ("x", "core"), 0, 0, tiled=True)
     partial = pl.pallas_call(
         gather_kernel,
-        out_shape=jax.ShapeDtypeStruct((NZ, 2 * ROWS, COLS), bf16),
+        out_shape=jax.ShapeDtypeStruct((PER_X // BACK, 2 * ROWS, COLS), bf16),
         in_specs=[smem_spec(), vmem_spec()],
         out_specs=vmem_spec(),
-        scratch_shapes=[pltpu.VMEM((NZ, 2 * ROWS, COLS), f32)],
+        scratch_shapes=[pltpu.VMEM((PER_X // BACK, 2 * ROWS, COLS), f32)],
         compiler_params=pltpu.CompilerParams(vmem_limit_bytes=8 * 2**20),
         name="gather",
     )(meta, *near_core(back))
-    pieces = lax.all_to_all(partial, "z", 0, 0, tiled=True)
+    pieces = lax.all_to_all(partial, ("zq", "zp"), 0, 0, tiled=True)
     obj_later = lax.optimization_barrier(obj_x)
     base = obj_later + dual_u
     center = denoise(base, meta, w_in, b_in, w_down, b_down, w_mid, b_mid, w_out, b_out)
@@ -559,7 +561,7 @@
 
 
 def solution(mesh):
-    split = Mesh(mesh.devices.reshape(NX, NZ, NC, NM), TILE_AXES + ("mode",))
+    split = Mesh(mesh.devices.reshape(NX, PER_X // OUT, OUT // 2, 2, NM), TILE_AXES + ("mode",))
     grid = P(None, TILE_AXES, "mode")
     return jax.shard_map(
         per_device,

time: 130 us -> 114 us (0.88)
  the two profiles are of different devices: /device:TPU:10 before, /device:TPU:8 now
where the time goes in v8:
time: 114 us; the launch traced here: 113 us
  starting transfers between devices  55.7 us (49%)
  waiting for transfers between devices  29.6 us (26%)
  Pallas kernels  19 us (17%)
  local copies, waits for them, and re-layouts  5.96 us (5%)
  other arithmetic  1.75 us (2%)
    all_to_all x1, starting transfers between devices, per_device(): near = lax.all_to_all(spread, 'zq', 0, 0, tiled=True)  15.1 us
    all_to_all x1, waiting for transfers between devices, per_device(): near = lax.all_to_all(spread, 'zq', 0, 0, tiled=True)  14.5 us
    all_to_all x1, waiting for transfers between devices, per_device(): back = lax.all_to_all(updates, ('x', 'core'), 0, 0, tiled=True)  9.3 us
    ppermute x4, starting transfers between devices, shifted(): return lax.ppermute(value, axes, pairs)  8.54 us
    all_to_all x1, starting transfers between devices, per_device(): back = lax.all_to_all(updates, ('x', 'core'), 0, 0, tiled=True)  7.96 us
    ppermute x2, starting transfers between devices, per_device(): lax.ppermute(probe0, 'mode', [(i, (i + k) % NM) for i in range(NM)])  7.8 us
    pallas_call x1, Pallas kernels, denoise(): pl.pallas_call(denoise_kernel, out_shape=jax.ShapeDtypeStruct((2, ROWS, C...  5.72 us
    all_to_all x1, starting transfers between devices, per_device(): wins = lax.all_to_all(window, 'mode', 0, 0, tiled=True)  5.05 us
  transfers between devices with their start and end apart: 12, of which 7 were waited for; matrix products, arithmetic and copies ran while one was open for 1% of the time, Pallas kernels for 14%

profile of v8, /device:TPU:8, one launch (start us, length us, event | category | flops | bytes accessed | tf_op | source)
XLA Modules:
  0.0 113.4 jit_solution(14538397430453921036)
XLA Ops:
  0.6 0.8 convert_element_type.27
  1.4 0.7 broadcast_in_dim.49
  2.1 15.1 %all-to-all-start = ((bf16[8,64,128]{2,1,0:T(8,128)(2,1)}), bf16[8,64,128]{2,1,0:T(8,128)(2,1)S(1)}, u32[]{:S(2)}, u32[]{:S(2)}) async-start(bf16[8,64,128]{2,1,0:T(8,128)(2,1)} %broadcast_in_dim.49), calls=%async_computation | async-start | bytes 262144 | tf_op jit(solution)/shard_map/all_to_all | solution.py:478
  17.2 0.6 copy-done.13
  17.8 0.7 copy-done.12
  18.5 0.1 select_reduce_fusion
  18.6 14.5 %all-to-all-done.near = bf16[8,64,128]{2,1,0:T(8,128)(2,1)S(1)} async-done(((bf16[8,64,128]{2,1,0:T(8,128)(2,1)}), bf16[8,64,128]{2,1,0:T(8,128)(2,1)S(1)}, u32[]{:S(2)}, u32[]{:S(2)}) %all-to-all-start) | async-done | bytes 131104 | tf_op jit(solution)/shard_map/all_to_all | solution.py:478
  33.1 1.8 %pack.1 = bf16[16,2,64,128]{3,2,1,0:T(8,128)(2,1)} custom-call(s32[3,128]{1,0:T(4,128)S(1)} %pad_add_fusion.meta, bf16[8,64,128]{2,1,0:T(8,128)(2,1)S(1)} %all-to-all-done.near), custom_call_target="tpu_custom_call" | custom-call | tf_op jit(solution)/shard_map/pack/pallas_call | solution.py:500
  35.0 0.0 copy-start.3
  35.0 4.8 %all-to-all-start.1 = ((bf16[16,2,64,128]{3,2,1,0:T(8,128)(2,1)}), bf16[16,2,64,128]{3,2,1,0:T(8,128)(2,1)S(1)}, u32[]{:S(2)}, u32[]{:S(2)}) async-start(bf16[16,2,64,128]{3,2,1,0:T(8,128)(2,1)} %pack.1), calls=%async_computation.1 | async-start | bytes 1048576 | tf_op jit(solution)/shard_map/all_to_all | solution.py:512
  39.8 3.5 %collective-permute-start = (bf16[2,256,256]{2,1,0:T(8,128)(2,1)S(1)}, bf16[2,256,256]{2,1,0:T(8,128)(2,1)S(1)}, u32[]{:S(2)}, u32[]{:S(2)}) collective-permute-start(bf16[2,256,256]{2,1,0:T(8,128)(2,1)S(1)} %convert_bitcast_fusion.probe0), channel_id=1, source_target_pairs={{0,1},{1,2},{2,3},{3,0},{4,5},{5,6},{6,7},{7,4},{8,9},{9,10},{10,1... | collective-permute-start | bytes 786440 | tf_op jit(solution)/shard_map/ppermute | solution.py:481
  43.3 2.8 %collective-permute-start.1 = (bf16[2,256,256]{2,1,0:T(8,128)(2,1)S(1)}, bf16[2,256,256]{2,1,0:T(8,128)(2,1)S(1)}, u32[]{:S(2)}, u32[]{:S(2)}) collective-permute-start(bf16[2,256,256]{2,1,0:T(8,128)(2,1)S(1)} %convert_bitcast_fusion.probe0), channel_id=1, source_target_pairs={{0,2},{1,3},{2,0},{3,1},{4,6},{5,7},{6,4},{7,5},{8,10},{9,11},{10,... | collective-permute-start | bytes 786440 | tf_op jit(solution)/shard_map/ppermute | solution.py:483
  46.2 4.3 %collective-permute-start.2 = (bf16[2,256,256]{2,1,0:T(8,128)(2,1)S(1)}, bf16[2,256,256]{2,1,0:T(8,128)(2,1)S(1)}, u32[]{:S(2)}, u32[]{:S(2)}) collective-permute-start(bf16[2,256,256]{2,1,0:T(8,128)(2,1)S(1)} %convert_bitcast_fusion.probe0), channel_id=1, source_target_pairs={{0,3},{1,0},{2,1},{3,2},{4,7},{5,4},{6,5},{7,6},{8,11},{9,8},{10,9... | collective-permute-start | bytes 786440 | tf_op jit(solution)/shard_map/ppermute | solution.py:481
  50.5 0.1 all-to-all-done.1.got
  50.6 1.5 %window.1 = bf16[4,2,256,128]{3,2,1,0:T(8,128)(2,1)} custom-call(s32[3,128]{1,0:T(4,128)S(1)} %pad_add_fusion.meta, bf16[16,2,64,128]{3,2,1,0:T(8,128)(2,1)S(1)} %all-to-all-done.1.got), custom_call_target="tpu_custom_call" | custom-call | tf_op jit(solution)/shard_map/window/pallas_call | solution.py:513
  52.1 0.0 copy-start.4
  52.1 0.0 copy-start.5
  52.1 0.0 copy-start
  52.2 5.1 %all-to-all-start.2 = ((bf16[4,2,256,128]{3,2,1,0:T(8,128)(2,1)}), bf16[4,2,256,128]{3,2,1,0:T(8,128)(2,1)S(1)}, u32[]{:S(2)}, u32[]{:S(2)}) async-start(bf16[4,2,256,128]{3,2,1,0:T(8,128)(2,1)} %window.1), calls=%async_computation.2 | async-start | bytes 1048576 | tf_op jit(solution)/shard_map/all_to_all | solution.py:526
  57.2 1.3 %collective-permute-start.3 = (bf16[2,6,128]{2,1,0:T(8,128)(2,1)S(1)}, bf16[2,6,128]{2,1,0:T(8,128)(2,1)S(1)}, u32[]{:S(2)}, u32[]{:S(2)}) collective-permute-start(bf16[2,6,128]{2,1,0:T(8,128)(2,1)S(1)} %get-tuple-element.23), channel_id=1, source_target_pairs={{0,4},{4,8},{8,12},{12,16},{16,20},{20,24},{24,28},{28,32},{32,36}... | collective-permute-start | bytes 9224 | tf_op jit(solution)/shard_map/ppermute | solution.py:30
  58.5 0.0 copy-start.1
  58.6 1.4 %collective-permute-start.4 = (bf16[2,6,128]{2,1,0:T(8,128)(2,1)S(1)}, bf16[2,6,128]{2,1,0:T(8,128)(2,1)S(1)}, u32[]{:S(2)}, u32[]{:S(2)}) collective-permute-start(bf16[2,6,128]{2,1,0:T(8,128)(2,1)S(1)} %get-tuple-element.24), channel_id=1, source_target_pairs={{4,0},{8,4},{12,8},{16,12},{20,16},{24,20},{28,24},{32,28},{36,32}... | collective-permute-start | bytes 9224 | tf_op jit(solution)/shard_map/ppermute | solution.py:30
  60.0 0.0 collective-permute-done.probe1
  60.0 0.0 collective-permute-done.1.probe2
  60.0 0.8 collective-permute-done.2.probe3
  60.8 3.8 %weight.1 = (f32[32,128]{1,0:T(8,128)S(1)}, bf16[2,2,256,256]{3,2,1,0:T(8,128)(2,1)S(1)}, bf16[512,256]{1,0:T(8,128)(2,1)S(1)}, bf16[512,256]{1,0:T(8,128)(2,1)S(1)}) custom-call(s32[3,128]{1,0:T(4,128)S(1)} %pad_add_fusion.meta, bf16[2,256,256]{2,1,0:T(8,128)(2,1)S(1)} %convert_bitcast_fusion.probe0, bf16[2,256,256]{2,1,0:T(8,128)(2,1)S(1)} %collective-permute-done.probe1, ...), custom_call_target="tpu_custom_call" | custom-call | tf_op jit(solution)/shard_map/weight/pallas_call | solution.py:486
  64.6 1.8 %all-to-all-done.2.wins = bf16[4,2,256,128]{3,2,1,0:T(8,128)(2,1)S(1)} async-done(((bf16[4,2,256,128]{3,2,1,0:T(8,128)(2,1)}), bf16[4,2,256,128]{3,2,1,0:T(8,128)(2,1)S(1)}, u32[]{:S(2)}, u32[]{:S(2)}) %all-to-all-start.2) | async-done | bytes 524320 | tf_op jit(solution)/shard_map/all_to_all | solution.py:526
  66.4 4.5 %wave.1 = (bf16[8,4,64,128]{3,2,1,0:T(8,128)(2,1)}, f32[1,1]{1,0:T(1,128)}) custom-call(s32[3,128]{1,0:T(4,128)S(1)} %pad_add_fusion.meta, bf16[4,2,256,128]{3,2,1,0:T(8,128)(2,1)S(1)} %all-to-all-done.2.wins, bf16[2,256,256]{2,1,0:T(8,128)(2,1)S(1)} %convert_bitcast_fusion.probe0, bf16[2,256,256]{2,1,0:T(8,128)(2,1)S(1)} %collective-permute-done.probe1, ...), custom_call_target="tpu_custom_call" | custom-call | tf_op jit(solution)/shard_map/wave/pallas_call | solution.py:527
  70.9 8.0 %all-to-all-start.3 = ((bf16[8,4,64,128]{3,2,1,0:T(8,128)(2,1)}), bf16[8,4,64,128]{3,2,1,0:T(8,128)(2,1)S(1)}, u32[]{:S(2)}, u32[]{:S(2)}) async-start(bf16[8,4,64,128]{3,2,1,0:T(8,128)(2,1)} %get-tuple-element.13), calls=%async_computation.3 | async-start | bytes 1048576 | tf_op jit(solution)/shard_map/all_to_all | solution.py:542
  78.9 0.0 copy-start.8
  78.9 0.2 convolution_bitcast_fusion
  79.1 0.5 copy-done.8
  79.7 0.2 fusion.1
  79.8 0.0 collective-permute-done.3
  79.9 0.0 collective-permute-done.4
  79.9 9.3 %all-to-all-done.3.got = bf16[8,4,64,128]{3,2,1,0:T(8,128)(2,1)S(1)} async-done(((bf16[8,4,64,128]{3,2,1,0:T(8,128)(2,1)}), bf16[8,4,64,128]{3,2,1,0:T(8,128)(2,1)S(1)}, u32[]{:S(2)}, u32[]{:S(2)}) %all-to-all-start.3) | async-done | bytes 524320 | tf_op jit(solution)/shard_map/all_to_all | solution.py:542
  89.2 1.7 %gather.1 = bf16[16,64,128]{2,1,0:T(8,128)(2,1)} custom-call(s32[3,128]{1,0:T(4,128)S(1)} %pad_add_fusion.meta, bf16[8,4,64,128]{3,2,1,0:T(8,128)(2,1)S(1)} %all-to-all-done.3.got), custom_call_target="tpu_custom_call" | custom-call | tf_op jit(solution)/shard_map/gather/pallas_call | solution.py:543
  90.8 3.5 %all-to-all-start.4 = ((bf16[16,64,128]{2,1,0:T(8,128)(2,1)}), bf16[16,64,128]{2,1,0:T(8,128)(2,1)S(1)}, u32[]{:S(2)}, u32[]{:S(2)}) async-start(bf16[16,64,128]{2,1,0:T(8,128)(2,1)} %gather.1), calls=%async_computation.4 | async-start | bytes 524288 | tf_op jit(solution)/shard_map/all_to_all | solution.py:552
  94.4 0.1 fusion.6
  94.5 3.4 %collective-permute-start.5 = (bf16[2,44,6]{2,1,0:T(8,128)(2,1)S(1)}, bf16[2,44,6]{2,1,0:T(8,128)(2,1)S(1)}, u32[]{:S(2)}, u32[]{:S(2)}) collective-permute-start(bf16[2,44,6]{2,1,0:T(8,128)(2,1)S(1)} %get-tuple-element.21), channel_id=1, source_target_pairs={{0,1},{1,2},{2,3},{4,5},{5,6},{6,7},{8,9},{9,10},{10,11},{12,13},{... | collective-permute-start | bytes 3176 | tf_op jit(solution)/shard_map/ppermute | solution.py:30
  97.9 2.4 %collective-permute-start.6 = (bf16[2,44,6]{2,1,0:T(8,128)(2,1)S(1)}, bf16[2,44,6]{2,1,0:T(8,128)(2,1)S(1)}, u32[]{:S(2)}, u32[]{:S(2)}) collective-permute-start(bf16[2,44,6]{2,1,0:T(8,128)(2,1)S(1)} %get-tuple-element.22), channel_id=1, source_target_pairs={{1,0},{2,1},{3,2},{5,4},{6,5},{7,6},{9,8},{10,9},{11,10},{13,12},{... | collective-permute-start | bytes 3176 | tf_op jit(solution)/shard_map/ppermute | solution.py:30
  100.3 0.0 copy-start.14
  100.3 0.0 copy-start.15
  100.3 0.0 copy-start.16
  100.3 0.6 copy-done.14
  101.0 0.0 copy-done.15
  101.0 0.0 copy-done.16
  101.0 0.0 copy-start.6
  101.1 0.1 reshape.76.last_w
  101.2 0.7 copy-done.6
  101.9 0.1 copy.47
  102.0 0.0 copy-start.7
  102.0 0.1 copy.50.mid_w
  102.1 0.7 copy-done.7
  102.9 0.1 reshape.74.down_w
  103.0 0.1 copy.51.biases
  103.1 0.0 collective-permute-done.5
  103.1 0.6 collective-permute-done.6
  103.6 0.1 pad_maximum_fusion.ext
  103.7 0.0 copy-start.2
  103.8 0.6 copy-done.2
  104.4 5.7 %denoise.1 = f32[2,32,128]{2,1,0:T(8,128)S(1)} custom-call(s32[3,128]{1,0:T(4,128)S(1)} %pad_add_fusion.meta, f32[2]{0:T(128)S(1)} %copy-done.2, bf16[2,44,140]{2,1,0:T(8,128)(2,1)S(1)} %pad_maximum_fusion.ext, bf16[192,72]{1,0:T(8,128)(2,1)S(1)} %bitcast.30, bf16[48,192]{1,0:T(8,128)(2,1)S(1)} %reshape.74.down_w, bf16[48,432]{1,0:T(8,128)(2,1)S(1)} %copy.50.mid_w, ...), custom_call_target="tpu_custom_call" | custom-call | flops 4000000000 | bytes 20000000 | tf_op jit(solution)/shard_map/denoise/pallas_call | solution.py:417
  110.1 2.5 %all-to-all-done.4 = bf16[16,64,128]{2,1,0:T(8,128)(2,1)S(1)} async-done(((bf16[16,64,128]{2,1,0:T(8,128)(2,1)}), bf16[16,64,128]{2,1,0:T(8,128)(2,1)S(1)}, u32[]{:S(2)}, u32[]{:S(2)}) %all-to-all-start.4) | async-done | bytes 262176 | tf_op jit(solution)/shard_map/all_to_all | solution.py:552
  112.7 0.6 add_subtract_fusion
  (25 shorter events, 0.2 us)
Async XLA Ops:
  2.1 31.1 %all-to-all-start = ((bf16[8,64,128]{2,1,0:T(8,128)(2,1)}), bf16[8,64,128]{2,1,0:T(8,128)(2,1)S(1)}, u32[]{:S(2)}, u32[]{:S(2)}) async-start(bf16[8,64,128]{2,1,0:T(8,128)(2,1)} %broadcast_in_dim.49), calls=%async_computation | async-start | bytes 262144 | tf_op jit(solution)/shard_map/all_to_all | solution.py:478
  17.2 0.7 copy-start.13
  17.8 0.7 copy-start.12
  35.0 4.8 %copy-start.3 = (f32[1,2,256,256]{3,2,1,0:T(8,128)S(1)}, f32[1,2,256,256]{3,2,1,0:T(8,128)}, u32[]{:S(2)}) copy-start(f32[1,2,256,256]{3,2,1,0:T(8,128)} %param.19) | copy-start | bytes 1572868
  35.0 15.7 %all-to-all-start.1 = ((bf16[16,2,64,128]{3,2,1,0:T(8,128)(2,1)}), bf16[16,2,64,128]{3,2,1,0:T(8,128)(2,1)S(1)}, u32[]{:S(2)}, u32[]{:S(2)}) async-start(bf16[16,2,64,128]{3,2,1,0:T(8,128)(2,1)} %pack.1), calls=%async_computation.1 | async-start | bytes 1048576 | tf_op jit(solution)/shard_map/all_to_all | solution.py:512
  39.8 20.1 %collective-permute-start = (bf16[2,256,256]{2,1,0:T(8,128)(2,1)S(1)}, bf16[2,256,256]{2,1,0:T(8,128)(2,1)S(1)}, u32[]{:S(2)}, u32[]{:S(2)}) collective-permute-start(bf16[2,256,256]{2,1,0:T(8,128)(2,1)S(1)} %convert_bitcast_fusion.probe0), channel_id=1, source_target_pairs={{0,1},{1,2},{2,3},{3,0},{4,5},{5,6},{6,7},{7,4},{8,9},{9,10},{10,1... | collective-permute-start | bytes 786440 | tf_op jit(solution)/shard_map/ppermute | solution.py:481
  43.3 16.7 %collective-permute-start.1 = (bf16[2,256,256]{2,1,0:T(8,128)(2,1)S(1)}, bf16[2,256,256]{2,1,0:T(8,128)(2,1)S(1)}, u32[]{:S(2)}, u32[]{:S(2)}) collective-permute-start(bf16[2,256,256]{2,1,0:T(8,128)(2,1)S(1)} %convert_bitcast_fusion.probe0), channel_id=1, source_target_pairs={{0,2},{1,3},{2,0},{3,1},{4,6},{5,7},{6,4},{7,5},{8,10},{9,11},{10,... | collective-permute-start | bytes 786440 | tf_op jit(solution)/shard_map/ppermute | solution.py:483
  46.2 14.6 %collective-permute-start.2 = (bf16[2,256,256]{2,1,0:T(8,128)(2,1)S(1)}, bf16[2,256,256]{2,1,0:T(8,128)(2,1)S(1)}, u32[]{:S(2)}, u32[]{:S(2)}) collective-permute-start(bf16[2,256,256]{2,1,0:T(8,128)(2,1)S(1)} %convert_bitcast_fusion.probe0), channel_id=1, source_target_pairs={{0,3},{1,0},{2,1},{3,2},{4,7},{5,4},{6,5},{7,6},{8,11},{9,8},{10,9... | collective-permute-start | bytes 786440 | tf_op jit(solution)/shard_map/ppermute | solution.py:481
  52.1 5.1 %copy-start.4 = (f32[2,32,128]{2,1,0:T(8,128)S(1)}, f32[2,32,128]{2,1,0:T(8,128)}, u32[]{:S(2)}) copy-start(f32[2,32,128]{2,1,0:T(8,128)} %param.18) | copy-start | bytes 98308
  52.1 5.1 %copy-start.5 = (f32[2,32,128]{2,1,0:T(8,128)S(1)}, f32[2,32,128]{2,1,0:T(8,128)}, u32[]{:S(2)}) copy-start(f32[2,32,128]{2,1,0:T(8,128)} %param.17) | copy-start | bytes 98308
  52.1 8.6 %copy-start = (bf16[2,256,256]{2,1,0:T(8,128)(2,1)S(1)}, bf16[2,256,256]{2,1,0:T(8,128)(2,1)}, u32[]{:S(2)}) copy-start(bf16[2,256,256]{2,1,0:T(8,128)(2,1)} %constant.47.table) | copy-start | bytes 786436
  52.2 14.2 %all-to-all-start.2 = ((bf16[4,2,256,128]{3,2,1,0:T(8,128)(2,1)}), bf16[4,2,256,128]{3,2,1,0:T(8,128)(2,1)S(1)}, u32[]{:S(2)}, u32[]{:S(2)}) async-start(bf16[4,2,256,128]{3,2,1,0:T(8,128)(2,1)} %window.1), calls=%async_computation.2 | async-start | bytes 1048576 | tf_op jit(solution)/shard_map/all_to_all | solution.py:526
  57.2 22.6 %collective-permute-start.3 = (bf16[2,6,128]{2,1,0:T(8,128)(2,1)S(1)}, bf16[2,6,128]{2,1,0:T(8,128)(2,1)S(1)}, u32[]{:S(2)}, u32[]{:S(2)}) collective-permute-start(bf16[2,6,128]{2,1,0:T(8,128)(2,1)S(1)} %get-tuple-element.23), channel_id=1, source_target_pairs={{0,4},{4,8},{8,12},{12,16},{16,20},{20,24},{24,28},{28,32},{32,36}... | collective-permute-start | bytes 9224 | tf_op jit(solution)/shard_map/ppermute | solution.py:30
  58.5 7.8 %copy-start.1 = (f32[1,256,256]{2,1,0:T(8,128)S(1)}, f32[1,256,256]{2,1,0:T(8,128)}, u32[]{:S(2)}) copy-start(f32[1,256,256]{2,1,0:T(8,128)} %intensity.1) | copy-start | bytes 786436
  58.6 21.3 %collective-permute-start.4 = (bf16[2,6,128]{2,1,0:T(8,128)(2,1)S(1)}, bf16[2,6,128]{2,1,0:T(8,128)(2,1)S(1)}, u32[]{:S(2)}, u32[]{:S(2)}) collective-permute-start(bf16[2,6,128]{2,1,0:T(8,128)(2,1)S(1)} %get-tuple-element.24), channel_id=1, source_target_pairs={{4,0},{8,4},{12,8},{16,12},{20,16},{24,20},{28,24},{32,28},{36,32}... | collective-permute-start | bytes 9224 | tf_op jit(solution)/shard_map/ppermute | solution.py:30
  70.9 8.0 %copy-start.9 = (bf16[9,36,4,1]{1,0,3,2:T(8,128)(2,1)S(1)}, bf16[9,36,4,1]{1,0,3,2:T(8,128)(2,1)}, u32[]{:S(2)}) copy-start(bf16[9,36,4,1]{1,0,3,2:T(8,128)(2,1)} %constant.50) | copy-start | bytes 7780
  70.9 8.0 %copy-start.10 = (bf16[9,2,48]{2,1,0:T(2,128)(2,1)S(1)}, bf16[9,2,48]{2,1,0:T(2,128)(2,1)}, u32[]{:S(2)}) copy-start(bf16[9,2,48]{2,1,0:T(2,128)(2,1)} %param.29) | copy-start | bytes 5188
  70.9 8.2 %copy-start.11 = (bf16[9,48,2]{1,2,0:T(2,128)(2,1)S(1)}, bf16[9,48,2]{1,2,0:T(2,128)(2,1)}, u32[]{:S(2)}) copy-start(bf16[9,48,2]{1,2,0:T(2,128)(2,1)} %param.23) | copy-start | bytes 5188
  70.9 18.3 %all-to-all-start.3 = ((bf16[8,4,64,128]{3,2,1,0:T(8,128)(2,1)}), bf16[8,4,64,128]{3,2,1,0:T(8,128)(2,1)S(1)}, u32[]{:S(2)}, u32[]{:S(2)}) async-start(bf16[8,4,64,128]{3,2,1,0:T(8,128)(2,1)} %get-tuple-element.13), calls=%async_computation.3 | async-start | bytes 1048576 | tf_op jit(solution)/shard_map/all_to_all | solution.py:542
  78.9 0.8 copy-start.8
  90.8 21.8 %all-to-all-start.4 = ((bf16[16,64,128]{2,1,0:T(8,128)(2,1)}), bf16[16,64,128]{2,1,0:T(8,128)(2,1)S(1)}, u32[]{:S(2)}, u32[]{:S(2)}) async-start(bf16[16,64,128]{2,1,0:T(8,128)(2,1)} %gather.1), calls=%async_computation.4 | async-start | bytes 524288 | tf_op jit(solution)/shard_map/all_to_all | solution.py:552
  94.5 8.6 %collective-permute-start.5 = (bf16[2,44,6]{2,1,0:T(8,128)(2,1)S(1)}, bf16[2,44,6]{2,1,0:T(8,128)(2,1)S(1)}, u32[]{:S(2)}, u32[]{:S(2)}) collective-permute-start(bf16[2,44,6]{2,1,0:T(8,128)(2,1)S(1)} %get-tuple-element.21), channel_id=1, source_target_pairs={{0,1},{1,2},{2,3},{4,5},{5,6},{6,7},{8,9},{9,10},{10,11},{12,13},{... | collective-permute-start | bytes 3176 | tf_op jit(solution)/shard_map/ppermute | solution.py:30
  97.9 5.7 %collective-permute-start.6 = (bf16[2,44,6]{2,1,0:T(8,128)(2,1)S(1)}, bf16[2,44,6]{2,1,0:T(8,128)(2,1)S(1)}, u32[]{:S(2)}, u32[]{:S(2)}) collective-permute-start(bf16[2,44,6]{2,1,0:T(8,128)(2,1)S(1)} %get-tuple-element.22), channel_id=1, source_target_pairs={{1,0},{2,1},{3,2},{5,4},{6,5},{7,6},{9,8},{10,9},{11,10},{13,12},{... | collective-permute-start | bytes 3176 | tf_op jit(solution)/shard_map/ppermute | solution.py:30
  100.3 0.7 copy-start.14
  100.3 0.7 copy-start.15
  100.3 0.7 copy-start.16
  101.0 0.9 copy-start.6
  102.0 0.8 copy-start.7
  103.7 0.7 copy-start.2
